TPU v7x, 256 devices: a whole 4x4x8 slice. The times are simulated.
256 devices in a mesh: rows: 8 (over z), cols: 32 (over y, x, core).
Axes of the slice: x: 4, y: 4, z: 8, core: 2. Of those that a mesh axis runs over, the one named last changes fastest.
Arguments:
- whitened: float32 [3, 1048576], P(None, ('rows', 'cols')), may hold values from -6 to 6
- cotangent: bfloat16 [64, 1048576], P(None, ('rows', 'cols')), may hold values from -6 to 6
- lift_weight: float32 [64, 3], replicated, may hold values from -3.5 to 3.5
- conv_now: bfloat16 [3, 128, 64], replicated, may hold values from -0.5 to 0.5
- conv_past: bfloat16 [3, 128, 64], replicated, may hold values from -0.5 to 0.5
- mix_weight: bfloat16 [3, 64, 64], replicated, may hold values from -0.75 to 0.75
- dilations: int32 [3], replicated, may hold values from 64 to 256, as said below
- psd_bin: int32 [4096, 32, 8], P(None, 'cols', 'rows'), may hold values from 0 to 1023, as said below
- psd_weight: float32 [2, 1024], replicated, may hold values from 0.2 to 5
Outputs:
- data_grad: float32 [3, 1048576], P(None, ('rows', 'cols'))
- grad_now: float32 [3, 128, 64], replicated
- grad_past: float32 [3, 128, 64], replicated
- grad_mix: float32 [3, 64, 64], replicated
- grad_lift: float32 [64, 3], replicated
Inputs may be any that keep to these rules, and one draw needn't show every extreme that they name: `dilations`: multiples of 4; one layer has 64, one has 256. `psd_bin`: frequencies k and 1048576 - k have the same bin.
All inputs are finite; a program needn't handle non-finite values.
Results may differ from a plain program's by a relative error of at most 0.0068.
Values may be sent and summed in bfloat16 or wider, within the bound.
No kernel may reach another device: no remote copies, remote signals or barrier semaphores. Data moves between devices by JAX's collectives and lax.ppermute only.
A program may use at most 64 MiB of HBM per device.

v0:
```python
import math

import jax
import jax.numpy as jnp
from jax import lax
from jax.sharding import PartitionSpec as P

DMAX = 256


def from_behind(array, axis, by):
    peers = lax.axis_size(axis)
    pairs = [(i, i + by) for i in range(peers) if 0 <= i + by < peers]
    return lax.ppermute(array, axis, pairs)


def lifted(lift_weight, inputs):
    return (
        lift_weight[:, 0:1] * inputs[0:1]
        + lift_weight[:, 1:2] * inputs[1:2]
        + lift_weight[:, 2:3] * inputs[2:3]
    )


def delayed(field_b, delay, before):
    joined = jnp.concatenate([before, field_b], axis=1)
    start_at = before.shape[1] - delay
    return lax.dynamic_slice_in_dim(joined, start_at, field_b.shape[1], 1)


def advanced(values, delay, head_rim):
    joined = jnp.concatenate([values, head_rim], axis=1)
    return lax.dynamic_slice_in_dim(joined, delay, values.shape[1], 1)


def gated_layer(field_now, field_b, before, weight_now, weight_past, weight_mix, delay):
    channel_count = weight_mix.shape[0]
    past_b = delayed(field_b, delay, before)
    pre_act = jnp.dot(weight_now, field_b, preferred_element_type=jnp.float32) + jnp.dot(
        weight_past, past_b, preferred_element_type=jnp.float32
    )
    tanh_part = jnp.tanh(pre_act[:channel_count])
    sigm_part = jax.nn.sigmoid(pre_act[channel_count:])
    gate_b = (tanh_part * sigm_part).astype(jnp.bfloat16)
    field_next = field_now + jnp.dot(weight_mix, gate_b, preferred_element_type=jnp.float32)
    return (field_next, (field_b, past_b, tanh_part, sigm_part, gate_b))


def phase_angle(product, modulus, sign_factor):
    return sign_factor * 2.0 * math.pi / modulus * (product % modulus).astype(jnp.float32)


def phase_table(modulus, sign_factor):
    ordinal = jnp.arange(modulus, dtype=jnp.int32)
    angles = phase_angle(ordinal[:, None] * ordinal[None, :], modulus, sign_factor)
    return (jnp.cos(angles), jnp.sin(angles))


def rotate(signals, angles):
    real_part, imag_part = signals
    cosine = jnp.cos(angles)
    sine_part = jnp.sin(angles)
    return (real_part * cosine - imag_part * sine_part, real_part * sine_part + imag_part * cosine)


def transform(pattern, table_pair, signals):
    cosine, sine_part = table_pair
    real_part, imag_part = signals
    first_term = jnp.einsum(pattern, cosine, real_part, precision=lax.Precision.HIGHEST)
    second = jnp.einsum(pattern, sine_part, real_part, precision=lax.Precision.HIGHEST)
    if imag_part is None:
        return (first_term, second)
    return (
        first_term - jnp.einsum(pattern, sine_part, imag_part, precision=lax.Precision.HIGHEST),
        second + jnp.einsum(pattern, cosine, imag_part, precision=lax.Precision.HIGHEST),
    )


def split_length(length_all):
    chosen = 1
    for factor in range(1, length_all + 1):
        if length_all % factor == 0 and factor * factor <= length_all:
            chosen = factor
    return (chosen, length_all // chosen)


def pair_up(moved):
    return ((moved, None), (0, 0, 1))


def local_section(signals, psd_bin, psd_weight, weight_rows):
    rows_count = lax.axis_size("rows")
    row_index = lax.axis_index("rows")
    col_index = lax.axis_index("cols")
    signal_count = len(weight_rows)
    segment = signals[0].shape[1]
    length_all = segment * rows_count * lax.axis_size("cols")
    slow_len, fast_len = split_length(segment)
    slow_ids = jnp.arange(slow_len, dtype=jnp.int32)
    fast_ids = jnp.arange(fast_len, dtype=jnp.int32)
    spectra = (
        signals[0].reshape(signal_count, slow_len, fast_len),
        signals[1].reshape(signal_count, slow_len, fast_len),
    )
    spectra = transform("pa,kpq->kaq", phase_table(slow_len, -1.0), spectra)
    spectra = rotate(
        spectra, phase_angle(slow_ids[:, None] * fast_ids[None, :], segment, -1.0)[None]
    )
    spectra = transform("qb,kaq->kab", phase_table(fast_len, -1.0), spectra)
    bins_here = psd_bin.reshape(fast_len, slow_len).T
    weights = jnp.take(psd_weight, bins_here, axis=1)
    factors = jnp.stack([weights[row_id] for row_id in weight_rows])
    spectra = (spectra[0] * factors, spectra[1] * factors)
    spectra = transform("bq,kab->kaq", phase_table(fast_len, 1.0), spectra)
    spectra = rotate(
        spectra, phase_angle(slow_ids[:, None] * fast_ids[None, :], segment, 1.0)[None]
    )
    spectra = transform("ap,kaq->kpq", phase_table(slow_len, 1.0), spectra)
    low_here = row_index + rows_count * col_index
    sample_all = jnp.arange(segment, dtype=jnp.int32)
    return rotate(
        (spectra[0].reshape(signal_count, segment), spectra[1].reshape(signal_count, segment)),
        phase_angle(sample_all * low_here, length_all, 1.0)[None],
    )


def per_axis_filter(signal, psd_bin, psd_weight):
    rows_count = lax.axis_size("rows")
    cols_count = lax.axis_size("cols")
    row_index = lax.axis_index("rows")
    col_index = lax.axis_index("cols")
    segment = signal.shape[1]
    groups = rows_count * cols_count
    length_all = segment * groups
    piece_len = segment // rows_count
    small_len = segment // groups
    outer_ids = jnp.arange(rows_count, dtype=jnp.int32)
    inner_ids = jnp.arange(cols_count, dtype=jnp.int32)
    moved = lax.all_to_all(
        signal.reshape(3, 1, segment), "rows", split_axis=2, concat_axis=1, tiled=True
    )
    signals, weight_rows = pair_up(moved)
    signal_count = len(weight_rows)
    signals = transform("ra,krj->kaj", phase_table(rows_count, -1.0), signals)
    signals = rotate(signals, phase_angle(col_index * outer_ids, groups, -1.0)[None, :, None])
    pieces = (
        lax.all_to_all(
            signals[0].reshape(signal_count, rows_count, 1, piece_len),
            "cols",
            split_axis=3,
            concat_axis=2,
            tiled=True,
        ),
        lax.all_to_all(
            signals[1].reshape(signal_count, rows_count, 1, piece_len),
            "cols",
            split_axis=3,
            concat_axis=2,
            tiled=True,
        ),
    )
    turned = transform("cb,kacm->kabm", phase_table(cols_count, -1.0), (pieces[0], pieces[1]))
    freq_low = outer_ids[:, None, None] + rows_count * inner_ids[None, :, None]
    sample_at = (
        row_index * piece_len
        + col_index * small_len
        + jnp.arange(small_len, dtype=jnp.int32)[None, None, :]
    )
    turned = rotate(turned, phase_angle(sample_at * freq_low, length_all, -1.0)[None])
    signals = (
        lax.all_to_all(turned[0], "cols", split_axis=2, concat_axis=3, tiled=True),
        lax.all_to_all(turned[1], "cols", split_axis=2, concat_axis=3, tiled=True),
    )
    signals = (
        lax.all_to_all(
            signals[0].reshape(signal_count, rows_count, piece_len),
            "rows",
            split_axis=1,
            concat_axis=2,
            tiled=True,
        ),
        lax.all_to_all(
            signals[1].reshape(signal_count, rows_count, piece_len),
            "rows",
            split_axis=1,
            concat_axis=2,
            tiled=True,
        ),
    )
    flat = local_section(
        (signals[0].reshape(signal_count, segment), signals[1].reshape(signal_count, segment)),
        psd_bin,
        psd_weight,
        weight_rows,
    )
    returned = (
        lax.all_to_all(
            flat[0].reshape(signal_count, 1, segment),
            "rows",
            split_axis=2,
            concat_axis=1,
            tiled=True,
        ),
        lax.all_to_all(
            flat[1].reshape(signal_count, 1, segment),
            "rows",
            split_axis=2,
            concat_axis=1,
            tiled=True,
        ),
    )
    pieces = (
        lax.all_to_all(
            returned[0].reshape(signal_count, rows_count, 1, piece_len),
            "cols",
            split_axis=3,
            concat_axis=2,
            tiled=True,
        ),
        lax.all_to_all(
            returned[1].reshape(signal_count, rows_count, 1, piece_len),
            "cols",
            split_axis=3,
            concat_axis=2,
            tiled=True,
        ),
    )
    turned = transform("bc,kabm->kacm", phase_table(cols_count, 1.0), (pieces[0], pieces[1]))
    turned = rotate(
        turned, phase_angle(inner_ids[None, :, None] * outer_ids[:, None, None], groups, 1.0)[None]
    )
    returned = (
        lax.all_to_all(turned[0], "cols", split_axis=2, concat_axis=3, tiled=True),
        lax.all_to_all(turned[1], "cols", split_axis=2, concat_axis=3, tiled=True),
    )
    real_in = returned[0].reshape(signal_count, rows_count, piece_len)
    imag_in = returned[1].reshape(signal_count, rows_count, piece_len)
    cos_rows, sin_rows = phase_table(rows_count, 1.0)
    real_out = jnp.einsum(
        "ar,kaj->krj", cos_rows, real_in, precision=lax.Precision.HIGHEST
    ) - jnp.einsum("ar,kaj->krj", sin_rows, imag_in, precision=lax.Precision.HIGHEST)
    homed = lax.all_to_all(real_out, "rows", split_axis=1, concat_axis=2, tiled=True)
    return homed.reshape(3, segment) / float(length_all)


def local(
    whitened,
    cotangent,
    lift_weight,
    conv_now,
    conv_past,
    mix_weight,
    dilations,
    psd_bin,
    psd_weight,
):
    segment = whitened.shape[1]
    layer_count = mix_weight.shape[0]
    saved = []
    field_now = lifted(lift_weight, whitened)
    for layer_id in range(layer_count):
        field_b = field_now.astype(jnp.bfloat16)
        before = from_behind(field_b[:, segment - DMAX :], ("rows", "cols"), 1)
        field_now, kept_parts = gated_layer(
            field_now,
            field_b,
            before,
            conv_now[layer_id],
            conv_past[layer_id],
            mix_weight[layer_id],
            dilations[layer_id],
        )
        saved.append(kept_parts)
    grad_field = cotangent.astype(jnp.float32)
    grads_now = [None] * layer_count
    grads_past = [None] * layer_count
    grads_mix = [None] * layer_count
    for layer_id in reversed(range(layer_count)):
        field_b, past_b, tanh_part, sigm_part, gate_b = saved[layer_id]
        grad_field_b = grad_field.astype(jnp.bfloat16)
        grad_gate = jnp.dot(
            mix_weight[layer_id].T, grad_field_b, preferred_element_type=jnp.float32
        )
        grads_mix[layer_id] = jnp.dot(grad_field_b, gate_b.T, preferred_element_type=jnp.float32)
        grad_pre = jnp.concatenate(
            [
                grad_gate * sigm_part * (1.0 - tanh_part * tanh_part),
                grad_gate * tanh_part * sigm_part * (1.0 - sigm_part),
            ],
            axis=0,
        ).astype(jnp.bfloat16)
        grads_now[layer_id] = jnp.dot(grad_pre, field_b.T, preferred_element_type=jnp.float32)
        grads_past[layer_id] = jnp.dot(grad_pre, past_b.T, preferred_element_type=jnp.float32)
        ahead_term = jnp.dot(conv_past[layer_id].T, grad_pre, preferred_element_type=jnp.float32)
        head_rim = from_behind(ahead_term[:, :DMAX], ("rows", "cols"), -1)
        grad_field = (
            grad_field
            + jnp.dot(conv_now[layer_id].T, grad_pre, preferred_element_type=jnp.float32)
            + advanced(ahead_term, dilations[layer_id], head_rim)
        )
    input_grad = jnp.dot(lift_weight.T, grad_field, precision=lax.Precision.HIGHEST)
    lift_part = jnp.dot(grad_field, whitened.T, precision=lax.Precision.HIGHEST)
    summed = lax.psum(
        (jnp.stack(grads_now), jnp.stack(grads_past), jnp.stack(grads_mix), lift_part),
        ("rows", "cols"),
    )
    scaling = 1.0 / math.sqrt(float(segment * lax.axis_size("rows") * lax.axis_size("cols")))
    data_grad = per_axis_filter(input_grad, psd_bin, psd_weight)
    return (
        data_grad,
        summed[0] * scaling,
        summed[1] * scaling,
        summed[2] * scaling,
        summed[3] * scaling,
    )


def solution(mesh):
    in_specs = (
        P(None, ("rows", "cols")),
        P(None, ("rows", "cols")),
        P(),
        P(),
        P(),
        P(),
        P(),
        P(None, "cols", "rows"),
        P(),
    )
    out_specs = (P(None, ("rows", "cols")), P(), P(), P(), P())
    return jax.shard_map(local, mesh=mesh, in_specs=in_specs, out_specs=out_specs, check_vma=False)
```

profile of v0, /device:TPU:1, one launch (start us, length us, event | category | flops | bytes accessed | tf_op | source)
XLA Modules:
  0.0 556.0 jit_solution(1703089150025152943)
XLA Ops:
  9.3 4.6 collective-permute-start
  21.3 10.8 %gather_fusion = f32[4096,2]{1,0:T(8,128)S(1)} fusion(f32[2,1024]{0,1:T(8,128)S(1)} %copy.178, s32[4096]{0:T(1024)S(1)} %broadcast_clamp_fusion), kind=kCustom, calls=%fused_computation | custom fusion | bytes 81920 | tf_op jit(solution)/shard_map/jit(_take)/gather | solution.py:111
  53.0 4.0 collective-permute-start.2
  63.9 3.1 collective-permute-done.3
  79.2 2.5 collective-permute-done.5
  83.1 3.7 copy.151
  87.3 20.4 %reduce.4 = f32[4096,3]{1,0:T(8,128)} reduce(f32[4096,1,3]{2,1,0:T(1,128)} %bitcast.335, f32[]{:T(128)} %broadcast.734), dimensions={1}, to_apply=%bitcast.265.reduce_sub_computation | reduce | bytes 98308
  107.7 3.7 reshape.486
  111.4 21.0 %all-to-all-start = ((f32[8,1,1536]{2,1,0:T(1,128)}), f32[8,1,1536]{2,1,0:T(1,128)S(1)}, u32[]{:S(2)}, u32[]{:S(2)}) async-start(f32[8,1,1536]{2,1,0:T(1,128)} %reshape.486), calls=%async_computation | async-start | bytes 98304 | tf_op jit(solution)/shard_map/all_to_all | solution.py:139
  134.4 5.1 all-to-all-done
  140.2 4.4 reshape.487
  149.9 4.2 reduce.6
  154.1 2.5 reshape.488
  156.6 14.5 %all-to-all-start.1 = ((f32[32,1,384]{2,1,0:T(1,128)}), f32[32,1,384]{2,1,0:T(1,128)S(1)}, u32[]{:S(2)}, u32[]{:S(2)}) async-start(f32[32,1,384]{2,1,0:T(1,128)} %reshape.488), calls=%async_computation.1 | async-start | bytes 98304 | tf_op jit(solution)/shard_map/all_to_all | solution.py:147
  175.2 4.0 reduce.8
  180.5 7.7 %all-to-all-start.2 = ((f32[32,1,384]{2,1,0:T(1,128)}), f32[32,1,384]{2,1,0:T(1,128)S(1)}, u32[]{:S(2)}, u32[]{:S(2)}) async-start(f32[32,1,384]{2,1,0:T(1,128)} %reshape.490), calls=%async_computation.2 | async-start | bytes 98304 | tf_op jit(solution)/shard_map/all_to_all | solution.py:154
  201.8 2.4 multiply_add_fusion.1
  206.2 6.2 %all-to-all-start.3 = ((f32[32,1,384]{2,1,0:T(1,128)}), f32[32,1,384]{2,1,0:T(1,128)}, u32[]{:S(2)}, u32[]{:S(2)}) async-start(f32[32,1,384]{2,1,0:T(1,128)} %reshape.492), calls=%async_computation.3 | async-start | bytes 98304 | tf_op jit(solution)/shard_map/all_to_all | solution.py:171
  215.7 4.1 all-to-all-done.3
  219.8 4.5 all-to-all-start.5
  227.9 3.8 all-to-all-done.5
  231.7 3.4 all-to-all-start.4
  242.2 4.7 all-to-all-start.6
  247.8 6.3 %all-to-all-done.6 = f32[3,8,512]{2,0,1:T(4,128)S(1)} async-done(((f32[3,8,512]{2,0,1:T(4,128)}), f32[3,8,512]{2,0,1:T(4,128)S(1)}, u32[]{:S(2)}, u32[]{:S(2)}) %all-to-all-start.6) | async-done | bytes 49184 | tf_op jit(solution)/shard_map/all_to_all | solution.py:182
  260.1 2.4 copy.188
  262.5 19.4 %reduce.12 = f32[4096,3]{1,0:T(8,128)} reduce(f32[4096,1,3]{2,1,0:T(1,128)S(1)} %bitcast.337, f32[]{:T(128)} %broadcast.734), dimensions={1}, to_apply=%bitcast.275.reduce_sub_computation | reduce | bytes 98308
  281.9 3.7 reshape.496
  285.6 3.3 all-to-all-start.7
  289.9 2.4 copy.193
  292.3 19.4 %reduce.16 = f32[4096,3]{1,0:T(8,128)} reduce(f32[4096,1,3]{2,1,0:T(1,128)S(1)} %bitcast.338, f32[]{:T(128)} %broadcast.734), dimensions={1}, to_apply=%bitcast.279.reduce_sub_computation | reduce | bytes 98308
  311.7 3.7 reshape.500
  315.5 6.8 %all-to-all-start.9 = ((f32[8,1,1536]{2,1,0:T(1,128)}), f32[8,1,1536]{2,1,0:T(1,128)S(1)}, u32[]{:S(2)}, u32[]{:S(2)}) async-start(f32[8,1,1536]{2,1,0:T(1,128)} %reshape.500), calls=%async_computation.9 | async-start | bytes 98304 | tf_op jit(solution)/shard_map/all_to_all | solution.py:204
  323.0 3.0 reshape.497
  326.1 4.3 copy.190
  330.3 4.0 reduce.14
  335.6 6.1 %all-to-all-start.8 = ((f32[32,1,384]{2,1,0:T(1,128)}), f32[32,1,384]{2,1,0:T(1,128)S(1)}, u32[]{:S(2)}, u32[]{:S(2)}) async-start(f32[32,1,384]{2,1,0:T(1,128)} %reshape.498), calls=%async_computation.8 | async-start | bytes 98304 | tf_op jit(solution)/shard_map/all_to_all | solution.py:213
  342.7 78.9 %all-reduce = (f32[3,64,64]{2,1,0:T(8,128)S(1)}, f32[64,3]{0,1:T(4,128)S(1)}) all-reduce(f32[3,64,64]{2,1,0:T(8,128)S(1)} %pad_maximum_fusion.6, f32[64,3]{0,1:T(4,128)S(1)} %fusion.359), channel_id=1, replica_groups=mesh['rows'=8,'cols'=32] {'rows','cols'}, use_global_device_ids=true, to_apply=%region_2.0 | all-reduce | flops 12480 | bytes 99840 | tf_op jit(solution)/shard_map/psum | solution.py:303
  422.4 3.0 reshape.501
  425.4 4.0 copy.195
  429.4 3.2 reduce.18
  433.9 4.8 all-to-all-start.10
  443.4 2.7 all-to-all-done.10
  451.7 4.8 all-to-all-start.12
  458.2 5.6 %all-to-all-done.12 = f32[32,1,384]{2,1,0:T(1,128)S(1)} async-done(((f32[32,1,384]{2,1,0:T(1,128)}), f32[32,1,384]{2,1,0:T(1,128)S(1)}, u32[]{:S(2)}, u32[]{:S(2)}) %all-to-all-start.12) | async-done | bytes 49184 | tf_op jit(solution)/shard_map/all_to_all | solution.py:234
  463.8 3.9 all-to-all-start.11
  469.5 5.6 %all-to-all-done.11 = f32[32,1,384]{2,1,0:T(1,128)S(1)} async-done(((f32[32,1,384]{2,1,0:T(1,128)}), f32[32,1,384]{2,1,0:T(1,128)S(1)}, u32[]{:S(2)}, u32[]{:S(2)}) %all-to-all-start.11) | async-done | bytes 49184 | tf_op jit(solution)/shard_map/all_to_all | solution.py:233
  477.4 5.5 all-to-all-start.13
  482.9 63.5 %all-reduce.4.cloned.1.call-done = (f32[3,128,64]{1,2,0:T(8,128)}, f32[3,128,64]{1,2,0:T(8,128)}) async-done(((f32[3,128,64]{1,2,0:T(8,128)}, f32[3,128,64]{1,2,0:T(8,128)}), (f32[3,128,64]{1,2,0:T(8,128)}, f32[3,128,64]{1,2,0:T(8,128)})) %all-reduce.4.cloned.1.call-update) | async-done | bytes 196624 | tf_op jit(solution)/shard_map/psum | solution.py:303
  (267 shorter events, 114.5 us)
Async XLA Ops:
  8.0 24.8 %copy-start.38 = (f32[64]{0:T(128)}, f32[64]{0:T(128)S(1)}, u32[]{:S(2)}) copy-start(f32[64]{0:T(128)S(1)} %get-tuple-element.29) | copy-start | bytes 772
  8.0 24.8 %copy-start.40 = (f32[64]{0:T(128)}, f32[64]{0:T(128)S(1)}, u32[]{:S(2)}) copy-start(f32[64]{0:T(128)S(1)} %get-tuple-element.30) | copy-start | bytes 772
  9.2 37.5 %copy-start.5 = (bf16[64,4096]{1,0:T(8,128)(2,1)}, bf16[64,4096]{1,0:T(8,128)(2,1)S(1)}, u32[]{:S(2)}) copy-start(bf16[64,4096]{1,0:T(8,128)(2,1)S(1)} %fusion.33) | copy-start | bytes 1572868
  9.2 23.6 %copy-start.24 = (bf16[3,128,64]{1,2,0:T(8,128)(2,1)S(1)}, bf16[3,128,64]{1,2,0:T(8,128)(2,1)}, u32[]{:S(2)}) copy-start(bf16[3,128,64]{1,2,0:T(8,128)(2,1)} %param.12) | copy-start | bytes 147460
  9.3 37.5 %collective-permute-start = (bf16[64,256]{1,0:T(8,128)(2,1)S(1)}, bf16[64,256]{1,0:T(8,128)(2,1)S(1)}, u32[]{:S(2)}, u32[]{:S(2)}) collective-permute-start(bf16[64,256]{1,0:T(8,128)(2,1)S(1)} %slice.140), channel_id=1, source_target_pairs={{0,1},{1,2},{2,3},{3,4},{4,5},{5,6},{6,7},{7,8},{8,9},{9,10},{10,1... | collective-permute-start | bytes 98312 | tf_op jit(solution)/shard_map/ppermute | solution.py:14
  32.1 14.7 %copy-start.23 = (bf16[3,128,64]{1,2,0:T(8,128)(2,1)S(1)}, bf16[3,128,64]{1,2,0:T(8,128)(2,1)}, u32[]{:S(2)}) copy-start(bf16[3,128,64]{1,2,0:T(8,128)(2,1)} %param.13) | copy-start | bytes 147460
  34.3 13.0 %copy-start.18 = (f32[2,64,64]{2,1,0:T(8,128)}, f32[2,64,64]{2,1,0:T(8,128)S(1)}, u32[]{:S(2)}) copy-start(f32[2,64,64]{2,1,0:T(8,128)S(1)} %select_bitcast_fusion) | copy-start | bytes 98308
  48.5 29.5 %copy-start = (bf16[64,4096]{1,0:T(8,128)(2,1)}, bf16[64,4096]{1,0:T(8,128)(2,1)S(1)}, u32[]{:S(2)}) copy-start(bf16[64,4096]{1,0:T(8,128)(2,1)S(1)} %get-tuple-element.34) | copy-start | bytes 1572868
  48.6 3.1 collective-permute-start.1
  53.0 5.1 collective-permute-start.2
  60.9 6.2 %collective-permute-start.3 = (f32[64,256]{1,0:T(8,128)S(1)}, f32[64,256]{1,0:T(8,128)S(1)}, u32[]{:S(2)}, u32[]{:S(2)}) collective-permute-start(f32[64,256]{1,0:T(8,128)S(1)} %slice.149), channel_id=1, source_target_pairs={{1,0},{2,1},{3,2},{4,3},{5,4},{6,5},{7,6},{8,7},{9,8},{10,9},{11,1... | collective-permute-start | bytes 196616 | tf_op jit(solution)/shard_map/ppermute | solution.py:14
  68.5 9.6 %copy-start.12 = (bf16[64,4096]{1,0:T(8,128)(2,1)}, bf16[64,4096]{1,0:T(8,128)(2,1)S(1)}, u32[]{:S(2)}) copy-start(bf16[64,4096]{1,0:T(8,128)(2,1)S(1)} %get-tuple-element.11) | copy-start | bytes 1572868
  68.5 9.6 %copy-start.13 = (bf16[64,4096]{1,0:T(8,128)(2,1)}, bf16[64,4096]{1,0:T(8,128)(2,1)S(1)}, u32[]{:S(2)}) copy-start(bf16[64,4096]{1,0:T(8,128)(2,1)S(1)} %get-tuple-element.12) | copy-start | bytes 1572868
  68.8 5.6 %collective-permute-start.4 = (f32[64,256]{1,0:T(8,128)S(1)}, f32[64,256]{1,0:T(8,128)S(1)}, u32[]{:S(2)}, u32[]{:S(2)}) collective-permute-start(f32[64,256]{1,0:T(8,128)S(1)} %slice.150), channel_id=1, source_target_pairs={{1,0},{2,1},{3,2},{4,3},{5,4},{6,5},{7,6},{8,7},{9,8},{10,9},{11,1... | collective-permute-start | bytes 196616 | tf_op jit(solution)/shard_map/ppermute | solution.py:14
  76.1 5.6 %collective-permute-start.5 = (f32[64,256]{1,0:T(8,128)S(1)}, f32[64,256]{1,0:T(8,128)S(1)}, u32[]{:S(2)}, u32[]{:S(2)}) collective-permute-start(f32[64,256]{1,0:T(8,128)S(1)} %slice.151), channel_id=1, source_target_pairs={{1,0},{2,1},{3,2},{4,3},{5,4},{6,5},{7,6},{8,7},{9,8},{10,9},{11,1... | collective-permute-start | bytes 196616 | tf_op jit(solution)/shard_map/ppermute | solution.py:14
  111.4 28.0 %all-to-all-start = ((f32[8,1,1536]{2,1,0:T(1,128)}), f32[8,1,1536]{2,1,0:T(1,128)S(1)}, u32[]{:S(2)}, u32[]{:S(2)}) async-start(f32[8,1,1536]{2,1,0:T(1,128)} %reshape.486), calls=%async_computation | async-start | bytes 98304 | tf_op jit(solution)/shard_map/all_to_all | solution.py:139
  146.8 24.3 %copy-start.1 = (bf16[64,4096]{1,0:T(8,128)(2,1)S(1)}, bf16[64,4096]{1,0:T(8,128)(2,1)}, u32[]{:S(2)}) copy-start(bf16[64,4096]{1,0:T(8,128)(2,1)} %copy-done) | copy-start | bytes 1572868
  154.1 19.4 %copy-start.25 = (f32[3,8,1,512]{3,1,0,2:T(8,128)S(1)}, f32[3,8,1,512]{3,1,0,2:T(8,128)}, u32[]{:S(2)}) copy-start(f32[3,8,1,512]{3,1,0,2:T(8,128)} %get-tuple-element.21) | copy-start | bytes 147460
  156.6 23.8 %all-to-all-start.1 = ((f32[32,1,384]{2,1,0:T(1,128)}), f32[32,1,384]{2,1,0:T(1,128)S(1)}, u32[]{:S(2)}, u32[]{:S(2)}) async-start(f32[32,1,384]{2,1,0:T(1,128)} %reshape.488), calls=%async_computation.1 | async-start | bytes 98304 | tf_op jit(solution)/shard_map/all_to_all | solution.py:147
  180.5 14.9 %all-to-all-start.2 = ((f32[32,1,384]{2,1,0:T(1,128)}), f32[32,1,384]{2,1,0:T(1,128)S(1)}, u32[]{:S(2)}, u32[]{:S(2)}) async-start(f32[32,1,384]{2,1,0:T(1,128)} %reshape.490), calls=%async_computation.2 | async-start | bytes 98304 | tf_op jit(solution)/shard_map/all_to_all | solution.py:154
  197.3 15.1 %copy-start.8 = (bf16[64,4096]{1,0:T(8,128)(2,1)S(1)}, bf16[64,4096]{1,0:T(8,128)(2,1)}, u32[]{:S(2)}) copy-start(bf16[64,4096]{1,0:T(8,128)(2,1)} %copy-done.7) | copy-start | bytes 1572868
  206.2 13.6 %all-to-all-start.3 = ((f32[32,1,384]{2,1,0:T(1,128)}), f32[32,1,384]{2,1,0:T(1,128)}, u32[]{:S(2)}, u32[]{:S(2)}) async-start(f32[32,1,384]{2,1,0:T(1,128)} %reshape.492), calls=%async_computation.3 | async-start | bytes 98304 | tf_op jit(solution)/shard_map/all_to_all | solution.py:171
  212.4 11.9 %copy-start.3 = (bf16[64,4096]{1,0:T(8,128)(2,1)S(1)}, bf16[64,4096]{1,0:T(8,128)(2,1)}, u32[]{:S(2)}) copy-start(bf16[64,4096]{1,0:T(8,128)(2,1)} %copy-done.2) | copy-start | bytes 1572868
  214.9 21.7 %copy-start.6 = (bf16[64,4096]{1,0:T(8,128)(2,1)S(1)}, bf16[64,4096]{1,0:T(8,128)(2,1)}, u32[]{:S(2)}) copy-start(bf16[64,4096]{1,0:T(8,128)(2,1)} %copy-done.5) | copy-start | bytes 1572868
  219.8 12.0 %all-to-all-start.5 = ((f32[32,1,384]{2,1,0:T(1,128)}), f32[32,1,384]{2,1,0:T(1,128)}, u32[]{:S(2)}, u32[]{:S(2)}) async-start(f32[32,1,384]{2,1,0:T(1,128)} %reshape.494), calls=%async_computation.5 | async-start | bytes 98304 | tf_op jit(solution)/shard_map/all_to_all | solution.py:172
  225.2 11.4 %copy-start.9 = (bf16[64,4096]{1,0:T(8,128)(2,1)S(1)}, bf16[64,4096]{1,0:T(8,128)(2,1)}, u32[]{:S(2)}) copy-start(bf16[64,4096]{1,0:T(8,128)(2,1)} %copy-done.7) | copy-start | bytes 1572868
  225.2 11.4 %copy-start.11 = (bf16[64,4096]{1,0:T(8,128)(2,1)S(1)}, bf16[64,4096]{1,0:T(8,128)(2,1)}, u32[]{:S(2)}) copy-start(bf16[64,4096]{1,0:T(8,128)(2,1)} %copy-done.10) | copy-start | bytes 1572868
  225.2 11.4 %copy-start.30 = (bf16[64,256]{1,0:T(8,128)(2,1)S(1)}, bf16[64,256]{1,0:T(8,128)(2,1)}, u32[]{:S(2)}) copy-start(bf16[64,256]{1,0:T(8,128)(2,1)} %copy-done.29) | copy-start | bytes 98308
  231.7 10.4 %all-to-all-start.4 = ((f32[3,8,512]{2,0,1:T(4,128)}), f32[3,8,512]{2,0,1:T(4,128)S(1)}, u32[]{:S(2)}, u32[]{:S(2)}) async-start(f32[3,8,512]{2,0,1:T(4,128)} %reshape.475), calls=%async_computation.4 | async-start | bytes 131072 | tf_op jit(solution)/shard_map/all_to_all | solution.py:175
  237.1 17.8 %copy-start.16 = (f32[64,64]{0,1:T(8,128)S(1)}, f32[64,64]{0,1:T(8,128)}, u32[]{:S(2)}) copy-start(f32[64,64]{0,1:T(8,128)} %copy.171) | copy-start | bytes 49156
  237.1 17.8 %copy-start.17 = (f32[64,64]{0,1:T(8,128)S(1)}, f32[64,64]{0,1:T(8,128)}, u32[]{:S(2)}) copy-start(f32[64,64]{0,1:T(8,128)} %copy.174) | copy-start | bytes 49156
  237.1 18.6 %copy-start.19 = (f32[2,64,64]{2,1,0:T(8,128)S(1)}, f32[2,64,64]{2,1,0:T(8,128)}, u32[]{:S(2)}) copy-start(f32[2,64,64]{2,1,0:T(8,128)} %copy-done.18) | copy-start | bytes 98308
  237.1 18.6 %copy-start.21 = (f32[1,64,64]{2,1,0:T(8,128)S(1)}, f32[1,64,64]{2,1,0:T(8,128)}, u32[]{:S(2)}) copy-start(f32[1,64,64]{2,1,0:T(8,128)} %slice.152) | copy-start | bytes 49156
  242.2 11.9 %all-to-all-start.6 = ((f32[3,8,512]{2,0,1:T(4,128)}), f32[3,8,512]{2,0,1:T(4,128)S(1)}, u32[]{:S(2)}, u32[]{:S(2)}) async-start(f32[3,8,512]{2,0,1:T(4,128)} %reshape.476), calls=%async_computation.6 | async-start | bytes 131072 | tf_op jit(solution)/shard_map/all_to_all | solution.py:182
  246.9 11.2 %copy-start.14 = (f32[64,64]{1,0:T(8,128)S(1)}, f32[64,64]{1,0:T(8,128)}, u32[]{:S(2)}) copy-start(f32[64,64]{1,0:T(8,128)} %get-tuple-element.40) | copy-start | bytes 49156
  246.9 11.2 %copy-start.15 = (f32[64,64]{1,0:T(8,128)S(1)}, f32[64,64]{1,0:T(8,128)}, u32[]{:S(2)}) copy-start(f32[64,64]{1,0:T(8,128)} %get-tuple-element.41) | copy-start | bytes 49156
  285.6 29.8 %all-to-all-start.7 = ((f32[8,1,1536]{2,1,0:T(1,128)}), f32[8,1,1536]{2,1,0:T(1,128)S(1)}, u32[]{:S(2)}, u32[]{:S(2)}) async-start(f32[8,1,1536]{2,1,0:T(1,128)} %reshape.496), calls=%async_computation.7 | async-start | bytes 98304 | tf_op jit(solution)/shard_map/all_to_all | solution.py:197
  289.0 257.4 %all-reduce.4.cloned.1.call-start = ((), (), s32[]{:S(2)}) async-start(), calls=%async_computation.14 | async-start | bytes 393216 | tf_op jit(solution)/shard_map/psum | solution.py:303
  311.7 10.5 %copy-start.26 = (f32[1,64,64]{2,1,0:T(8,128)S(1)}, f32[1,64,64]{2,1,0:T(8,128)}, u32[]{:S(2)}) copy-start(f32[1,64,64]{2,1,0:T(8,128)} %convolution_bitcast_fusion.18) | copy-start | bytes 49156
  311.7 10.5 %copy-start.27 = (f32[1,64,64]{2,1,0:T(8,128)S(1)}, f32[1,64,64]{2,1,0:T(8,128)}, u32[]{:S(2)}) copy-start(f32[1,64,64]{2,1,0:T(8,128)} %convolution_bitcast_fusion.19) | copy-start | bytes 49156
  311.7 10.5 %copy-start.32 = (f32[1,64,64]{2,1,0:T(8,128)S(1)}, f32[1,64,64]{2,1,0:T(8,128)}, u32[]{:S(2)}) copy-start(f32[1,64,64]{2,1,0:T(8,128)} %convolution_bitcast_fusion.17) | copy-start | bytes 49156
  315.5 20.1 %all-to-all-start.9 = ((f32[8,1,1536]{2,1,0:T(1,128)}), f32[8,1,1536]{2,1,0:T(1,128)S(1)}, u32[]{:S(2)}, u32[]{:S(2)}) async-start(f32[8,1,1536]{2,1,0:T(1,128)} %reshape.500), calls=%async_computation.9 | async-start | bytes 98304 | tf_op jit(solution)/shard_map/all_to_all | solution.py:204
  330.3 11.4 %copy-start.22 = (f32[3,4096]{1,0:T(4,128)S(1)}, f32[3,4096]{1,0:T(4,128)}, u32[]{:S(2)}) copy-start(f32[3,4096]{1,0:T(4,128)} %param.9) | copy-start | bytes 147460
  335.6 98.3 %all-to-all-start.8 = ((f32[32,1,384]{2,1,0:T(1,128)}), f32[32,1,384]{2,1,0:T(1,128)S(1)}, u32[]{:S(2)}, u32[]{:S(2)}) async-start(f32[32,1,384]{2,1,0:T(1,128)} %reshape.498), calls=%async_computation.8 | async-start | bytes 98304 | tf_op jit(solution)/shard_map/all_to_all | solution.py:213
  433.9 12.1 %all-to-all-start.10 = ((f32[32,1,384]{2,1,0:T(1,128)}), f32[32,1,384]{2,1,0:T(1,128)S(1)}, u32[]{:S(2)}, u32[]{:S(2)}) async-start(f32[32,1,384]{2,1,0:T(1,128)} %reshape.502), calls=%async_computation.10 | async-start | bytes 98304 | tf_op jit(solution)/shard_map/all_to_all | solution.py:220
  451.7 12.1 %all-to-all-start.12 = ((f32[32,1,384]{2,1,0:T(1,128)}), f32[32,1,384]{2,1,0:T(1,128)S(1)}, u32[]{:S(2)}, u32[]{:S(2)}) async-start(f32[32,1,384]{2,1,0:T(1,128)} %reshape.506), calls=%async_computation.12 | async-start | bytes 98304 | tf_op jit(solution)/shard_map/all_to_all | solution.py:234
  463.8 11.3 %all-to-all-start.11 = ((f32[32,1,384]{2,1,0:T(1,128)}), f32[32,1,384]{2,1,0:T(1,128)S(1)}, u32[]{:S(2)}, u32[]{:S(2)}) async-start(f32[32,1,384]{2,1,0:T(1,128)} %reshape.504), calls=%async_computation.11 | async-start | bytes 98304 | tf_op jit(solution)/shard_map/all_to_all | solution.py:233
  477.4 70.6 %all-to-all-start.13 = ((f32[3,8,512]{2,0,1:T(4,128)}), f32[3,8,512]{2,0,1:T(4,128)S(1)}, u32[]{:S(2)}, u32[]{:S(2)}) async-start(f32[3,8,512]{2,0,1:T(4,128)} %copy.204), calls=%async_computation.13 | async-start | bytes 131072 | tf_op jit(solution)/shard_map/all_to_all | solution.py:242
  (19 other events, 77.5 us)
Sparse Core Ops, SparseCore 0:
  296.0 250.3 all-reduce.3
where the time goes:
time: 566 us; the launch traced here: 556 us
  starting transfers between devices  114 us (20%)
  waiting for transfers between devices  109 us (19%)
  other arithmetic  97.2 us (17%)
  local copies, waits for them, and re-layouts  90 us (16%)
  blocking collectives  78.9 us (14%)
  matrix products  40.8 us (7%)
  between operations  25.7 us (5%)
    psum x1, blocking collectives, local(): lax.psum((jnp.stack(grads_now), jnp.stack(grads_past), jnp.stack(grads_mi...  78.9 us
    unnamed x8, other arithmetic  76 us
    psum x1, waiting for transfers between devices, local(): lax.psum((jnp.stack(grads_now), jnp.stack(grads_past), jnp.stack(grads_mi...  63.5 us
    unnamed x117, local copies, waits for them, and re-layouts  39.2 us
    all_to_all x1, starting transfers between devices, per_axis_filter(): lax.all_to_all(signal.reshape(3, 1, segment), 'rows', split_axis=2, conca...  21 us
    ppermute x6, starting transfers between devices, from_behind(): return lax.ppermute(array, axis, pairs)  16.8 us
    all_to_all x1, starting transfers between devices, per_axis_filter(): lax.all_to_all(signals[0].reshape(signal_count, rows_count, 1, piece_len)...  14.5 us
    gather x2, local copies, waits for them, and re-layouts, local_section(): weights = jnp.take(psd_weight, bins_here, axis=1)  11.5 us
  transfers between devices with their start and end apart: 21, of which 15 were waited for; matrix products, arithmetic and copies ran while one was open for 23% of the time, Pallas kernels for 0%

commit v1 on v0

v1 whole, which is shorter than its diff:
```python
import functools
import math

import jax
import jax.numpy as jnp
import numpy as np
from jax import lax
from jax.experimental import pallas as pl
from jax.experimental.pallas import tpu as pltpu
from jax.sharding import PartitionSpec as P

F32 = jnp.float32
BF16 = jnp.bfloat16
BOTH = ("rows", "cols")
RIM = 640
BASE = 1024
SEG = 4096
WIDE = BASE + SEG + 1024
STEP = 512
LANES = 128


def lane_ids(rows):
    return lax.broadcasted_iota(jnp.int32, (rows, LANES), 1)


def dot32(a, b):
    return jnp.dot(a, b, preferred_element_type=F32)


def dot_nt(a, b, precision=None):
    return lax.dot_general(
        a, b, (((1,), (1,)), ((), ())), preferred_element_type=F32, precision=precision
    )


def columns(start, width):
    return pl.ds(pl.multiple_of(start, LANES), width)


def conv_kernel(
    dil, wh, wh_left, wh_right, cot, cot_right, lift, lift_rows, w_cat, w_cat_t, mix, mix_t,
    sent, late, f0, f1, f2, x1, x2, fl1, fl2, sg1, sg2, gt1, gt2, ah, ah2, dp, dp2,
    g_conv, g_mix, g_lift, x_t,
):
    lane = lane_ids(64)

    def split(layer):
        d = dil[layer]
        return pl.multiple_of((d // LANES) * LANES, LANES), d % LANES

    def behind(ref, start, width, layer):
        whole, rest = split(layer)
        first = start - whole - LANES
        turned = [
            pltpu.roll(ref[:, columns(first + LANES * k, LANES)], rest, 1)
            for k in range(width // LANES + 1)
        ]
        keep = lane < rest
        return jnp.concatenate(
            [jnp.where(keep, turned[k], turned[k + 1]) for k in range(width // LANES)], axis=1
        )

    def beyond(ref, start, width, layer):
        whole, rest = split(layer)
        first = start + whole
        back = (LANES - rest) % LANES
        turned = [
            pltpu.roll(ref[:, columns(first + LANES * k, LANES)], back, 1)
            for k in range(width // LANES + 1)
        ]
        keep = lane < LANES - rest
        return jnp.concatenate(
            [jnp.where(keep, turned[k], turned[k + 1]) for k in range(width // LANES)], axis=1
        )

    lift_cols = [jnp.broadcast_to(lift[:, i : i + 1], (64, LANES)) for i in range(3)]

    def lift_tile(src, at, dst_at):
        tile = src[:, columns(at, LANES)]
        f0[:, columns(dst_at, LANES)] = (
            lift_cols[0] * tile[0:1] + lift_cols[1] * tile[1:2] + lift_cols[2] * tile[2:3]
        )

    zero_tile = jnp.zeros((64, LANES), F32)
    for k in range(3):
        f0[:, k * LANES : (k + 1) * LANES] = zero_tile
    f1[:, 384:512] = zero_tile
    f2[:, 640:768] = zero_tile
    for k in range(RIM // LANES):
        lift_tile(wh_left, k * LANES, BASE - RIM + k * LANES)
        lift_tile(wh_right, k * LANES, BASE + SEG + k * LANES)

    def lift_step(i, carry):
        for k in range(4):
            lift_tile(wh, (i * 4 + k) * LANES, BASE + (i * 4 + k) * LANES)
        return carry

    lax.fori_loop(0, SEG // (4 * LANES), lift_step, 0)
    for k in range(3):
        at = BASE + SEG + RIM + k * LANES
        ah[:, at : at + LANES] = zero_tile
        ah2[:, at : at + LANES] = zero_tile
        ah2[:, at - LANES : at] = zero_tile

    def gates(layer, field, start, width):
        now = field[:, columns(start, width)]
        both = jnp.concatenate(
            [now.astype(BF16), behind(field, start, width, layer).astype(BF16)], axis=0
        )
        pre = dot32(w_cat[layer], both)
        filt = jnp.tanh(pre[:64])
        sig = 0.5 * jnp.tanh(0.5 * pre[64:]) + 0.5
        gate = (filt * sig).astype(BF16)
        return now, both, filt, sig, gate

    def forward(layer, field, field_next, x, fl, sg, gt, start, width):
        now, both, filt, sig, gate = gates(layer, field, start, width)
        at = columns(start, width)
        x[:, at] = both
        fl[:, at] = filt
        sg[:, at] = sig
        gt[:, at] = gate
        field_next[:, at] = now + dot32(mix[layer], gate)

    def run_forward(layer, field, field_next, x, fl, sg, gt, left):
        forward(layer, field, field_next, x, fl, sg, gt, BASE - left, left)

        def step(i, carry):
            forward(layer, field, field_next, x, fl, sg, gt, BASE + i * STEP, STEP)
            return carry

        lax.fori_loop(0, SEG // STEP, step, 0)
        forward(layer, field, field_next, x, fl, sg, gt, BASE + SEG, RIM)

    run_forward(0, f0, f1, x1, fl1, sg1, gt1, 512)
    run_forward(1, f1, f2, x2, fl2, sg2, gt2, 256)

    g_conv[...] = jnp.zeros_like(g_conv)
    g_mix[...] = jnp.zeros_like(g_mix)

    def backward(layer, dfield, dfield_b, both, filt, sig, gate, ah_out, dp_out, start, width, own):
        d_gate = dot32(mix_t[layer], dfield_b)
        d_pre = jnp.concatenate(
            [d_gate * sig * (1.0 - filt * filt), d_gate * filt * sig * (1.0 - sig)], axis=0
        ).astype(BF16)
        back = dot32(w_cat_t[layer], d_pre)
        at = columns(start, width)
        dp_out[:, at] = dfield + back[:64]
        ah_out[:, at] = back[64:]
        if own:
            g_conv[layer] += dot_nt(d_pre, both)
            g_mix[layer] += dot_nt(
                dfield_b, jnp.concatenate([jnp.zeros((64, width), BF16), gate], axis=0)
            )

    def last_layer(start, width, cot_ref, cot_at, own):
        now, both, filt, sig, gate = gates(2, f2, start, width)
        dfield_b = cot_ref[:, columns(cot_at, width)]
        backward(2, dfield_b.astype(F32), dfield_b, both, filt, sig, gate, ah, dp, start, width, own)

    def step3(i, carry):
        last_layer(BASE + i * STEP, STEP, cot, i * STEP, True)
        return carry

    lax.fori_loop(0, SEG // STEP, step3, 0)
    last_layer(BASE + SEG, RIM, cot_right, 0, False)

    def saved_layer(layer, x, fl, sg, gt, ah_in, dp_in, ah_out, dp_out, start, width, own):
        at = columns(start, width)
        dfield = dp_in[:, at] + beyond(ah_in, start, width, layer + 1)
        backward(
            layer, dfield, dfield.astype(BF16), x[:, at], fl[:, at], sg[:, at], gt[:, at],
            ah_out, dp_out, start, width, own,
        )

    def step2(i, carry):
        saved_layer(1, x2, fl2, sg2, gt2, ah, dp, ah2, dp2, BASE + i * STEP, STEP, True)
        return carry

    lax.fori_loop(0, SEG // STEP, step2, 0)
    saved_layer(1, x2, fl2, sg2, gt2, ah, dp, ah2, dp2, BASE + SEG, 512, False)

    def step1(i, carry):
        saved_layer(0, x1, fl1, sg1, gt1, ah2, dp2, ah, dp, BASE + i * STEP, STEP, True)
        return carry

    lax.fori_loop(0, SEG // STEP, step1, 0)
    saved_layer(0, x1, fl1, sg1, gt1, ah2, dp2, ah, dp, BASE + SEG, 256, False)

    x_t[...] = jnp.zeros_like(x_t)
    g_lift[...] = jnp.zeros_like(g_lift)
    row_of = lax.broadcasted_iota(jnp.int32, (64, 64), 0) % 16
    rows_all = lift_rows[...]

    def step0(i, carry):
        start = BASE + i * 256
        dfield = dp[:, columns(start, 256)] + beyond(ah, start, 256, 0)
        placed = jnp.where(row_of == i, rows_all, 0.0)
        x_t[0:64] += lax.dot(
            placed, dfield, precision=lax.Precision.HIGHEST, preferred_element_type=F32
        )
        seen = jnp.concatenate(
            [jnp.zeros((64, 256), F32), wh[:, columns(i * 256, 256)], jnp.zeros((56, 256), F32)],
            axis=0,
        )
        g_lift[...] += dot_nt(dfield, seen, lax.Precision.HIGHEST)
        return carry

    lax.fori_loop(0, 16, step0, 0)

    low = lane_ids(256) < 64
    early = jnp.concatenate([g_conv[2], g_mix[1], g_lift[...]], axis=0)
    sent[:, 0, 0:128] = jnp.where(low, x_t[...].T, early)
    sent[:, 0, 128:256] = jnp.concatenate([g_conv[0], g_conv[1]], axis=0)
    late[...] = jnp.concatenate([pltpu.roll(g_conv[2], 64, 1), g_mix[0], g_mix[2]], axis=0)


def swap(x):
    first = (lane_ids(x.shape[0]) // 16) % 2 == 0
    return jnp.where(first, pltpu.roll(x, LANES - 16, 1), -pltpu.roll(x, 16, 1))


def wide_dot(table, x, sign):
    low = lane_ids(256) < 64
    parts = []
    for value in (x, sign * swap(x)):
        high = value.astype(BF16)
        rest = value - high.astype(F32)
        parts.append((high, jnp.where(low, high.astype(F32), pltpu.roll(rest, 64, 1)).astype(BF16)))
    mixed = dot32(table[0], jnp.concatenate([parts[0][1], parts[1][1]], axis=0))
    small = dot32(table[1], jnp.concatenate([parts[0][0], parts[1][0]], axis=0))
    return mixed + pltpu.roll(mixed, 64, 1) + small


def first_kernel(got, late, table, twist_cos, twist_sin, inner, sent, sums):
    data = got[:, 0, 0:128]
    rest = got[:, 0, 128:256]
    low = lane_ids(256) < 64
    x = jnp.where(low, data, 0.0)
    sums[:, 0:128] = jnp.broadcast_to(jnp.sum(data, axis=0, keepdims=True), (8, 128))
    sums[:, 128:256] = jnp.broadcast_to(jnp.sum(rest, axis=0, keepdims=True), (8, 128))
    y = wide_dot(table, x, 1.0)
    y = y * twist_cos[...] + swap(y) * twist_sin[...]
    y = lax.dot(y, inner[...], precision=lax.Precision.HIGHEST, preferred_element_type=F32)
    sent[:, 0, :] = jnp.where(low, y, late[...])


def middle_kernel(got, sums, weights, table, sent, sums_late):
    data = got[:, 0, :]
    low = lane_ids(256) < 64
    x = jnp.where(low, data, 0.0)
    sums_late[...] = jnp.broadcast_to(jnp.sum(data, axis=0, keepdims=True), (8, 128))
    y = wide_dot(table, x, 1.0)
    y = jnp.where(low, y * weights[...], 0.0)
    y = wide_dot(table, y, -1.0)
    sent[:, 0, 0:128] = jnp.where(low, y, jnp.broadcast_to(sums[0:1, 0:128], (256, 128)))
    sent[:, 0, 128:256] = jnp.broadcast_to(sums[0:1, 128:256], (256, 128))


def third_kernel(got, sums_late, table, twist_cos, twist_sin, inner, sent):
    low = lane_ids(256) < 64
    x = jnp.where(low, got[:, 0, 0:128], 0.0)
    y = dot_nt(x, inner[...], lax.Precision.HIGHEST)
    y = y * twist_cos[...] - swap(y) * twist_sin[...]
    y = wide_dot(table, y, -1.0)
    sent[:, 0, :] = jnp.where(low, y, jnp.broadcast_to(sums_late[0:1], (256, 128)))


def last_kernel(scaling, got, got_before, data_grad, grad_now, grad_past, grad_mix, grad_lift):
    last = got[:, 0, :]
    turned = last.T
    for channel in range(3):
        for m in range(16):
            row = channel * 16 + m
            data_grad[channel : channel + 1, m * 256 : (m + 1) * 256] = turned[row : row + 1]
    late = pltpu.roll(last, 64, 1) * scaling
    early = pltpu.roll(got_before[:, 0, 0:128], 64, 1) * scaling
    main = got_before[:, 0, 128:256] * scaling
    main_past = pltpu.roll(main, 64, 1)
    for layer in range(2):
        grad_now[layer] = main[layer * 128 : (layer + 1) * 128, 0:64]
        grad_past[layer] = main_past[layer * 128 : (layer + 1) * 128, 0:64]
    grad_now[2] = late[0:128, 0:64]
    grad_past[2] = early[0:128, 0:64]
    grad_mix[0] = late[128:192, 0:64]
    grad_mix[1] = early[128:192, 0:64]
    grad_mix[2] = late[192:256, 0:64]
    grad_lift[...] = early[192:256, 0:3]


def weight_kernel(bins, psd, out):
    at = bins[...]
    high = at // LANES
    low = at % LANES
    second = lane_ids(256) >= 32
    total = jnp.zeros((256, LANES), F32)
    for h in range(8):
        rows = [
            jnp.take_along_axis(
                jnp.broadcast_to(psd[8 * j + h : 8 * j + h + 1, :], (256, LANES)), low, axis=1
            )
            for j in range(2)
        ]
        total = jnp.where(high == h, jnp.where(second, rows[1], rows[0]), total)
    out[...] = total


def call(kernel, outs, scratch=(), smem=0, n_in=0):
    vmem = pl.BlockSpec(memory_space=pltpu.VMEM)
    in_specs = [pl.BlockSpec(memory_space=pltpu.SMEM)] * smem + [vmem] * n_in
    out_shape = [jax.ShapeDtypeStruct(shape, F32) for shape in outs]
    return pl.pallas_call(
        kernel,
        out_shape=out_shape,
        in_specs=in_specs,
        out_specs=[vmem] * len(outs),
        scratch_shapes=list(scratch),
        compiler_params=pltpu.CompilerParams(vmem_limit_bytes=56 * 1024 * 1024),
    )


def two_parts(table):
    high = table.astype(jnp.bfloat16)
    low = (table - high.astype(np.float32)).astype(jnp.bfloat16)
    return np.stack([high, low])


def tables(rows_count, cols_count):
    n = rows_count * cols_count
    ids = np.arange(n)
    residue = rows_count * (ids % cols_count) + ids // cols_count

    def pair(product):
        angle = 2.0 * np.pi / n * (product % n)
        return two_parts(
            np.concatenate([np.cos(angle), np.sin(angle)], axis=1).astype(np.float32)
        )

    outward = pair(residue[:, None] * ids[None, :])
    plain = pair(ids[:, None] * ids[None, :])
    inward = pair(ids[:, None] * residue[None, :])
    return residue, outward, plain, inward


def exchange(x):
    return lax.all_to_all(x, BOTH, split_axis=0, concat_axis=0, tiled=True)


def local(
    rows_count, cols_count,
    whitened, cotangent, lift_weight, conv_now, conv_past, mix_weight, dilations, psd_bin, psd_weight,
):
    n = rows_count * cols_count
    total = n * SEG
    me = lax.axis_index("rows") * cols_count + lax.axis_index("cols")
    up = [(i, i + 1) for i in range(n - 1)]
    down = [(i + 1, i) for i in range(n - 1)]
    wh = jnp.pad(whitened, ((0, 5), (0, 0)))
    wh_left = lax.ppermute(wh[:, SEG - RIM :], BOTH, up)
    cot_right = lax.ppermute(cotangent[:, :RIM], BOTH, down)
    wh_right = lax.ppermute(wh[:, :RIM], BOTH, down)

    residue, outward, plain, inward = tables(rows_count, cols_count)
    m_ids = np.tile(np.arange(16), 4)
    r_ids = jnp.asarray(residue, jnp.int32)
    angle = (2.0 * math.pi / total) * (
        r_ids[:, None] * (256 * jnp.asarray(m_ids, jnp.int32)[None, :] + me)
    ).astype(F32)
    twist_cos = jnp.pad(jnp.cos(angle), ((0, 0), (0, 64)))
    twist_sin = jnp.pad(jnp.sin(angle), ((0, 0), (0, 64)))
    row = np.arange(LANES)
    same = (row[:, None] // 32 == row[None, :] // 32) & (row[:, None] < 64) & (row[None, :] < 64)
    part_in, part_out = (row // 16) % 2, (row // 16) % 2
    alike = same & (part_in[:, None] == part_out[None, :])
    sign = np.where(part_in[:, None] > part_out[None, :], 1.0, -1.0) * (same & ~alike)
    phase = (2.0 * math.pi / SEG) * (
        (jnp.asarray(row % 16, jnp.int32)[None, :]
         * (256 * jnp.asarray(row % 16, jnp.int32)[:, None] + me)) % SEG
    ).astype(F32)
    inner = jnp.cos(phase) * alike.astype(np.float32) + jnp.sin(phase) * sign.astype(np.float32)

    bins = psd_bin.reshape(256, 16)
    bins = jnp.concatenate([bins, bins, bins, bins, jnp.zeros((256, 64), jnp.int32)], axis=1)
    weights = call(weight_kernel, [(256, LANES)], n_in=2)(
        bins, (psd_weight * (1.0 / total)).reshape(16, LANES)
    )[0]

    w_cat = jnp.concatenate([conv_now, conv_past], axis=2)
    w_cat_t = jnp.swapaxes(w_cat, 1, 2)
    mix_t = jnp.swapaxes(mix_weight, 1, 2)
    lift_rows = jnp.pad(jnp.repeat(lift_weight.T, 16, axis=0), ((0, 16), (0, 0)))
    big = lambda rows, dtype: pltpu.VMEM((rows, WIDE), dtype)
    scratch = (
        [big(64, F32)] * 3 + [big(128, BF16)] * 2 + [big(64, F32)] * 4 + [big(64, BF16)] * 2
        + [big(64, F32)] * 4
        + [
            pltpu.VMEM((3, 128, 128), F32), pltpu.VMEM((3, 64, 128), F32),
            pltpu.VMEM((64, 128), F32), pltpu.VMEM((128, 256), F32),
        ]
    )
    sent, late = call(conv_kernel, [(n, 1, 256), (n, LANES)], scratch, smem=1, n_in=11)(
        dilations, wh, wh_left, wh_right, cotangent, cot_right, lift_weight, lift_rows,
        w_cat, w_cat_t, mix_weight, mix_t,
    )
    got = exchange(sent)
    sent, sums = call(first_kernel, [(n, 1, LANES), (8, 256)], n_in=6)(
        got, late, outward, twist_cos, twist_sin, inner
    )
    got = exchange(sent)
    sent, sums_late = call(middle_kernel, [(n, 1, 256), (8, LANES)], n_in=4)(
        got, sums, weights, plain
    )
    before = exchange(sent)
    sent, = call(third_kernel, [(n, 1, LANES)], n_in=6)(
        before, sums_late, inward, twist_cos, twist_sin, inner
    )
    got = exchange(sent)
    outs = [(3, SEG), (3, 128, 64), (3, 128, 64), (3, 64, 64), (64, 3)]
    return tuple(
        call(functools.partial(last_kernel, total ** -0.5), outs, n_in=2)(got, before)
    )


def solution(mesh):
    in_specs = (
        P(None, BOTH), P(None, BOTH), P(), P(), P(), P(), P(), P(None, "cols", "rows"), P(),
    )
    out_specs = (P(None, BOTH), P(), P(), P(), P())
    body = functools.partial(local, mesh.shape["rows"], mesh.shape["cols"])
    return jax.shard_map(body, mesh=mesh, in_specs=in_specs, out_specs=out_specs, check_vma=False)
```

time: 566 us -> 157 us (0.28); the launches traced: 556 us -> 156 us
  other arithmetic: 97.2 us -> 2.21 us
  waiting for transfers between devices: 109 us -> 18.4 us
  starting transfers between devices: 114 us -> 31.5 us
  local copies, waits for them, and re-layouts: 90 us -> 15.9 us
  Pallas kernels: 0 us -> 44.3 us
  matrix products: 40.8 us -> 0 us
  blocking collectives: 78.9 us -> 42.6 us
  between operations: 25.7 us -> 0.84 us
    psum x1 -> x0, blocking collectives: 78.9 us -> none  [local(): lax.psum((jnp.stack(grads_now), jnp.stack(grads_past), jnp.stack(grads_mi...]
    unnamed x8 -> x1, other arithmetic: 76 us -> 0.68 us
    all_to_all x14 -> x2, starting transfers between devices: 97.3 us -> 23 us  [exchange(): return lax.all_to_all(x, BOTH, split_axis=0, concat_axis=0, tiled=True)]
    psum x1 -> x0, waiting for transfers between devices: 63.5 us -> none  [local(): lax.psum((jnp.stack(grads_now), jnp.stack(grads_past), jnp.stack(grads_mi...]
    pallas_call x0 -> x6, Pallas kernels: none -> 44.3 us  [the longest x1 30.4 us: local(): call(conv_kernel, [(n, 1, 256), (n, LANES)], scratch, smem=1, n_in=11)]
    all_to_all x0 -> x2, blocking collectives: none -> 42.6 us  [exchange(): return lax.all_to_all(x, BOTH, split_axis=0, concat_axis=0, tiled=True)]
    dot_general x56 -> x0, matrix products: 40.8 us -> none  [the longest x6 4.75 us: transform(): jnp.einsum(pattern, cosine, imag_part, precision=lax.Precision.HIGHEST)]
    unnamed x117 -> x46, local copies, waits for them, and re-layouts: 39.2 us -> 6.25 us
  transfers between devices with their start and end apart: 21 -> 5, of which waited for: 15 -> 2; matrix products, arithmetic and copies ran while one was open for 23% -> 6% of each run, Pallas kernels for 0% -> 2%
where the time goes in v1:
time: 157 us; the launch traced here: 156 us
  Pallas kernels  44.3 us (28%)
  blocking collectives  42.6 us (27%)
  starting transfers between devices  31.5 us (20%)
  waiting for transfers between devices  18.4 us (12%)
  local copies, waits for them, and re-layouts  15.9 us (10%)
  other arithmetic  2.21 us (1%)
    all_to_all x2, blocking collectives, exchange(): return lax.all_to_all(x, BOTH, split_axis=0, concat_axis=0, tiled=True)  42.6 us
    pallas_call x1, Pallas kernels, local(): call(conv_kernel, [(n, 1, 256), (n, LANES)], scratch, smem=1, n_in=11)  30.4 us
    all_to_all x2, starting transfers between devices, exchange(): return lax.all_to_all(x, BOTH, split_axis=0, concat_axis=0, tiled=True)  23 us
    all_to_all x2, waiting for transfers between devices, exchange(): return lax.all_to_all(x, BOTH, split_axis=0, concat_axis=0, tiled=True)  18.3 us
    unnamed x46, local copies, waits for them, and re-layouts  6.25 us
    ppermute x1, starting transfers between devices, local(): wh_left = lax.ppermute(wh[:, SEG - RIM:], BOTH, up)  4.49 us
  transfers between devices with their start and end apart: 5, of which 2 were waited for; matrix products, arithmetic and copies ran while one was open for 6% of the time, Pallas kernels for 2%

profile of v1, /device:TPU:1, one launch (start us, length us, event | category | flops | bytes accessed | tf_op | source)
XLA Modules:
  0.0 155.6 jit_solution(5175381057494097444)
XLA Ops:
  0.6 0.7 pad_slice_fusion
  1.4 4.5 %collective-permute-start = (f32[8,640]{1,0:T(8,128)S(1)}, f32[8,640]{1,0:T(8,128)S(1)}, u32[]{:S(2)}, u32[]{:S(2)}) collective-permute-start(f32[8,640]{1,0:T(8,128)S(1)} %get-tuple-element.28), channel_id=1, source_target_pairs={{0,1},{1,2},{2,3},{3,4},{4,5},{5,6},{6,7},{7,8},{8,9},{9,10},{10,1... | collective-permute-start | bytes 61448 | tf_op jit(solution)/shard_map/ppermute | solution.py:360
  5.9 2.1 %collective-permute-start.1 = (f32[8,640]{1,0:T(8,128)S(1)}, f32[8,640]{1,0:T(8,128)S(1)}, u32[]{:S(2)}, u32[]{:S(2)}) collective-permute-start(f32[8,640]{1,0:T(8,128)S(1)} %get-tuple-element.27), channel_id=1, source_target_pairs={{1,0},{2,1},{3,2},{4,3},{5,4},{6,5},{7,6},{8,7},{9,8},{10,9},{11,1... | collective-permute-start | bytes 61448 | tf_op jit(solution)/shard_map/ppermute | solution.py:362
  7.9 0.9 slice.11
  8.8 1.9 %collective-permute-start.2 = (bf16[64,640]{1,0:T(8,128)(2,1)S(1)}, bf16[64,640]{1,0:T(8,128)(2,1)S(1)}, u32[]{:S(2)}, u32[]{:S(2)}) collective-permute-start(bf16[64,640]{1,0:T(8,128)(2,1)S(1)} %slice.11), channel_id=1, source_target_pairs={{1,0},{2,1},{3,2},{4,3},{5,4},{6,5},{7,6},{8,7},{9,8},{10,9},{11,1... | collective-permute-start | bytes 245768 | tf_op jit(solution)/shard_map/ppermute | solution.py:361
  10.8 0.6 copy-done.20
  11.4 0.1 copy-done.10
  11.6 0.8 copy.31.w_cat
  12.3 0.1 copy-done.3
  12.5 0.7 pad.15.wh
  13.1 0.0 copy-done.16
  13.1 0.7 copy.30.lift
  13.8 0.6 pad.16.lift_rows
  14.5 0.2 copy-done.4
  14.6 0.7 copy.29
  15.4 0.6 copy-done.12
  16.0 0.0 copy-done.13
  16.0 0.1 copy-done.6
  16.0 30.4 %shard_map.209 = (f32[256,1,256]{2,1,0:T(1,128)}, f32[256,128]{1,0:T(8,128)}) custom-call(s32[3]{0:T(128)} %dil.1, f32[8,4096]{1,0:T(8,128)} %pad.15.wh, f32[8,640]{1,0:T(8,128)} %copy-done.12, f32[8,640]{1,0:T(8,128)} %copy-done.13, bf16[64,4096]{1,0:T(8,128)(2,1)} %cot.1, bf16[64,640]{1,0:T(8,128)(2,1)} %copy-done.6, f32[64,3]{1,0:T(8,128)} %copy.30.lift, ...), custom_call_target="tpu_custom_call" | custom-call | tf_op jit(solution)/shard_map/pallas_call | solution.py:402
  46.5 17.1 %all-to-all-start = ((f32[256,1,256]{2,1,0:T(1,128)}), f32[256,1,256]{2,1,0:T(1,128)S(1)}, u32[]{:S(2)}, u32[]{:S(2)}) async-start(f32[256,1,256]{2,1,0:T(1,128)} %get-tuple-element.11), calls=%async_computation | async-start | bytes 524288 | tf_op jit(solution)/shard_map/all_to_all | solution.py:347
  63.6 0.5 fusion
  64.1 0.7 pad.17.twist_cos
  64.8 0.7 pad.18.twist_sin
  65.5 0.2 copy-done.7
  65.7 0.1 copy-done.8
  65.7 0.4 copy-done.18
  66.1 1.0 multiply_add_fusion.inner
  67.1 11.7 %all-to-all-done.got = f32[256,1,256]{2,1,0:T(1,128)S(1)} async-done(((f32[256,1,256]{2,1,0:T(1,128)}), f32[256,1,256]{2,1,0:T(1,128)S(1)}, u32[]{:S(2)}, u32[]{:S(2)}) %all-to-all-start) | async-done | bytes 262176 | tf_op jit(solution)/shard_map/all_to_all | solution.py:347
  78.8 0.7 copy-done
  79.5 2.9 %shard_map.210 = (f32[256,1,128]{2,1,0:T(1,128)}, f32[8,256]{1,0:T(8,128)}) custom-call(f32[256,1,256]{2,1,0:T(1,128)} %copy-done, f32[256,128]{1,0:T(8,128)} %get-tuple-element.12.late, bf16[2,256,512]{2,1,0:T(8,128)(2,1)} %constant.60.clone.table, f32[256,128]{1,0:T(8,128)} %pad.17.twist_cos, f32[256,128]{1,0:T(8,128)} %pad.18.twist_sin, ...), custom_call_target="tpu_custom_call" | custom-call | tf_op jit(solution)/shard_map/pallas_call | solution.py:407
  82.4 5.9 %all-to-all-start.1 = ((f32[256,1,128]{2,1,0:T(1,128)}), f32[256,1,128]{2,1,0:T(1,128)S(1)}, u32[]{:S(2)}, u32[]{:S(2)}) async-start(f32[256,1,128]{2,1,0:T(1,128)} %get-tuple-element.13), calls=%async_computation.1 | async-start | bytes 262144 | tf_op jit(solution)/shard_map/all_to_all | solution.py:347
  88.4 0.5 broadcast.27
  88.9 0.7 reduce.3
  89.6 0.1 reshape.28
  89.7 0.6 copy-done.15
  90.3 0.6 reshape.29.psd
  90.9 0.8 concatenate.7.bins
  91.7 3.1 %shard_map.211.weights = f32[256,128]{1,0:T(8,128)} custom-call(s32[256,128]{1,0:T(8,128)} %concatenate.7.bins, f32[16,128]{1,0:T(8,128)} %reshape.29.psd), custom_call_target="tpu_custom_call" | custom-call | tf_op jit(solution)/shard_map/pallas_call | solution.py:385
  94.8 6.7 %all-to-all-done.1.got = f32[256,1,128]{2,1,0:T(1,128)S(1)} async-done(((f32[256,1,128]{2,1,0:T(1,128)}), f32[256,1,128]{2,1,0:T(1,128)S(1)}, u32[]{:S(2)}, u32[]{:S(2)}) %all-to-all-start.1) | async-done | bytes 131104 | tf_op jit(solution)/shard_map/all_to_all | solution.py:347
  101.5 0.6 copy-done.2
  102.1 2.9 %shard_map.212 = (f32[256,1,256]{2,1,0:T(1,128)}, f32[8,128]{1,0:T(8,128)}) custom-call(f32[256,1,128]{2,1,0:T(1,128)} %copy-done.2, f32[8,256]{1,0:T(8,128)} %get-tuple-element.14.sums, f32[256,128]{1,0:T(8,128)} %shard_map.211.weights, bf16[2,256,512]{2,1,0:T(8,128)(2,1)} %constant.61.clone.table), custom_call_target="tpu_custom_call" | custom-call | tf_op jit(solution)/shard_map/pallas_call | solution.py:411
  105.0 22.5 %all_to_all.20.got.got_before = f32[256,1,256]{2,1,0:T(1,128)} all-to-all(f32[256,1,256]{2,1,0:T(1,128)} %get-tuple-element.15), channel_id=1, replica_groups=mesh['rows'=8,'cols'=32] {'rows','cols'}, dimensions={0} | all-to-all | bytes 524288 | tf_op jit(solution)/shard_map/all_to_all | solution.py:347
  127.5 2.9 %shard_map.213 = f32[256,1,128]{2,1,0:T(1,128)} custom-call(f32[256,1,256]{2,1,0:T(1,128)} %all_to_all.20.got.got_before, f32[8,128]{1,0:T(8,128)} %get-tuple-element.16.sums_late, bf16[2,256,512]{2,1,0:T(8,128)(2,1)} %constant.62.clone.table, f32[256,128]{1,0:T(8,128)} %pad.17.twist_cos, f32[256,128]{1,0:T(8,128)} %pad.18.twist_sin, ...), custom_call_target="tpu_custom_call" | custom-call | tf_op jit(solution)/shard_map/pallas_call | solution.py:415
  130.4 20.1 %all_to_all.21.got = f32[256,1,128]{2,1,0:T(1,128)} all-to-all(f32[256,1,128]{2,1,0:T(1,128)} %shard_map.213), channel_id=1, replica_groups=mesh['rows'=8,'cols'=32] {'rows','cols'}, dimensions={0} | all-to-all | bytes 262144 | tf_op jit(solution)/shard_map/all_to_all | solution.py:347
  150.5 2.0 %shard_map.214 = (f32[3,4096]{1,0:T(4,128)}, f32[3,128,64]{2,1,0:T(8,128)}, f32[3,128,64]{2,1,0:T(8,128)}, f32[3,64,64]{2,1,0:T(8,128)}, f32[64,3]{1,0:T(8,128)}) custom-call(f32[256,1,128]{2,1,0:T(1,128)} %all_to_all.21.got, f32[256,1,256]{2,1,0:T(1,128)} %all_to_all.20.got.got_before), custom_call_target="tpu_custom_call" | custom-call | tf_op jit(solution)/shard_map/pallas_call | solution.py:421
  152.5 1.7 %copy.32 = f32[3,128,64]{1,2,0:T(8,128)} copy(f32[3,128,64]{2,1,0:T(8,128)} %get-tuple-element.23) | data formatting | bytes 196608 | tf_op jit(solution)/shard_map/pallas_call | solution.py:421
  154.2 0.8 copy.33
  155.0 0.7 copy.34
  (38 shorter events, 0.1 us)
Async XLA Ops:
  1.4 14.0 %collective-permute-start = (f32[8,640]{1,0:T(8,128)S(1)}, f32[8,640]{1,0:T(8,128)S(1)}, u32[]{:S(2)}, u32[]{:S(2)}) collective-permute-start(f32[8,640]{1,0:T(8,128)S(1)} %get-tuple-element.28), channel_id=1, source_target_pairs={{0,1},{1,2},{2,3},{3,4},{4,5},{5,6},{6,7},{7,8},{8,9},{9,10},{10,1... | collective-permute-start | bytes 61448 | tf_op jit(solution)/shard_map/ppermute | solution.py:360
  5.9 4.9 %copy-start.9 = (bf16[3,128,64]{1,2,0:T(8,128)(2,1)S(1)}, bf16[3,128,64]{1,2,0:T(8,128)(2,1)}, u32[]{:S(2)}) copy-start(bf16[3,128,64]{1,2,0:T(8,128)(2,1)} %param.21) | copy-start | bytes 147460
  5.9 9.5 %collective-permute-start.1 = (f32[8,640]{1,0:T(8,128)S(1)}, f32[8,640]{1,0:T(8,128)S(1)}, u32[]{:S(2)}, u32[]{:S(2)}) collective-permute-start(f32[8,640]{1,0:T(8,128)S(1)} %get-tuple-element.27), channel_id=1, source_target_pairs={{1,0},{2,1},{3,2},{4,3},{5,4},{6,5},{7,6},{8,7},{9,8},{10,9},{11,1... | collective-permute-start | bytes 61448 | tf_op jit(solution)/shard_map/ppermute | solution.py:362
  8.8 6.5 %collective-permute-start.2 = (bf16[64,640]{1,0:T(8,128)(2,1)S(1)}, bf16[64,640]{1,0:T(8,128)(2,1)S(1)}, u32[]{:S(2)}, u32[]{:S(2)}) collective-permute-start(bf16[64,640]{1,0:T(8,128)(2,1)S(1)} %slice.11), channel_id=1, source_target_pairs={{1,0},{2,1},{3,2},{4,3},{5,4},{6,5},{7,6},{8,7},{9,8},{10,9},{11,1... | collective-permute-start | bytes 245768 | tf_op jit(solution)/shard_map/ppermute | solution.py:361
  10.8 0.8 copy-start.10
  10.8 0.7 copy-start.20
  11.6 0.8 copy-start.1
  11.6 0.9 copy-start.3
  12.5 0.7 copy-start.16
  13.8 0.8 copy-start.4
  15.3 0.6 copy-start.12
  15.4 0.6 copy-start.13
  15.4 0.6 copy-start.6
  46.5 17.1 %copy-start.17 = (s32[256]{0:T(256)S(1)}, s32[256]{0:T(256)}, u32[]{:S(2)}) copy-start(s32[256]{0:T(256)} %constant.55.clone) | copy-start | bytes 3076
  46.5 32.3 %all-to-all-start = ((f32[256,1,256]{2,1,0:T(1,128)}), f32[256,1,256]{2,1,0:T(1,128)S(1)}, u32[]{:S(2)}, u32[]{:S(2)}) async-start(f32[256,1,256]{2,1,0:T(1,128)} %get-tuple-element.11), calls=%async_computation | async-start | bytes 524288 | tf_op jit(solution)/shard_map/all_to_all | solution.py:347
  64.8 0.7 copy-start.19
  64.8 0.9 copy-start.7
  64.8 0.9 copy-start.8
  65.4 0.7 copy-start.18
  78.8 0.7 copy-start
  82.4 6.5 %copy-start.14 = (s32[4096,1,1]{0,2,1:T(1,128)S(1)}, s32[4096,1,1]{0,2,1:T(1,128)}, u32[]{:S(2)}) copy-start(s32[4096,1,1]{0,2,1:T(1,128)} %param.25) | copy-start | bytes 49156
  82.4 19.1 %all-to-all-start.1 = ((f32[256,1,128]{2,1,0:T(1,128)}), f32[256,1,128]{2,1,0:T(1,128)S(1)}, u32[]{:S(2)}, u32[]{:S(2)}) async-start(f32[256,1,128]{2,1,0:T(1,128)} %get-tuple-element.13), calls=%async_computation.1 | async-start | bytes 262144 | tf_op jit(solution)/shard_map/all_to_all | solution.py:347
  89.6 0.7 copy-start.15
  101.5 0.6 copy-start.2
  152.5 1.7 %copy-start.5 = (f32[3,128,64]{2,1,0:T(8,128)S(1)}, f32[3,128,64]{2,1,0:T(8,128)}, u32[]{:S(2)}) copy-start(f32[3,128,64]{2,1,0:T(8,128)} %get-tuple-element.24) | copy-start | bytes 294916
  154.2 0.8 copy-start.11

commit v2 on v1

v2 whole, which is shorter than its diff:
```python
import functools
import math

import jax
import jax.numpy as jnp
import numpy as np
from jax import lax
from jax.experimental import pallas as pl
from jax.experimental.pallas import tpu as pltpu
from jax.sharding import PartitionSpec as P

F32 = jnp.float32
BF16 = jnp.bfloat16
BOTH = ("rows", "cols")
SEG = 4096
SHIFT = 768
LEFT = 640
SPAN = SEG + 640
BASE = 1024
WIDE = BASE + SEG + 1024
STEP = 1024
LANES = 128


def lane_ids(rows):
    return lax.broadcasted_iota(jnp.int32, (rows, LANES), 1)


def dot32(a, b):
    return jnp.dot(a, b, preferred_element_type=F32)


def dot_nt(a, b, precision=None):
    return lax.dot_general(
        a, b, (((1,), (1,)), ((), ())), preferred_element_type=F32, precision=precision
    )


def columns(start, width):
    if isinstance(start, int):
        return pl.ds(start, width)
    return pl.ds(pl.multiple_of(start, LANES), width)


def pack_kernel(cot, wh, out, parts):
    out[0:64] = cot[:, 256:1024]
    parts[...] = jnp.zeros_like(parts)
    for half in range(2):
        left = wh[:, 512 + half * 768 : 512 + (half + 1) * 768]
        for part in range(3):
            piece = left.astype(BF16).astype(F32)
            parts[half * 16 + part * 3 : half * 16 + part * 3 + 3] = piece
            left = left - piece
    out[64:96] = parts[...].astype(BF16)


def conv_kernel(
    dil, got, wh, cot, lift_t, now_t, past_t, mix,
    sent, late, parts, w_cat, w_cat_t, mix_t, square, whu, cotu,
    f0, f1, f2, x1, x2, fl1, fl2, sg1, sg2, gt1, gt2, ah, ah2, dp, dp2, g_conv, g_mix, x_t,
):
    lane = lane_ids(64)
    one_lane = lane_ids(1)
    at_start = (lax.axis_index("rows") == 0) & (lax.axis_index("cols") == 0)
    edge = jnp.where(at_start, SHIFT, 1 << 20)

    def shifted(ref, first, turn, keep_below, width):
        turned = [
            pltpu.roll(ref[:, columns(first + LANES * k, LANES)], turn, 1)
            for k in range(width // LANES + 1)
        ]
        keep = lane < keep_below
        return [jnp.where(keep, turned[k], turned[k + 1]) for k in range(width // LANES)]

    def cut(tiles, start, low, high):
        done = []
        for k, tile in enumerate(tiles):
            at = one_lane + (start - BASE + LANES * k)
            done.append(tile * jnp.where((at >= low) & (at < high), 0.0, 1.0))
        return jnp.concatenate(done, axis=1)

    def behind(ref, start, width, layer):
        d = dil[layer]
        whole = pl.multiple_of((d // LANES) * LANES, LANES)
        rest = d % LANES
        tiles = shifted(ref, start - whole - LANES, rest, rest, width)
        return cut(tiles, start, edge, edge + d)

    def beyond(ref, start, width, layer):
        d = dil[layer]
        whole = pl.multiple_of((d // LANES) * LANES, LANES)
        rest = d % LANES
        tiles = shifted(ref, start + whole, (LANES - rest) % LANES, LANES - rest, width)
        return cut(tiles, start, edge - d, edge)

    parts[...] = got[64:96].astype(F32)
    whu[...] = jnp.zeros_like(whu)
    for half in range(2):
        whole = (
            parts[half * 16 : half * 16 + 3] + parts[half * 16 + 3 : half * 16 + 6]
            + parts[half * 16 + 6 : half * 16 + 9]
        )
        if half == 0:
            whu[0:3, 0:640] = whole[:, 128:768]
        else:
            whu[0:3, 640:1408] = whole
    own = SPAN - SHIFT
    whu[0:3, 1408 : 1408 + own] = wh[:, 0:own]
    cotu[:, 0:SHIFT] = got[0:64]
    cotu[:, SHIFT:SPAN] = cot[:, 0:own]

    for layer in range(3):
        stacked = jnp.concatenate([now_t[layer], past_t[layer]], axis=0)
        w_cat_t[layer] = stacked
        w_cat[layer] = stacked.astype(F32).T.astype(BF16)
        square[...] = jnp.zeros_like(square)
        square[0:64, 0:64] = mix[layer].astype(F32)
        mix_t[layer] = square[...].T[0:64, 0:64].astype(BF16)
    square[...] = jnp.zeros_like(square)
    square[0:3, 0:64] = lift_t[...]
    lift_cols = square[...].T[0:64]
    lift_cols = [jnp.broadcast_to(lift_cols[:, i : i + 1], (64, LANES)) for i in range(3)]
    lift_8 = square[0:8, 0:64]
    lift_high = lift_8.astype(BF16)
    lift_16 = jnp.concatenate([lift_high.astype(F32), lift_8 - lift_high.astype(F32)], axis=0)
    lift_16 = lift_16.astype(BF16)

    zero_tile = jnp.zeros((64, LANES), F32)
    for k in range(3):
        f0[:, k * LANES : (k + 1) * LANES] = zero_tile
        f1[:, (k + 1) * LANES : (k + 2) * LANES] = zero_tile
        at = BASE + SPAN + k * LANES
        ah[:, at : at + LANES] = zero_tile
        ah2[:, at : at + LANES] = zero_tile
        ah2[:, at - LANES : at] = zero_tile
    f2[:, 384:512] = zero_tile
    f2[:, 512:640] = zero_tile

    def lift_step(i, carry):
        for k in range(6):
            at = (i * 6 + k) * LANES
            tile = whu[:, columns(at, LANES)]
            f0[:, columns(BASE - LEFT + at, LANES)] = (
                lift_cols[0] * tile[0:1] + lift_cols[1] * tile[1:2] + lift_cols[2] * tile[2:3]
            )
        return carry

    lax.fori_loop(0, 7, lift_step, 0)

    def gates(layer, field, start, width):
        now = field[:, columns(start, width)]
        both = jnp.concatenate(
            [now.astype(BF16), behind(field, start, width, layer).astype(BF16)], axis=0
        )
        pre = dot32(w_cat[layer], both)
        filt = jnp.tanh(pre[:64])
        sig = 0.5 * jnp.tanh(0.5 * pre[64:]) + 0.5
        gate = (filt * sig).astype(BF16)
        return now, both, filt, sig, gate

    def forward(layer, field, field_next, x, fl, sg, gt, start, width):
        now, both, filt, sig, gate = gates(layer, field, start, width)
        at = columns(start, width)
        x[:, at] = both
        fl[:, at] = filt
        sg[:, at] = sig
        gt[:, at] = gate
        field_next[:, at] = now + dot32(mix[layer], gate)

    def run_forward(layer, field, field_next, x, fl, sg, gt, start, rest):
        def step(i, carry):
            forward(layer, field, field_next, x, fl, sg, gt, start + i * STEP, STEP)
            return carry

        lax.fori_loop(0, 5, step, 0)
        if rest:
            forward(layer, field, field_next, x, fl, sg, gt, start + 5 * STEP, rest)

    run_forward(0, f0, f1, x1, fl1, sg1, gt1, BASE - 512, 128)
    run_forward(1, f1, f2, x2, fl2, sg2, gt2, BASE - 384, 0)

    g_conv[...] = jnp.zeros_like(g_conv)
    g_mix[...] = jnp.zeros_like(g_mix)

    def backward(layer, dfield, dfield_b, both, filt, sig, gate, ah_out, dp_out, start, width, own):
        d_gate = dot32(mix_t[layer], dfield_b)
        d_pre = jnp.concatenate(
            [d_gate * sig * (1.0 - filt * filt), d_gate * filt * sig * (1.0 - sig)], axis=0
        ).astype(BF16)
        back = dot32(w_cat_t[layer], d_pre)
        at = columns(start, width)
        dp_out[:, at] = dfield + back[:64]
        ah_out[:, at] = back[64:]
        if own:
            g_conv[layer] += dot_nt(both, d_pre)
            g_mix[layer] += dot_nt(
                dfield_b, jnp.concatenate([jnp.zeros((64, width), BF16), gate], axis=0)
            )

    def last_layer(start, width, own):
        now, both, filt, sig, gate = gates(2, f2, start, width)
        dfield_b = cotu[:, columns(start - BASE, width)]
        backward(2, dfield_b.astype(F32), dfield_b, both, filt, sig, gate, ah, dp, start, width, own)

    def step3(i, carry):
        last_layer(BASE + i * STEP, STEP, True)
        return carry

    lax.fori_loop(0, SEG // STEP, step3, 0)
    last_layer(BASE + SEG, 640, False)

    def saved_layer(layer, x, fl, sg, gt, ah_in, dp_in, ah_out, dp_out, start, width, own):
        at = columns(start, width)
        dfield = dp_in[:, at] + beyond(ah_in, start, width, layer + 1)
        backward(
            layer, dfield, dfield.astype(BF16), x[:, at], fl[:, at], sg[:, at], gt[:, at],
            ah_out, dp_out, start, width, own,
        )

    def step2(i, carry):
        saved_layer(1, x2, fl2, sg2, gt2, ah, dp, ah2, dp2, BASE + i * STEP, STEP, True)
        return carry

    lax.fori_loop(0, SEG // STEP, step2, 0)
    saved_layer(1, x2, fl2, sg2, gt2, ah, dp, ah2, dp2, BASE + SEG, 512, False)

    def step1(i, carry):
        saved_layer(0, x1, fl1, sg1, gt1, ah2, dp2, ah, dp, BASE + i * STEP, STEP, True)
        return carry

    lax.fori_loop(0, SEG // STEP, step1, 0)
    saved_layer(0, x1, fl1, sg1, gt1, ah2, dp2, ah, dp, BASE + SEG, 256, False)

    x_t[...] = jnp.zeros_like(x_t)
    g_lift = jnp.zeros((8, LANES), F32)
    blank = jnp.zeros((64, 256), BF16)
    for m in range(16):
        start = BASE + m * 256
        dfield = dp[:, start : start + 256] + beyond(ah, start, 256, 0)
        high = dfield.astype(BF16)
        low = (dfield - high.astype(F32)).astype(BF16)
        on_high = dot32(lift_16, high)
        x8 = on_high[0:8] + on_high[8:16] + dot32(lift_16, low)[0:8]
        for channel in range(3):
            x_t[channel * 16 + m : channel * 16 + m + 1] = x8[channel : channel + 1]
        seen = whu[:, LEFT + m * 256 : LEFT + (m + 1) * 256]
        seen_high = seen.astype(BF16).astype(F32)
        seen_16 = jnp.concatenate([seen_high, seen - seen_high], axis=0).astype(BF16)
        on_high = dot_nt(seen_16, jnp.concatenate([blank, high], axis=0))
        g_lift += (
            on_high[0:8] + on_high[8:16]
            + dot_nt(seen_16, jnp.concatenate([blank, low], axis=0))[0:8]
        )

    low = lane_ids(256) < 64
    early = jnp.concatenate([g_conv[2], g_mix[1], g_lift, jnp.zeros((56, LANES), F32)], axis=0)
    sent[:, 0, 0:128] = jnp.where(low, x_t[...].T, early)
    sent[:, 0, 128:256] = jnp.concatenate([g_conv[0], g_conv[1]], axis=0)
    late[...] = jnp.concatenate([pltpu.roll(g_conv[2], 64, 1), g_mix[0], g_mix[2]], axis=0)


def swap(x):
    first = (lane_ids(x.shape[0]) // 16) % 2 == 0
    return jnp.where(first, pltpu.roll(x, LANES - 16, 1), -pltpu.roll(x, 16, 1))


def wide_dot(table, x, sign):
    low = lane_ids(256) < 64
    parts = []
    for value in (x, sign * swap(x)):
        high = value.astype(BF16)
        rest = value - high.astype(F32)
        parts.append((high, jnp.where(low, high.astype(F32), pltpu.roll(rest, 64, 1)).astype(BF16)))
    mixed = dot32(table[0], jnp.concatenate([parts[0][1], parts[1][1]], axis=0))
    small = dot32(table[1], jnp.concatenate([parts[0][0], parts[1][0]], axis=0))
    return mixed + pltpu.roll(mixed, 64, 1) + small


def first_kernel(got, late, table, twist_cos, twist_sin, inner, sent, sums):
    data = got[:, 0, 0:128]
    rest = got[:, 0, 128:256]
    low = lane_ids(256) < 64
    x = jnp.where(low, data, 0.0)
    sums[:, 0:128] = jnp.broadcast_to(jnp.sum(data, axis=0, keepdims=True), (8, 128))
    sums[:, 128:256] = jnp.broadcast_to(jnp.sum(rest, axis=0, keepdims=True), (8, 128))
    y = wide_dot(table, x, 1.0)
    y = y * twist_cos[...] + swap(y) * twist_sin[...]
    y = lax.dot(y, inner[...], precision=lax.Precision.HIGHEST, preferred_element_type=F32)
    sent[:, 0, :] = jnp.where(low, y, late[...])


def middle_kernel(got, sums, weights, table, sent, sums_late):
    data = got[:, 0, :]
    low = lane_ids(256) < 64
    x = jnp.where(low, data, 0.0)
    sums_late[...] = jnp.broadcast_to(jnp.sum(data, axis=0, keepdims=True), (8, 128))
    y = wide_dot(table, x, 1.0)
    y = jnp.where(low, y * weights[...], 0.0)
    y = wide_dot(table, y, -1.0)
    sent[:, 0, 0:128] = jnp.where(low, y, jnp.broadcast_to(sums[0:1, 0:128], (256, 128)))
    sent[:, 0, 128:256] = jnp.broadcast_to(sums[0:1, 128:256], (256, 128))


def third_kernel(got, sums_late, table, twist_cos, twist_sin, inner, sent):
    low = lane_ids(256) < 64
    x = jnp.where(low, got[:, 0, 0:128], 0.0)
    y = dot_nt(x, inner[...], lax.Precision.HIGHEST)
    y = y * twist_cos[...] - swap(y) * twist_sin[...]
    y = wide_dot(table, y, -1.0)
    sent[:, 0, :] = jnp.where(low, y, jnp.broadcast_to(sums_late[0:1], (256, 128)))


def last_kernel(scaling, got, got_before, data_grad, now_t, past_t, grad_mix, lift_t):
    last = got[:, 0, :]
    turned = last.T
    for channel in range(3):
        for slot in range(16):
            row = channel * 16 + slot
            m = (slot - SHIFT // 256) % 16
            data_grad[channel : channel + 1, m * 256 : (m + 1) * 256] = turned[row : row + 1]
    late = pltpu.roll(last, 64, 1) * scaling
    early = got_before[:, 0, 0:128] * scaling
    main = got_before[:, 0, 128:256] * scaling
    third = jnp.where(lane_ids(128) < 64, late[0:128], early[0:128])
    for layer, value in enumerate((main[0:128], main[128:256], third)):
        now_t[layer] = value[0:64]
        past_t[layer] = value[64:128]
    early = pltpu.roll(early[128:256], 64, 1)
    grad_mix[0] = late[128:192, 0:64]
    grad_mix[1] = early[0:64, 0:64]
    grad_mix[2] = late[192:256, 0:64]
    lift_t[...] = early[64:67, 0:64]


def weight_kernel(bins, psd, out):
    at = bins[...]
    high = at // LANES
    low = at % LANES
    second = lane_ids(256) >= 32
    total = jnp.zeros((256, LANES), F32)
    for h in range(8):
        rows = [
            jnp.take_along_axis(
                jnp.broadcast_to(psd[8 * j + h : 8 * j + h + 1, :], (256, LANES)), low, axis=1
            )
            for j in range(2)
        ]
        total = jnp.where(high == h, jnp.where(second, rows[1], rows[0]), total)
    out[...] = total


def call(kernel, outs, scratch=(), smem=0, n_in=0, in_specs=None, grid=()):
    vmem = pl.BlockSpec(memory_space=pltpu.VMEM)
    if in_specs is None:
        in_specs = [pl.BlockSpec(memory_space=pltpu.SMEM)] * smem + [vmem] * n_in
    out_shape = [
        out if isinstance(out, jax.ShapeDtypeStruct) else jax.ShapeDtypeStruct(out, F32)
        for out in outs
    ]
    return pl.pallas_call(
        kernel,
        grid=grid,
        out_shape=out_shape,
        in_specs=in_specs,
        out_specs=[vmem] * len(outs),
        scratch_shapes=list(scratch),
        compiler_params=pltpu.CompilerParams(vmem_limit_bytes=56 * 1024 * 1024),
    )


def two_parts(table):
    high = table.astype(jnp.bfloat16)
    low = (table - high.astype(np.float32)).astype(jnp.bfloat16)
    return np.stack([high, low])


def tables(rows_count, cols_count):
    n = rows_count * cols_count
    ids = np.arange(n)
    residue = rows_count * (ids % cols_count) + ids // cols_count

    def pair(product):
        angle = 2.0 * np.pi / n * (product % n)
        return two_parts(
            np.concatenate([np.cos(angle), np.sin(angle)], axis=1).astype(np.float32)
        )

    outward = pair(residue[:, None] * ids[None, :])
    plain = pair(ids[:, None] * ids[None, :])
    inward = pair(ids[:, None] * residue[None, :])
    return residue, outward, plain, inward


def exchange(x):
    return lax.all_to_all(x, BOTH, split_axis=0, concat_axis=0, tiled=True)


def local(
    rows_count, cols_count,
    whitened, cotangent, lift_weight, conv_now, conv_past, mix_weight, dilations, psd_bin, psd_weight,
):
    n = rows_count * cols_count
    total = n * SEG
    me = lax.axis_index("rows") * cols_count + lax.axis_index("cols")
    message, = call(
        pack_kernel, [jax.ShapeDtypeStruct((96, SHIFT), BF16)], [pltpu.VMEM((32, SHIFT), F32)],
        in_specs=[
            pl.BlockSpec((64, 1024), lambda i: (0, 3)), pl.BlockSpec((3, 2048), lambda i: (0, 1)),
        ],
        grid=(1,),
    )(cotangent, whitened)
    received = lax.ppermute(message, BOTH, [(i, (i + 1) % n) for i in range(n)])

    residue, outward, plain, inward = tables(rows_count, cols_count)
    row = np.arange(LANES)
    slot = row % 16
    later = np.where(slot < SHIFT // 256, slot + 16, slot)
    inside = (row < 64).astype(np.float32)

    def twist(steps):
        fixed = jnp.asarray(residue[:, None] * (256 * steps)[None, :], jnp.int32)
        product = (fixed + jnp.asarray(residue, jnp.int32)[:, None] * me) % total
        angle = (2.0 * math.pi / total) * product.astype(F32)
        return jnp.cos(angle) * inside, jnp.sin(angle) * inside

    twist_cos, twist_sin = twist(slot)
    back_cos, back_sin = twist(later)
    same = (row[:, None] // 32 == row[None, :] // 32) & (row[:, None] < 64) & (row[None, :] < 64)
    part = (row // 16) % 2
    alike = same & (part[:, None] == part[None, :])
    sign = np.where(part[:, None] > part[None, :], 1.0, -1.0) * (same & ~alike)
    fixed = jnp.asarray(256 * slot[:, None] * slot[None, :], jnp.int32)
    product = (fixed + jnp.asarray(slot, jnp.int32)[None, :] * me) % SEG
    phase = (2.0 * math.pi / SEG) * product.astype(F32)
    inner = jnp.cos(phase) * alike.astype(np.float32) + jnp.sin(phase) * sign.astype(np.float32)

    bins = psd_bin.reshape(256, 16)
    bins = jnp.concatenate([bins, bins, bins, bins, jnp.zeros((256, 64), jnp.int32)], axis=1)
    weights = call(weight_kernel, [(256, LANES)], n_in=2)(
        bins, (psd_weight * (1.0 / total)).reshape(16, LANES)
    )[0]

    big = lambda rows, dtype: pltpu.VMEM((rows, WIDE), dtype)
    square = pltpu.VMEM((LANES, LANES), F32)
    scratch = (
        [
            pltpu.VMEM((32, SHIFT), F32), pltpu.VMEM((3, 128, 128), BF16),
            pltpu.VMEM((3, 128, 128), BF16), pltpu.VMEM((3, 64, 64), BF16), square,
            pltpu.VMEM((8, LEFT + SPAN), F32), pltpu.VMEM((64, SPAN), BF16),
        ]
        + [big(64, F32)] * 3 + [big(128, BF16)] * 2 + [big(64, F32)] * 4 + [big(64, BF16)] * 2
        + [big(64, F32)] * 4
        + [pltpu.VMEM((3, 128, 128), F32), pltpu.VMEM((3, 64, 128), F32), pltpu.VMEM((128, 256), F32)]
    )
    sent, late = call(conv_kernel, [(n, 1, 256), (n, LANES)], scratch, smem=1, n_in=7)(
        dilations, received, whitened, cotangent, lift_weight.T, jnp.swapaxes(conv_now, 1, 2),
        jnp.swapaxes(conv_past, 1, 2), mix_weight,
    )
    got = exchange(sent)
    sent, sums = call(first_kernel, [(n, 1, LANES), (8, 256)], n_in=6)(
        got, late, outward, twist_cos, twist_sin, inner
    )
    got = exchange(sent)
    sent, sums_late = call(middle_kernel, [(n, 1, 256), (8, LANES)], n_in=4)(
        got, sums, weights, plain
    )
    before = exchange(sent)
    sent, = call(third_kernel, [(n, 1, LANES)], n_in=6)(
        before, sums_late, inward, back_cos, back_sin, inner
    )
    got = exchange(sent)
    outs = [(3, SEG), (3, 64, 128), (3, 64, 128), (3, 64, 64), (3, 64)]
    data_grad, now_t, past_t, grad_mix, lift_t = call(
        functools.partial(last_kernel, total ** -0.5), outs, n_in=2
    )(got, before)
    return (
        data_grad, jnp.swapaxes(now_t, 1, 2), jnp.swapaxes(past_t, 1, 2), grad_mix, lift_t.T
    )


def solution(mesh):
    in_specs = (
        P(None, BOTH), P(None, BOTH), P(), P(), P(), P(), P(), P(None, "cols", "rows"), P(),
    )
    out_specs = (P(None, BOTH), P(), P(), P(), P())
    body = functools.partial(local, mesh.shape["rows"], mesh.shape["cols"])
    return jax.shard_map(body, mesh=mesh, in_specs=in_specs, out_specs=out_specs, check_vma=False)
```

time: 157 us -> 131 us (0.83)
  Pallas kernels: 44.3 us -> 33.3 us
  local copies, waits for them, and re-layouts: 15.9 us -> 5.41 us
  starting transfers between devices: 31.5 us -> 24.3 us
  waiting for transfers between devices: 18.4 us -> 20.7 us
    pallas_call x1 -> x2, Pallas kernels: 30.4 us -> 19.6 us  [the longest x1 18 us: local(): call(conv_kernel, [(n, 1, 256), (n, LANES)], scratch, smem=1, n_in=7)]
    ppermute x3 -> x1, starting transfers between devices: 8.45 us -> 2.59 us  [local(): received = lax.ppermute(message, BOTH, [(i, (i + 1) % n) for i in range(n)])]
    pallas_call x3 -> x0, local copies, waits for them, and re-layouts: 3.13 us -> none  [local(): call(functools.partial(last_kernel, total ** (-0.5)), outs, n_in=2)]
    pad x4 -> x0, local copies, waits for them, and re-layouts: 2.61 us -> none  [the longest x1 0.67 us: local(): wh = jnp.pad(whitened, ((0, 5), (0, 0)))]
    unnamed x46 -> x27, local copies, waits for them, and re-layouts: 6.25 us -> 3.85 us
    mul x0 -> x3, other arithmetic: none -> 1.93 us  [the longest x1 1.92 us: twist(): return (jnp.cos(angle) * inside, jnp.sin(angle) * inside)]
    ppermute x3 -> x1, waiting for transfers between devices: 0.01 us -> 1.74 us  [local(): received = lax.ppermute(message, BOTH, [(i, (i + 1) % n) for i in range(n)])]
    slice x2 -> x0, local copies, waits for them, and re-layouts: 1.62 us -> none  [the longest x1 0.9 us: local(): cot_right = lax.ppermute(cotangent[:, :RIM], BOTH, down)]
  transfers between devices with their start and end apart: 5 -> 3, of which waited for: 2 -> 3; matrix products, arithmetic and copies ran while one was open for 6% -> 4% of each run, Pallas kernels for 2% -> 2%
where the time goes in v2:
time: 131 us
  blocking collectives  42.5 us (32%)
  Pallas kernels  33.3 us (25%)
  starting transfers between devices  24.3 us (19%)
  waiting for transfers between devices  20.7 us (16%)
  local copies, waits for them, and re-layouts  5.41 us (4%)
  other arithmetic  3.53 us (3%)
    all_to_all x2, blocking collectives, exchange(): return lax.all_to_all(x, BOTH, split_axis=0, concat_axis=0, tiled=True)  42.5 us
    all_to_all x2, starting transfers between devices, exchange(): return lax.all_to_all(x, BOTH, split_axis=0, concat_axis=0, tiled=True)  21.7 us
    all_to_all x2, waiting for transfers between devices, exchange(): return lax.all_to_all(x, BOTH, split_axis=0, concat_axis=0, tiled=True)  19 us
    pallas_call x1, Pallas kernels, local(): call(conv_kernel, [(n, 1, 256), (n, LANES)], scratch, smem=1, n_in=7)  18 us
    unnamed x27, local copies, waits for them, and re-layouts  3.85 us
    pallas_call x1, Pallas kernels, local(): call(weight_kernel, [(256, LANES)], n_in=2)  3.06 us
    pallas_call x1, Pallas kernels, local(): call(first_kernel, [(n, 1, LANES), (8, 256)], n_in=6)  2.92 us
    pallas_call x1, Pallas kernels, local(): call(third_kernel, [(n, 1, LANES)], n_in=6)  2.88 us
  transfers between devices with their start and end apart: 3, of which 3 were waited for; matrix products, arithmetic and copies ran while one was open for 4% of the time, Pallas kernels for 2%

profile of v2, /device:TPU:1, one launch (start us, length us, event | category | flops | bytes accessed | tf_op | source)
XLA Modules:
  0.0 130.5 jit_solution(955312829212967266)
XLA Ops:
  0.6 1.6 %shard_map.236 = bf16[96,768]{1,0:T(8,128)(2,1)} custom-call(bf16[64,4096]{1,0:T(8,128)(2,1)} %cot.3, f32[3,4096]{1,0:T(4,128)} %wh.3), custom_call_target="tpu_custom_call" | custom-call | tf_op jit(solution)/shard_map/pallas_call | solution.py:405
  2.2 2.6 %collective-permute-start = (bf16[96,768]{1,0:T(8,128)(2,1)}, bf16[96,768]{1,0:T(8,128)(2,1)S(1)}, u32[]{:S(2)}, u32[]{:S(2)}) collective-permute-start(bf16[96,768]{1,0:T(8,128)(2,1)} %shard_map.236), channel_id=1, source_target_pairs={{0,1},{1,2},{2,3},{3,4},{4,5},{5,6},{6,7},{7,8},{8,9},{9,10},{10,1... | collective-permute-start | bytes 442376 | tf_op jit(solution)/shard_map/ppermute | solution.py:412
  4.8 0.0 copy-start.10
  4.8 0.7 copy-done.10
  5.5 1.7 %collective-permute-done.got = bf16[96,768]{1,0:T(8,128)(2,1)S(1)} collective-permute-done((bf16[96,768]{1,0:T(8,128)(2,1)}, bf16[96,768]{1,0:T(8,128)(2,1)S(1)}, u32[]{:S(2)}, u32[]{:S(2)}) %collective-permute-start) | collective-permute-done | bytes 147488 | tf_op jit(solution)/shard_map/ppermute | solution.py:412
  7.2 0.0 copy-start.2
  7.2 0.7 copy-done.2
  7.9 18.0 %shard_map.237 = (f32[256,1,256]{2,1,0:T(1,128)}, f32[256,128]{1,0:T(8,128)}) custom-call(s32[3]{0:T(128)} %dil.1, bf16[96,768]{1,0:T(8,128)(2,1)} %copy-done.2, f32[3,4096]{1,0:T(4,128)} %wh.3, bf16[64,4096]{1,0:T(8,128)(2,1)} %cot.3, f32[3,64]{1,0:T(4,128)} %bitcast.9, bf16[3,64,128]{2,1,0:T(8,128)(2,1)} %bitcast.7, bf16[3,64,128]{2,1,0:T(8,128)(2,1)} %bitcast.8, ...), custom_call_target="tpu_custom_call" | custom-call | tf_op jit(solution)/shard_map/pallas_call | solution.py:455
  25.9 0.0 copy-start.12
  25.9 0.0 copy-start.5
  25.9 0.0 copy-start.6
  25.9 0.0 copy-start.7
  26.0 15.8 %all-to-all-start = ((f32[256,1,256]{2,1,0:T(1,128)}), f32[256,1,256]{2,1,0:T(1,128)S(1)}, u32[]{:S(2)}, u32[]{:S(2)}) async-start(f32[256,1,256]{2,1,0:T(1,128)} %get-tuple-element.16), calls=%async_computation | async-start | bytes 524288 | tf_op jit(solution)/shard_map/all_to_all | solution.py:395
  41.7 0.0 copy-done.12
  41.7 0.0 copy-done.5
  41.8 0.0 copy-done.6
  41.8 0.0 copy-done.7
  41.8 0.0 copy-start.3
  41.8 0.0 copy-start.4
  41.8 0.0 copy-start.11
  41.8 0.9 multiply_add_fusion.inner
  42.7 0.0 copy-done.3
  42.7 0.0 copy-done.4
  42.7 0.0 copy-done.11
  42.7 1.9 %sine_multiply_fusion = (f32[256,128]{1,0:T(8,128)}, f32[256,128]{1,0:T(8,128)}, f32[256,128]{1,0:T(8,128)}, f32[256,128]{1,0:T(8,128)}) fusion(f32[128]{0:T(128)S(1)} %copy-done.11, s32[256,128]{1,0:T(8,128)S(1)} %copy-done.3, s32[256]{0:T(256)S(1)} %broadcast_multiply_fusion.1, s32[256,128]{1,0:T(8,128)S(1)} %copy-done.4), kind=kLoop, calls=%fused_computation.16 | loop fusion | flops 1048576 | bytes 787968 | tf_op jit(solution)/shard_map/mul | solution.py:424
  44.7 12.3 %all-to-all-done.got = f32[256,1,256]{2,1,0:T(1,128)S(1)} async-done(((f32[256,1,256]{2,1,0:T(1,128)}), f32[256,1,256]{2,1,0:T(1,128)S(1)}, u32[]{:S(2)}, u32[]{:S(2)}) %all-to-all-start) | async-done | bytes 262176 | tf_op jit(solution)/shard_map/all_to_all | solution.py:395
  57.0 0.0 copy-start
  57.0 0.7 copy-done
  57.7 2.9 %shard_map.238 = (f32[256,1,128]{2,1,0:T(1,128)}, f32[8,256]{1,0:T(8,128)}) custom-call(f32[256,1,256]{2,1,0:T(1,128)} %copy-done, f32[256,128]{1,0:T(8,128)} %get-tuple-element.17.late, bf16[2,256,512]{2,1,0:T(8,128)(2,1)} %constant.82.clone.table, f32[256,128]{1,0:T(8,128)} %get-tuple-element.31.twist_cos, f32[256,128]{1,0:T(8,128)} %get-tuple-element.32.twist_sin, ...), custom_call_target="tpu_custom_call" | custom-call | tf_op jit(solution)/shard_map/pallas_call | solution.py:460
  60.6 0.0 copy-start.8
  60.6 5.9 %all-to-all-start.1 = ((f32[256,1,128]{2,1,0:T(1,128)}), f32[256,1,128]{2,1,0:T(1,128)S(1)}, u32[]{:S(2)}, u32[]{:S(2)}) async-start(f32[256,1,128]{2,1,0:T(1,128)} %get-tuple-element.18), calls=%async_computation.1 | async-start | bytes 262144 | tf_op jit(solution)/shard_map/all_to_all | solution.py:395
  66.5 0.5 broadcast.52
  67.1 0.0 copy-done.8
  67.1 0.7 reduce.3
  67.8 0.0 copy-start.9
  67.8 0.1 reshape.23
  67.9 0.6 copy-done.9
  68.5 0.6 reshape.24.psd
  69.1 0.9 concatenate.3.bins
  69.9 3.1 %shard_map.239.weights = f32[256,128]{1,0:T(8,128)} custom-call(s32[256,128]{1,0:T(8,128)} %concatenate.3.bins, f32[16,128]{1,0:T(8,128)} %reshape.24.psd), custom_call_target="tpu_custom_call" | custom-call | tf_op jit(solution)/shard_map/pallas_call | solution.py:439
  73.0 6.7 %all-to-all-done.1.got = f32[256,1,128]{2,1,0:T(1,128)S(1)} async-done(((f32[256,1,128]{2,1,0:T(1,128)}), f32[256,1,128]{2,1,0:T(1,128)S(1)}, u32[]{:S(2)}, u32[]{:S(2)}) %all-to-all-start.1) | async-done | bytes 131104 | tf_op jit(solution)/shard_map/all_to_all | solution.py:395
  79.7 0.0 copy-start.1
  79.7 0.6 copy-done.1
  80.3 2.9 %shard_map.240 = (f32[256,1,256]{2,1,0:T(1,128)}, f32[8,128]{1,0:T(8,128)}) custom-call(f32[256,1,128]{2,1,0:T(1,128)} %copy-done.1, f32[8,256]{1,0:T(8,128)} %get-tuple-element.19.sums, f32[256,128]{1,0:T(8,128)} %shard_map.239.weights, bf16[2,256,512]{2,1,0:T(8,128)(2,1)} %constant.83.clone.table), custom_call_target="tpu_custom_call" | custom-call | tf_op jit(solution)/shard_map/pallas_call | solution.py:464
  83.2 22.4 %all_to_all.20.got.got_before = f32[256,1,256]{2,1,0:T(1,128)} all-to-all(f32[256,1,256]{2,1,0:T(1,128)} %get-tuple-element.20), channel_id=1, replica_groups=mesh['rows'=8,'cols'=32] {'rows','cols'}, dimensions={0} | all-to-all | bytes 524288 | tf_op jit(solution)/shard_map/all_to_all | solution.py:395
  105.6 2.9 %shard_map.241 = f32[256,1,128]{2,1,0:T(1,128)} custom-call(f32[256,1,256]{2,1,0:T(1,128)} %all_to_all.20.got.got_before, f32[8,128]{1,0:T(8,128)} %get-tuple-element.21.sums_late, bf16[2,256,512]{2,1,0:T(8,128)(2,1)} %constant.84.clone.table, f32[256,128]{1,0:T(8,128)} %get-tuple-element.28.twist_cos, f32[256,128]{1,0:T(8,128)} %get-tuple-element.27.twist_sin, ...), custom_call_target="tpu_custom_call" | custom-call | tf_op jit(solution)/shard_map/pallas_call | solution.py:468
  108.5 20.1 %all_to_all.21.got = f32[256,1,128]{2,1,0:T(1,128)} all-to-all(f32[256,1,128]{2,1,0:T(1,128)} %shard_map.241), channel_id=1, replica_groups=mesh['rows'=8,'cols'=32] {'rows','cols'}, dimensions={0} | all-to-all | bytes 262144 | tf_op jit(solution)/shard_map/all_to_all | solution.py:395
  128.6 2.0 %shard_map.242 = (f32[3,4096]{1,0:T(4,128)}, f32[3,64,128]{2,1,0:T(8,128)}, f32[3,64,128]{2,1,0:T(8,128)}, f32[3,64,64]{2,1,0:T(8,128)}, f32[3,64]{1,0:T(4,128)}) custom-call(f32[256,1,128]{2,1,0:T(1,128)} %all_to_all.21.got, f32[256,1,256]{2,1,0:T(1,128)} %all_to_all.20.got.got_before), custom_call_target="tpu_custom_call" | custom-call | tf_op jit(solution)/shard_map/pallas_call | solution.py:473
  (4 shorter events, 0.0 us)
Async XLA Ops:
  2.2 5.0 %collective-permute-start = (bf16[96,768]{1,0:T(8,128)(2,1)}, bf16[96,768]{1,0:T(8,128)(2,1)S(1)}, u32[]{:S(2)}, u32[]{:S(2)}) collective-permute-start(bf16[96,768]{1,0:T(8,128)(2,1)} %shard_map.236), channel_id=1, source_target_pairs={{0,1},{1,2},{2,3},{3,4},{4,5},{5,6},{6,7},{7,8},{8,9},{9,10},{10,1... | collective-permute-start | bytes 442376 | tf_op jit(solution)/shard_map/ppermute | solution.py:412
  4.8 0.7 copy-start.10
  7.2 0.7 copy-start.2
  25.9 15.8 %copy-start.12 = (s32[128]{0:T(128)S(1)}, s32[128]{0:T(128)}, u32[]{:S(2)}) copy-start(s32[128]{0:T(128)} %constant.79.clone) | copy-start | bytes 1540
  25.9 15.8 %copy-start.5 = (f32[128,128]{1,0:T(8,128)S(1)}, f32[128,128]{1,0:T(8,128)}, u32[]{:S(2)}) copy-start(f32[128,128]{1,0:T(8,128)} %constant.81.clone) | copy-start | bytes 196612
  25.9 15.8 %copy-start.6 = (f32[128,128]{1,0:T(8,128)S(1)}, f32[128,128]{1,0:T(8,128)}, u32[]{:S(2)}) copy-start(f32[128,128]{1,0:T(8,128)} %constant.80.clone) | copy-start | bytes 196612
  25.9 15.8 %copy-start.7 = (s32[128,128]{1,0:T(8,128)S(1)}, s32[128,128]{1,0:T(8,128)}, u32[]{:S(2)}) copy-start(s32[128,128]{1,0:T(8,128)} %constant.78.clone) | copy-start | bytes 196612
  26.0 31.0 %all-to-all-start = ((f32[256,1,256]{2,1,0:T(1,128)}), f32[256,1,256]{2,1,0:T(1,128)S(1)}, u32[]{:S(2)}, u32[]{:S(2)}) async-start(f32[256,1,256]{2,1,0:T(1,128)} %get-tuple-element.16), calls=%async_computation | async-start | bytes 524288 | tf_op jit(solution)/shard_map/all_to_all | solution.py:395
  41.8 1.0 copy-start.3
  41.8 1.0 copy-start.4
  41.8 1.0 copy-start.11
  57.0 0.7 copy-start
  60.6 6.5 %copy-start.8 = (s32[4096,1,1]{0,2,1:T(1,128)S(1)}, s32[4096,1,1]{0,2,1:T(1,128)}, u32[]{:S(2)}) copy-start(s32[4096,1,1]{0,2,1:T(1,128)} %param.28) | copy-start | bytes 49156
  60.6 19.1 %all-to-all-start.1 = ((f32[256,1,128]{2,1,0:T(1,128)}), f32[256,1,128]{2,1,0:T(1,128)S(1)}, u32[]{:S(2)}, u32[]{:S(2)}) async-start(f32[256,1,128]{2,1,0:T(1,128)} %get-tuple-element.18), calls=%async_computation.1 | async-start | bytes 262144 | tf_op jit(solution)/shard_map/all_to_all | solution.py:395
  67.8 0.7 copy-start.9
  79.7 0.6 copy-start.1

commit v3 on v2

--- a/solution.py
+++ b/solution.py
@@ -56,7 +56,7 @@
 
 def conv_kernel(
     dil, got, wh, cot, lift_t, now_t, past_t, mix,
-    sent, late, parts, w_cat, w_cat_t, mix_t, square, whu, cotu,
+    sent, parts, w_cat, w_cat_t, mix_t, square, whu, cotu,
     f0, f1, f2, x1, x2, fl1, fl2, sg1, sg2, gt1, gt2, ah, ah2, dp, dp2, g_conv, g_mix, x_t,
 ):
     lane = lane_ids(64)
@@ -193,9 +193,9 @@
         ah_out[:, at] = back[64:]
         if own:
             g_conv[layer] += dot_nt(both, d_pre)
-            g_mix[layer] += dot_nt(
-                dfield_b, jnp.concatenate([jnp.zeros((64, width), BF16), gate], axis=0)
-            )
+            empty = jnp.zeros((64, width), BF16)
+            placed = [empty, gate] if layer == 1 else [gate, empty]
+            g_mix[layer] += dot_nt(dfield_b, jnp.concatenate(placed, axis=0))
 
     def last_layer(start, width, own):
         now, both, filt, sig, gate = gates(2, f2, start, width)
@@ -231,7 +231,6 @@
     lax.fori_loop(0, SEG // STEP, step1, 0)
     saved_layer(0, x1, fl1, sg1, gt1, ah2, dp2, ah, dp, BASE + SEG, 256, False)
 
-    x_t[...] = jnp.zeros_like(x_t)
     g_lift = jnp.zeros((8, LANES), F32)
     blank = jnp.zeros((64, 256), BF16)
     for m in range(16):
@@ -241,8 +240,11 @@
         low = (dfield - high.astype(F32)).astype(BF16)
         on_high = dot32(lift_16, high)
         x8 = on_high[0:8] + on_high[8:16] + dot32(lift_16, low)[0:8]
-        for channel in range(3):
-            x_t[channel * 16 + m : channel * 16 + m + 1] = x8[channel : channel + 1]
+        for half in range(2):
+            for channel in range(3):
+                x_t[2 * m + half : 2 * m + half + 1, channel * LANES : (channel + 1) * LANES] = x8[
+                    channel : channel + 1, half * LANES : (half + 1) * LANES
+                ]
         seen = whu[:, LEFT + m * 256 : LEFT + (m + 1) * 256]
         seen_high = seen.astype(BF16).astype(F32)
         seen_16 = jnp.concatenate([seen_high, seen - seen_high], axis=0).astype(BF16)
@@ -252,101 +254,129 @@
             + dot_nt(seen_16, jnp.concatenate([blank, low], axis=0))[0:8]
         )
 
-    low = lane_ids(256) < 64
-    early = jnp.concatenate([g_conv[2], g_mix[1], g_lift, jnp.zeros((56, LANES), F32)], axis=0)
-    sent[:, 0, 0:128] = jnp.where(low, x_t[...].T, early)
-    sent[:, 0, 128:256] = jnp.concatenate([g_conv[0], g_conv[1]], axis=0)
-    late[...] = jnp.concatenate([pltpu.roll(g_conv[2], 64, 1), g_mix[0], g_mix[2]], axis=0)
-
-
-def swap(x):
-    first = (lane_ids(x.shape[0]) // 16) % 2 == 0
-    return jnp.where(first, pltpu.roll(x, LANES - 16, 1), -pltpu.roll(x, 16, 1))
-
-
-def wide_dot(table, x, sign):
-    low = lane_ids(256) < 64
-    parts = []
-    for value in (x, sign * swap(x)):
-        high = value.astype(BF16)
-        rest = value - high.astype(F32)
-        parts.append((high, jnp.where(low, high.astype(F32), pltpu.roll(rest, 64, 1)).astype(BF16)))
-    mixed = dot32(table[0], jnp.concatenate([parts[0][1], parts[1][1]], axis=0))
-    small = dot32(table[1], jnp.concatenate([parts[0][0], parts[1][0]], axis=0))
-    return mixed + pltpu.roll(mixed, 64, 1) + small
-
-
-def first_kernel(got, late, table, twist_cos, twist_sin, inner, sent, sums):
-    data = got[:, 0, 0:128]
-    rest = got[:, 0, 128:256]
-    low = lane_ids(256) < 64
-    x = jnp.where(low, data, 0.0)
-    sums[:, 0:128] = jnp.broadcast_to(jnp.sum(data, axis=0, keepdims=True), (8, 128))
-    sums[:, 128:256] = jnp.broadcast_to(jnp.sum(rest, axis=0, keepdims=True), (8, 128))
-    y = wide_dot(table, x, 1.0)
-    y = y * twist_cos[...] + swap(y) * twist_sin[...]
-    y = lax.dot(y, inner[...], precision=lax.Precision.HIGHEST, preferred_element_type=F32)
-    sent[:, 0, :] = jnp.where(low, y, late[...])
-
-
-def middle_kernel(got, sums, weights, table, sent, sums_late):
-    data = got[:, 0, :]
-    low = lane_ids(256) < 64
-    x = jnp.where(low, data, 0.0)
-    sums_late[...] = jnp.broadcast_to(jnp.sum(data, axis=0, keepdims=True), (8, 128))
-    y = wide_dot(table, x, 1.0)
-    y = jnp.where(low, y * weights[...], 0.0)
-    y = wide_dot(table, y, -1.0)
-    sent[:, 0, 0:128] = jnp.where(low, y, jnp.broadcast_to(sums[0:1, 0:128], (256, 128)))
-    sent[:, 0, 128:256] = jnp.broadcast_to(sums[0:1, 128:256], (256, 128))
-
-
-def third_kernel(got, sums_late, table, twist_cos, twist_sin, inner, sent):
-    low = lane_ids(256) < 64
-    x = jnp.where(low, got[:, 0, 0:128], 0.0)
-    y = dot_nt(x, inner[...], lax.Precision.HIGHEST)
-    y = y * twist_cos[...] - swap(y) * twist_sin[...]
-    y = wide_dot(table, y, -1.0)
-    sent[:, 0, :] = jnp.where(low, y, jnp.broadcast_to(sums_late[0:1], (256, 128)))
-
-
-def last_kernel(scaling, got, got_before, data_grad, now_t, past_t, grad_mix, lift_t):
-    last = got[:, 0, :]
-    turned = last.T
-    for channel in range(3):
-        for slot in range(16):
-            row = channel * 16 + slot
-            m = (slot - SHIFT // 256) % 16
-            data_grad[channel : channel + 1, m * 256 : (m + 1) * 256] = turned[row : row + 1]
-    late = pltpu.roll(last, 64, 1) * scaling
-    early = got_before[:, 0, 0:128] * scaling
-    main = got_before[:, 0, 128:256] * scaling
-    third = jnp.where(lane_ids(128) < 64, late[0:128], early[0:128])
-    for layer, value in enumerate((main[0:128], main[128:256], third)):
+    sent[:, 0, :] = jnp.concatenate([x_t[...].astype(BF16)] * 8, axis=0)
+    corner = jnp.concatenate(
+        [g_mix[0] + g_mix[1], g_mix[2, 0:8] + g_lift, g_mix[2, 8:64]], axis=0
+    )
+    sent[:, 1, 0:128] = jnp.concatenate([g_conv[0], g_conv[1]], axis=0).astype(BF16)
+    sent[:, 1, 128:256] = jnp.concatenate([g_conv[2], corner], axis=0).astype(BF16)
+    sent[:, 1, 256:384] = jnp.zeros((256, LANES), BF16)
+
+
+def halves(value):
+    high = value.astype(BF16)
+    return high, (value - high.astype(F32)).astype(BF16)
+
+
+def left_dot(table, value):
+    high, low = halves(value)
+    return dot32(table[...], jnp.concatenate([high, low, high], axis=0))
+
+
+def right_dot(dot, table, value):
+    high, low = halves(value)
+    rows = value.shape[0]
+    mixed = dot(jnp.concatenate([high, low], axis=0), table[0])
+    return mixed[:rows] + mixed[rows:] + dot(high, table[1])
+
+
+def first_kernel(got, table, twist_cos, twist_sin, sent, sums):
+    grads = jnp.sum(got[:, 1, 0:256].astype(F32), axis=0, keepdims=True)
+    sums[...] = jnp.broadcast_to(grads, (8, 256))
+    both = dot32(table[...], got[:, 0, :])
+    both = both[0:64] + both[64:128]
+    cos = [both[0:32, k * LANES : (k + 1) * LANES] for k in range(3)]
+    sin = [both[32:64, k * LANES : (k + 1) * LANES] for k in range(3)]
+    for k, (real, imag) in enumerate(
+        ((cos[0] + sin[1], cos[1] - sin[0]), (cos[2], -sin[2]))
+    ):
+        sent[:, 2 * k, :] = real * twist_cos[...] + imag * twist_sin[...]
+        sent[:, 2 * k + 1, :] = imag * twist_cos[...] - real * twist_sin[...]
+
+
+def middle_kernel(got, weights, outer, fast, outer_back, turn_cos, turn_sin, sent):
+    pieces = [got[:, k, :] for k in range(4)]
+    y = jnp.concatenate(
+        [
+            jnp.concatenate([pieces[0], pieces[2]], axis=1),
+            jnp.concatenate([pieces[1], pieces[3]], axis=1),
+        ],
+        axis=0,
+    )
+    y = left_dot(outer, y)
+    cos, sin = turn_cos[...], turn_sin[...]
+    rows = []
+    for k in range(2):
+        real = y[0:32, k * LANES : (k + 1) * LANES]
+        imag = y[32:64, k * LANES : (k + 1) * LANES]
+        rows.append(jnp.concatenate([real * cos + imag * sin, imag * cos - real * sin], axis=1))
+    y = right_dot(dot32, fast, jnp.concatenate(rows, axis=0))
+    y = y * jnp.concatenate([weights[...], weights[...]], axis=1)
+    y = right_dot(dot_nt, fast, y)
+    reals, imags = [], []
+    for k in range(2):
+        real = y[k * 32 : (k + 1) * 32, 0:LANES]
+        imag = y[k * 32 : (k + 1) * 32, LANES:]
+        reals.append(real * cos - imag * sin)
+        imags.append(imag * cos + real * sin)
+    y = jnp.concatenate(
+        [jnp.concatenate(reals, axis=1), jnp.concatenate(imags, axis=1)], axis=0
+    )
+    y = left_dot(outer_back, y)
+    for k in range(2):
+        sent[:, 2 * k, :] = y[0:32, k * LANES : (k + 1) * LANES]
+        sent[:, 2 * k + 1, :] = y[32:64, k * LANES : (k + 1) * LANES]
+
+
+def third_kernel(got, sums, table, twist_cos, twist_sin, sent):
+    cos, sin = twist_cos[...], twist_sin[...]
+    real = [got[:, k, :] * cos - got[:, k + 1, :] * sin for k in (0, 2)]
+    imag = [got[:, k + 1, :] * cos + got[:, k, :] * sin for k in (0, 2)]
+    y = jnp.concatenate(
+        [
+            jnp.concatenate([real[0], imag[0], real[1]], axis=1),
+            jnp.concatenate([imag[0], -real[0], imag[1]], axis=1),
+        ],
+        axis=0,
+    )
+    sent[:, 0, :] = left_dot(table, y).astype(BF16)
+    sent[:, 1, 0:256] = jnp.broadcast_to(sums[0:1], (256, 256)).astype(BF16)
+    sent[:, 1, 256:384] = jnp.zeros((256, LANES), BF16)
+
+
+def last_kernel(scaling, got, data_grad, now_t, past_t, grad_mix, lift_t):
+    value = got[:, 0, :].astype(F32)
+    total = value[0:32]
+    for k in range(1, 8):
+        total = total + value[32 * k : 32 * (k + 1)]
+    for piece in range(32):
+        for channel in range(3):
+            data_grad[channel : channel + 1, piece * LANES : (piece + 1) * LANES] = total[
+                piece : piece + 1, channel * LANES : (channel + 1) * LANES
+            ]
+    grads = got[:, 1, 0:256].astype(F32) * scaling
+    layers = (grads[0:128, 0:128], grads[128:256, 0:128], grads[0:128, 128:256])
+    for layer, value in enumerate(layers):
         now_t[layer] = value[0:64]
         past_t[layer] = value[64:128]
-    early = pltpu.roll(early[128:256], 64, 1)
-    grad_mix[0] = late[128:192, 0:64]
-    grad_mix[1] = early[0:64, 0:64]
-    grad_mix[2] = late[192:256, 0:64]
-    lift_t[...] = early[64:67, 0:64]
+    corner = grads[128:256, 128:256]
+    turned = pltpu.roll(corner, 64, 1)
+    grad_mix[0] = corner[0:64, 0:64]
+    grad_mix[1] = turned[0:64, 0:64]
+    grad_mix[2] = corner[64:128, 0:64]
+    lift_t[...] = turned[64:67, 0:64]
 
 
 def weight_kernel(bins, psd, out):
     at = bins[...]
     high = at // LANES
     low = at % LANES
-    second = lane_ids(256) >= 32
-    total = jnp.zeros((256, LANES), F32)
-    for h in range(8):
-        rows = [
-            jnp.take_along_axis(
-                jnp.broadcast_to(psd[8 * j + h : 8 * j + h + 1, :], (256, LANES)), low, axis=1
-            )
-            for j in range(2)
-        ]
-        total = jnp.where(high == h, jnp.where(second, rows[1], rows[0]), total)
-    out[...] = total
+    for j in range(2):
+        total = jnp.zeros((32, LANES), F32)
+        for h in range(8):
+            row = jnp.broadcast_to(psd[8 * j + h : 8 * j + h + 1, :], (32, LANES))
+            total = jnp.where(high == h, jnp.take_along_axis(row, low, axis=1), total)
+        out[32 * j : 32 * (j + 1)] = total
 
 
 def call(kernel, outs, scratch=(), smem=0, n_in=0, in_specs=None, grid=()):
@@ -369,30 +399,46 @@
 
 
 def two_parts(table):
-    high = table.astype(jnp.bfloat16)
-    low = (table - high.astype(np.float32)).astype(jnp.bfloat16)
-    return np.stack([high, low])
+    high = table.astype(np.float32).astype(jnp.bfloat16)
+    low = (table - high.astype(np.float64)).astype(np.float32).astype(jnp.bfloat16)
+    return high, low
+
+
+def for_left(table):
+    high, low = two_parts(table)
+    return np.concatenate([high, high, low], axis=-1)
 
 
 def tables(rows_count, cols_count):
     n = rows_count * cols_count
-    ids = np.arange(n)
-    residue = rows_count * (ids % cols_count) + ids // cols_count
-
-    def pair(product):
-        angle = 2.0 * np.pi / n * (product % n)
-        return two_parts(
-            np.concatenate([np.cos(angle), np.sin(angle)], axis=1).astype(np.float32)
-        )
-
-    outward = pair(residue[:, None] * ids[None, :])
-    plain = pair(ids[:, None] * ids[None, :])
-    inward = pair(ids[:, None] * residue[None, :])
-    return residue, outward, plain, inward
-
-
-def exchange(x):
-    return lax.all_to_all(x, BOTH, split_axis=0, concat_axis=0, tiled=True)
+    residue = rows_count * np.arange(cols_count)[None, :] + np.arange(rows_count)[:, None]
+    angle = 2.0 * np.pi / n * (residue[:, :, None] * np.arange(n)[None, None, :] % n)
+    outward = np.concatenate([np.cos(angle), np.sin(angle)], axis=1)
+    inward = np.swapaxes(np.concatenate([np.cos(angle), -np.sin(angle)], axis=1), 1, 2)
+    outward = np.concatenate(two_parts(outward), axis=1)
+    inward = for_left(inward)
+
+    def mixing(product, size, sign):
+        angle = 2.0 * np.pi / size * (product % size)
+        cos, sin = np.cos(angle), sign * np.sin(angle)
+        return np.block([[cos, sin], [-sin, cos]])
+
+    c = np.arange(cols_count)
+    l = np.arange(LANES)
+    outer = for_left(mixing(c[:, None] * c[None, :], cols_count, 1.0))
+    outer_back = for_left(
+        mixing((c[:, None] + SHIFT // LANES) * c[None, :], cols_count, -1.0)
+    )
+    fast = np.stack(two_parts(mixing(l[:, None] * l[None, :], LANES, -1.0)))
+    angle = 2.0 * np.pi / SEG * (c[:, None] * l[None, :])
+    return (
+        outward, inward, outer, outer_back, fast,
+        np.cos(angle).astype(np.float32), np.sin(angle).astype(np.float32),
+    )
+
+
+def exchange(x, axes):
+    return lax.all_to_all(x, axes, split_axis=0, concat_axis=0, tiled=True)
 
 
 def local(
@@ -401,7 +447,6 @@
 ):
     n = rows_count * cols_count
     total = n * SEG
-    me = lax.axis_index("rows") * cols_count + lax.axis_index("cols")
     message, = call(
         pack_kernel, [jax.ShapeDtypeStruct((96, SHIFT), BF16)], [pltpu.VMEM((32, SHIFT), F32)],
         in_specs=[
@@ -411,32 +456,22 @@
     )(cotangent, whitened)
     received = lax.ppermute(message, BOTH, [(i, (i + 1) % n) for i in range(n)])
 
-    residue, outward, plain, inward = tables(rows_count, cols_count)
-    row = np.arange(LANES)
-    slot = row % 16
-    later = np.where(slot < SHIFT // 256, slot + 16, slot)
-    inside = (row < 64).astype(np.float32)
-
-    def twist(steps):
-        fixed = jnp.asarray(residue[:, None] * (256 * steps)[None, :], jnp.int32)
-        product = (fixed + jnp.asarray(residue, jnp.int32)[:, None] * me) % total
-        angle = (2.0 * math.pi / total) * product.astype(F32)
-        return jnp.cos(angle) * inside, jnp.sin(angle) * inside
-
-    twist_cos, twist_sin = twist(slot)
-    back_cos, back_sin = twist(later)
-    same = (row[:, None] // 32 == row[None, :] // 32) & (row[:, None] < 64) & (row[None, :] < 64)
-    part = (row // 16) % 2
-    alike = same & (part[:, None] == part[None, :])
-    sign = np.where(part[:, None] > part[None, :], 1.0, -1.0) * (same & ~alike)
-    fixed = jnp.asarray(256 * slot[:, None] * slot[None, :], jnp.int32)
-    product = (fixed + jnp.asarray(slot, jnp.int32)[None, :] * me) % SEG
-    phase = (2.0 * math.pi / SEG) * product.astype(F32)
-    inner = jnp.cos(phase) * alike.astype(np.float32) + jnp.sin(phase) * sign.astype(np.float32)
-
-    bins = psd_bin.reshape(256, 16)
-    bins = jnp.concatenate([bins, bins, bins, bins, jnp.zeros((256, 64), jnp.int32)], axis=1)
-    weights = call(weight_kernel, [(256, LANES)], n_in=2)(
+    outward, inward, outer, outer_back, fast, turn_cos, turn_sin = tables(rows_count, cols_count)
+    my_row, my_col = lax.axis_index("rows"), lax.axis_index("cols")
+    outward = lax.dynamic_index_in_dim(jnp.asarray(outward), my_row, 0, keepdims=False)
+    inward = lax.dynamic_index_in_dim(jnp.asarray(inward), my_row, 0, keepdims=False)
+
+    def twist(ahead):
+        residue = rows_count * lax.broadcasted_iota(jnp.int32, (cols_count, LANES), 0) + my_row
+        sample = lax.broadcasted_iota(jnp.int32, (cols_count, LANES), 1) + LANES * (my_col + ahead)
+        angle = (2.0 * math.pi / total) * ((residue * sample) % total).astype(F32)
+        return jnp.cos(angle), jnp.sin(angle)
+
+    twist_cos, twist_sin = twist(0)
+    back_cos, back_sin = twist(SHIFT // LANES)
+
+    bins = psd_bin.reshape(LANES, cols_count).T
+    weights = call(weight_kernel, [(2 * cols_count, LANES)], n_in=2)(
         bins, (psd_weight * (1.0 / total)).reshape(16, LANES)
     )[0]
 
@@ -450,29 +485,27 @@
         ]
         + [big(64, F32)] * 3 + [big(128, BF16)] * 2 + [big(64, F32)] * 4 + [big(64, BF16)] * 2
         + [big(64, F32)] * 4
-        + [pltpu.VMEM((3, 128, 128), F32), pltpu.VMEM((3, 64, 128), F32), pltpu.VMEM((128, 256), F32)]
-    )
-    sent, late = call(conv_kernel, [(n, 1, 256), (n, LANES)], scratch, smem=1, n_in=7)(
+        + [pltpu.VMEM((3, 128, 128), F32), pltpu.VMEM((3, 64, 128), F32), pltpu.VMEM((32, 384), F32)]
+    )
+    packed = jax.ShapeDtypeStruct((n, 2, 3 * LANES), BF16)
+    sent, = call(conv_kernel, [packed], scratch, smem=1, n_in=7)(
         dilations, received, whitened, cotangent, lift_weight.T, jnp.swapaxes(conv_now, 1, 2),
         jnp.swapaxes(conv_past, 1, 2), mix_weight,
     )
-    got = exchange(sent)
-    sent, sums = call(first_kernel, [(n, 1, LANES), (8, 256)], n_in=6)(
-        got, late, outward, twist_cos, twist_sin, inner
-    )
-    got = exchange(sent)
-    sent, sums_late = call(middle_kernel, [(n, 1, 256), (8, LANES)], n_in=4)(
-        got, sums, weights, plain
-    )
-    before = exchange(sent)
-    sent, = call(third_kernel, [(n, 1, LANES)], n_in=6)(
-        before, sums_late, inward, back_cos, back_sin, inner
-    )
-    got = exchange(sent)
+    got = exchange(sent, BOTH)
+    pieces = (cols_count, 4, LANES)
+    sent, sums = call(first_kernel, [pieces, (8, 256)], n_in=4)(got, outward, twist_cos, twist_sin)
+    got = exchange(sent, "cols")
+    sent, = call(middle_kernel, [pieces], n_in=7)(
+        got, weights, outer, fast, outer_back, turn_cos, turn_sin
+    )
+    got = exchange(sent, "cols")
+    sent, = call(third_kernel, [packed], n_in=5)(got, sums, inward, back_cos, back_sin)
+    got = exchange(sent, BOTH)
     outs = [(3, SEG), (3, 64, 128), (3, 64, 128), (3, 64, 64), (3, 64)]
     data_grad, now_t, past_t, grad_mix, lift_t = call(
-        functools.partial(last_kernel, total ** -0.5), outs, n_in=2
-    )(got, before)
+        functools.partial(last_kernel, total ** -0.5), outs, n_in=1
+    )(got)
     return (
         data_grad, jnp.swapaxes(now_t, 1, 2), jnp.swapaxes(past_t, 1, 2), grad_mix, lift_t.T
     )

time: 131 us -> 119 us (0.908)
  blocking collectives: 42.5 us -> 23.9 us
  waiting for transfers between devices: 20.7 us -> 25.8 us
  starting transfers between devices: 24.3 us -> 27.9 us
  Pallas kernels: 33.3 us -> 30.6 us
  local copies, waits for them, and re-layouts: 5.41 us -> 7.75 us
  other arithmetic: 3.53 us -> 1.52 us
    all_to_all x2 -> x1, blocking collectives: 42.5 us -> 23.9 us  [exchange(): return lax.all_to_all(x, axes, split_axis=0, concat_axis=0, tiled=True)]
    all_to_all x2 -> x3, waiting for transfers between devices: 19 us -> 23.4 us  [exchange(): return lax.all_to_all(x, axes, split_axis=0, concat_axis=0, tiled=True)]
    all_to_all x2 -> x3, starting transfers between devices: 21.7 us -> 25.3 us  [exchange(): return lax.all_to_all(x, axes, split_axis=0, concat_axis=0, tiled=True)]
    squeeze x0 -> x2, local copies, waits for them, and re-layouts: none -> 3.04 us  [the longest x1 1.56 us: local(): lax.dynamic_index_in_dim(jnp.asarray(inward), my_row, 0, keepdims=False)]
    pallas_call x6, Pallas kernels: 31.7 us -> 29 us  [the longest x1 18.3 us: local(): call(conv_kernel, [packed], scratch, smem=1, n_in=7)]
    mul x3 -> x0, other arithmetic: 1.93 us -> none  [the longest x1 1.92 us: twist(): return (jnp.cos(angle) * inside, jnp.sin(angle) * inside)]
    unnamed x27 -> x13, local copies, waits for them, and re-layouts: 3.85 us -> 3.34 us
  transfers between devices with their start and end apart: 3 -> 4, of which waited for: 3 -> 4; matrix products, arithmetic and copies ran while one was open for 4% -> 5% of each run, Pallas kernels for 2% -> 1%
where the time goes in v3:
time: 119 us; the launch traced here: 118 us
  Pallas kernels  30.6 us (26%)
  starting transfers between devices  27.9 us (23%)
  waiting for transfers between devices  25.8 us (22%)
  blocking collectives  23.9 us (20%)
  local copies, waits for them, and re-layouts  7.75 us (7%)
  other arithmetic  1.52 us (1%)
    all_to_all x3, starting transfers between devices, exchange(): return lax.all_to_all(x, axes, split_axis=0, concat_axis=0, tiled=True)  25.3 us
    all_to_all x1, blocking collectives, exchange(): return lax.all_to_all(x, axes, split_axis=0, concat_axis=0, tiled=True)  23.9 us
    all_to_all x3, waiting for transfers between devices, exchange(): return lax.all_to_all(x, axes, split_axis=0, concat_axis=0, tiled=True)  23.4 us
    pallas_call x1, Pallas kernels, local(): call(conv_kernel, [packed], scratch, smem=1, n_in=7)  18.3 us
    unnamed x13, local copies, waits for them, and re-layouts  3.34 us
    ppermute x1, starting transfers between devices, local(): received = lax.ppermute(message, BOTH, [(i, (i + 1) % n) for i in range(n)])  2.59 us
    ppermute x1, waiting for transfers between devices, local(): received = lax.ppermute(message, BOTH, [(i, (i + 1) % n) for i in range(n)])  2.42 us
    pallas_call x1, Pallas kernels, local(): call(first_kernel, [pieces, (8, 256)], n_in=4)  2.42 us
  transfers between devices with their start and end apart: 4, of which 4 were waited for; matrix products, arithmetic and copies ran while one was open for 5% of the time, Pallas kernels for 1%

profile of v3, /device:TPU:1, one launch (start us, length us, event | category | flops | bytes accessed | tf_op | source)
XLA Modules:
  0.0 118.2 jit_solution(10504208344066712787)
XLA Ops:
  0.6 1.6 %shard_map.191 = bf16[96,768]{1,0:T(8,128)(2,1)} custom-call(bf16[64,4096]{1,0:T(8,128)(2,1)} %cot.3, f32[3,4096]{1,0:T(4,128)} %wh.3), custom_call_target="tpu_custom_call" | custom-call | tf_op jit(solution)/shard_map/pallas_call | solution.py:450
  2.2 2.6 %collective-permute-start = (bf16[96,768]{1,0:T(8,128)(2,1)}, bf16[96,768]{1,0:T(8,128)(2,1)S(1)}, u32[]{:S(2)}, u32[]{:S(2)}) collective-permute-start(bf16[96,768]{1,0:T(8,128)(2,1)} %shard_map.191), channel_id=1, source_target_pairs={{0,1},{1,2},{2,3},{3,4},{4,5},{5,6},{6,7},{7,8},{8,9},{9,10},{10,1... | collective-permute-start | bytes 442376 | tf_op jit(solution)/shard_map/ppermute | solution.py:457
  4.8 2.4 %collective-permute-done.got = bf16[96,768]{1,0:T(8,128)(2,1)S(1)} collective-permute-done((bf16[96,768]{1,0:T(8,128)(2,1)}, bf16[96,768]{1,0:T(8,128)(2,1)S(1)}, u32[]{:S(2)}, u32[]{:S(2)}) %collective-permute-start) | collective-permute-done | bytes 147488 | tf_op jit(solution)/shard_map/ppermute | solution.py:457
  7.3 0.0 copy-start.3
  7.3 0.6 copy-done.3
  7.9 18.3 %shard_map.192 = bf16[256,2,384]{2,1,0:T(2,128)(2,1)} custom-call(s32[3]{0:T(128)} %dil.1, bf16[96,768]{1,0:T(8,128)(2,1)} %copy-done.3, f32[3,4096]{1,0:T(4,128)} %wh.3, bf16[64,4096]{1,0:T(8,128)(2,1)} %cot.3, f32[3,64]{1,0:T(4,128)} %bitcast.15, bf16[3,64,128]{2,1,0:T(8,128)(2,1)} %bitcast.13, bf16[3,64,128]{2,1,0:T(8,128)(2,1)} %bitcast.14, ...), custom_call_target="tpu_custom_call" | custom-call | tf_op jit(solution)/shard_map/pallas_call | solution.py:491
  26.2 15.8 %all-to-all-start = ((bf16[256,2,384]{2,1,0:T(2,128)(2,1)}), bf16[256,2,384]{2,1,0:T(2,128)(2,1)S(1)}, u32[]{:S(2)}, u32[]{:S(2)}) async-start(bf16[256,2,384]{2,1,0:T(2,128)(2,1)} %shard_map.192), calls=%async_computation | async-start | bytes 786432 | tf_op jit(solution)/shard_map/all_to_all | solution.py:441
  42.0 1.5 %dynamic-slice_bitcast_fusion.1.table = bf16[128,256]{1,0:T(8,128)(2,1)} fusion(bf16[8,128,256]{2,1,0:T(8,128)(2,1)} %constant.61.clone, s32[]{:T(128)S(6)} %select_n.17), kind=kLoop, calls=%fused_computation.1 | loop fusion | bytes 131076 | tf_op jit(solution)/shard_map/jit(dynamic_index_in_dim)/squeeze | solution.py:461
  43.5 0.8 fusion.6
  44.3 14.7 %all-to-all-done.got = bf16[256,2,384]{2,1,0:T(2,128)(2,1)S(1)} async-done(((bf16[256,2,384]{2,1,0:T(2,128)(2,1)}), bf16[256,2,384]{2,1,0:T(2,128)(2,1)S(1)}, u32[]{:S(2)}, u32[]{:S(2)}) %all-to-all-start) | async-done | bytes 393248 | tf_op jit(solution)/shard_map/all_to_all | solution.py:441
  59.0 0.0 copy-start
  59.0 0.7 copy-done
  59.8 2.4 %shard_map.193 = (f32[32,4,128]{2,1,0:T(4,128)}, f32[8,256]{1,0:T(8,128)}) custom-call(bf16[256,2,384]{2,1,0:T(2,128)(2,1)} %copy-done, bf16[128,256]{1,0:T(8,128)(2,1)} %dynamic-slice_bitcast_fusion.1.table, f32[32,128]{1,0:T(8,128)} %get-tuple-element.23.twist_cos, f32[32,128]{1,0:T(8,128)} %get-tuple-element.24.twist_sin), custom_call_target="tpu_custom_call" | custom-call | tf_op jit(solution)/shard_map/pallas_call | solution.py:497
  62.2 0.0 copy-start.5
  62.2 5.1 %all-to-all-start.1 = ((f32[32,4,128]{2,1,0:T(4,128)}), f32[32,4,128]{2,1,0:T(4,128)S(1)}, u32[]{:S(2)}, u32[]{:S(2)}) async-start(f32[32,4,128]{2,1,0:T(4,128)} %get-tuple-element.12), calls=%async_computation.1 | async-start | bytes 131072 | tf_op jit(solution)/shard_map/all_to_all | solution.py:441
  67.4 0.0 copy-done.5
  67.4 0.0 copy-start.4
  67.4 0.5 broadcast.50
  67.9 0.2 copy-done.4
  68.1 0.7 reduce.3
  68.8 0.1 reshape.16
  68.8 0.7 copy.21
  69.5 0.6 reshape.17.psd
  70.1 1.6 %shard_map.194.weights = f32[64,128]{1,0:T(8,128)} custom-call(s32[32,128]{1,0:T(8,128)} %bitcast.12, f32[16,128]{1,0:T(8,128)} %reshape.17.psd), custom_call_target="tpu_custom_call" | custom-call | tf_op jit(solution)/shard_map/pallas_call | solution.py:474
  71.7 2.9 %all-to-all-done.1.got = f32[32,4,128]{2,1,0:T(4,128)S(1)} async-done(((f32[32,4,128]{2,1,0:T(4,128)}), f32[32,4,128]{2,1,0:T(4,128)S(1)}, u32[]{:S(2)}, u32[]{:S(2)}) %all-to-all-start.1) | async-done | bytes 65568 | tf_op jit(solution)/shard_map/all_to_all | solution.py:441
  74.7 0.0 copy-start.2
  74.7 0.6 copy-done.2
  75.3 2.3 %shard_map.195 = f32[32,4,128]{2,1,0:T(4,128)} custom-call(f32[32,4,128]{2,1,0:T(4,128)} %copy-done.2, f32[64,128]{1,0:T(8,128)} %shard_map.194.weights, bf16[64,192]{1,0:T(8,128)(2,1)} %constant.63.clone.outer, bf16[2,256,256]{2,1,0:T(8,128)(2,1)} %constant.64.clone.fast, bf16[64,192]{1,0:T(8,128)(2,1)} %constant.65.clone.outer_back, ...), custom_call_target="tpu_custom_call" | custom-call | tf_op jit(solution)/shard_map/pallas_call | solution.py:499
  77.6 4.4 %all-to-all-start.2 = ((f32[32,4,128]{2,1,0:T(4,128)}), f32[32,4,128]{2,1,0:T(4,128)S(1)}, u32[]{:S(2)}, u32[]{:S(2)}) async-start(f32[32,4,128]{2,1,0:T(4,128)} %shard_map.195), calls=%async_computation.2 | async-start | bytes 131072 | tf_op jit(solution)/shard_map/all_to_all | solution.py:441
  82.1 1.6 %dynamic-slice_bitcast_fusion.table = bf16[256,192]{1,0:T(8,128)(2,1)} fusion(bf16[8,256,192]{2,1,0:T(8,128)(2,1)} %constant.62.clone, s32[]{:T(128)S(6)} %select_n.17), kind=kLoop, calls=%fused_computation | loop fusion | bytes 196612 | tf_op jit(solution)/shard_map/jit(dynamic_index_in_dim)/squeeze | solution.py:462
  83.6 5.8 %all-to-all-done.2.got = f32[32,4,128]{2,1,0:T(4,128)S(1)} async-done(((f32[32,4,128]{2,1,0:T(4,128)}), f32[32,4,128]{2,1,0:T(4,128)S(1)}, u32[]{:S(2)}, u32[]{:S(2)}) %all-to-all-start.2) | async-done | bytes 65568 | tf_op jit(solution)/shard_map/all_to_all | solution.py:441
  89.4 0.0 copy-start.1
  89.4 0.6 copy-done.1
  90.0 2.2 %shard_map.196 = bf16[256,2,384]{2,1,0:T(2,128)(2,1)} custom-call(f32[32,4,128]{2,1,0:T(4,128)} %copy-done.1, f32[8,256]{1,0:T(8,128)} %get-tuple-element.13.sums, bf16[256,192]{1,0:T(8,128)(2,1)} %dynamic-slice_bitcast_fusion.table, f32[32,128]{1,0:T(8,128)} %get-tuple-element.20.twist_cos, f32[32,128]{1,0:T(8,128)} %get-tuple-element.19.twist_sin), custom_call_target="tpu_custom_call" | custom-call | tf_op jit(solution)/shard_map/pallas_call | solution.py:503
  92.3 23.9 %all_to_all.20.got = bf16[256,2,384]{2,1,0:T(2,128)(2,1)} all-to-all(bf16[256,2,384]{2,1,0:T(2,128)(2,1)} %shard_map.196), channel_id=1, replica_groups=mesh['rows'=8,'cols'=32] {'rows','cols'}, dimensions={0} | all-to-all | bytes 786432 | tf_op jit(solution)/shard_map/all_to_all | solution.py:441
  116.1 2.1 %shard_map.197 = (f32[3,4096]{1,0:T(4,128)}, f32[3,64,128]{2,1,0:T(8,128)}, f32[3,64,128]{2,1,0:T(8,128)}, f32[3,64,64]{2,1,0:T(8,128)}, f32[3,64]{1,0:T(4,128)}) custom-call(bf16[256,2,384]{2,1,0:T(2,128)(2,1)} %all_to_all.20.got), custom_call_target="tpu_custom_call" | custom-call | tf_op jit(solution)/shard_map/pallas_call | solution.py:506
  (3 shorter events, 0.0 us)
Async XLA Ops:
  2.2 5.0 %collective-permute-start = (bf16[96,768]{1,0:T(8,128)(2,1)}, bf16[96,768]{1,0:T(8,128)(2,1)S(1)}, u32[]{:S(2)}, u32[]{:S(2)}) collective-permute-start(bf16[96,768]{1,0:T(8,128)(2,1)} %shard_map.191), channel_id=1, source_target_pairs={{0,1},{1,2},{2,3},{3,4},{4,5},{5,6},{6,7},{7,8},{8,9},{9,10},{10,1... | collective-permute-start | bytes 442376 | tf_op jit(solution)/shard_map/ppermute | solution.py:457
  7.3 0.6 copy-start.3
  26.2 32.8 %all-to-all-start = ((bf16[256,2,384]{2,1,0:T(2,128)(2,1)}), bf16[256,2,384]{2,1,0:T(2,128)(2,1)S(1)}, u32[]{:S(2)}, u32[]{:S(2)}) async-start(bf16[256,2,384]{2,1,0:T(2,128)(2,1)} %shard_map.192), calls=%async_computation | async-start | bytes 786432 | tf_op jit(solution)/shard_map/all_to_all | solution.py:441
  59.0 0.7 copy-start
  62.2 5.2 %copy-start.5 = (f32[2,1024]{1,0:T(2,128)S(1)}, f32[2,1024]{1,0:T(2,128)}, u32[]{:S(2)}) copy-start(f32[2,1024]{1,0:T(2,128)} %param.24) | copy-start | bytes 24580
  62.2 12.5 %all-to-all-start.1 = ((f32[32,4,128]{2,1,0:T(4,128)}), f32[32,4,128]{2,1,0:T(4,128)S(1)}, u32[]{:S(2)}, u32[]{:S(2)}) async-start(f32[32,4,128]{2,1,0:T(4,128)} %get-tuple-element.12), calls=%async_computation.1 | async-start | bytes 131072 | tf_op jit(solution)/shard_map/all_to_all | solution.py:441
  67.4 0.7 copy-start.4
  74.7 0.6 copy-start.2
  77.6 11.8 %all-to-all-start.2 = ((f32[32,4,128]{2,1,0:T(4,128)}), f32[32,4,128]{2,1,0:T(4,128)S(1)}, u32[]{:S(2)}, u32[]{:S(2)}) async-start(f32[32,4,128]{2,1,0:T(4,128)} %shard_map.195), calls=%async_computation.2 | async-start | bytes 131072 | tf_op jit(solution)/shard_map/all_to_all | solution.py:441
  89.4 0.6 copy-start.1

commit v4 on v3

--- a/solution.py
+++ b/solution.py
@@ -18,7 +18,8 @@
 SPAN = SEG + 640
 BASE = 1024
 WIDE = BASE + SEG + 1024
-STEP = 1024
+STEP = 2048
+STRIDE = 2560
 LANES = 128
 
 
@@ -169,12 +170,12 @@
 
     def run_forward(layer, field, field_next, x, fl, sg, gt, start, rest):
         def step(i, carry):
-            forward(layer, field, field_next, x, fl, sg, gt, start + i * STEP, STEP)
+            forward(layer, field, field_next, x, fl, sg, gt, start + i * STRIDE, STRIDE)
             return carry
 
-        lax.fori_loop(0, 5, step, 0)
+        lax.fori_loop(0, 2, step, 0)
         if rest:
-            forward(layer, field, field_next, x, fl, sg, gt, start + 5 * STEP, rest)
+            forward(layer, field, field_next, x, fl, sg, gt, start + 2 * STRIDE, rest)
 
     run_forward(0, f0, f1, x1, fl1, sg1, gt1, BASE - 512, 128)
     run_forward(1, f1, f2, x2, fl2, sg2, gt2, BASE - 384, 0)
@@ -437,8 +438,12 @@
     )
 
 
+def near(x):
+    return pltpu.with_memory_space_constraint(x, pltpu.VMEM)
+
+
 def exchange(x, axes):
-    return lax.all_to_all(x, axes, split_axis=0, concat_axis=0, tiled=True)
+    return near(lax.all_to_all(x, axes, split_axis=0, concat_axis=0, tiled=True))
 
 
 def local(
@@ -454,7 +459,7 @@
         ],
         grid=(1,),
     )(cotangent, whitened)
-    received = lax.ppermute(message, BOTH, [(i, (i + 1) % n) for i in range(n)])
+    received = near(lax.ppermute(message, BOTH, [(i, (i + 1) % n) for i in range(n)]))
 
     outward, inward, outer, outer_back, fast, turn_cos, turn_sin = tables(rows_count, cols_count)
     my_row, my_col = lax.axis_index("rows"), lax.axis_index("cols")
@@ -494,13 +499,13 @@
     )
     got = exchange(sent, BOTH)
     pieces = (cols_count, 4, LANES)
-    sent, sums = call(first_kernel, [pieces, (8, 256)], n_in=4)(got, outward, twist_cos, twist_sin)
+    sent, sums = call(first_kernel, [pieces, (8, 256)], n_in=4)(got, near(outward), near(twist_cos), near(twist_sin))
     got = exchange(sent, "cols")
     sent, = call(middle_kernel, [pieces], n_in=7)(
-        got, weights, outer, fast, outer_back, turn_cos, turn_sin
+        got, near(weights), near(outer), near(fast), near(outer_back), near(turn_cos), near(turn_sin)
     )
     got = exchange(sent, "cols")
-    sent, = call(third_kernel, [packed], n_in=5)(got, sums, inward, back_cos, back_sin)
+    sent, = call(third_kernel, [packed], n_in=5)(got, near(sums), near(inward), near(back_cos), near(back_sin))
     got = exchange(sent, BOTH)
     outs = [(3, SEG), (3, 64, 128), (3, 64, 128), (3, 64, 64), (3, 64)]
     data_grad, now_t, past_t, grad_mix, lift_t = call(

time: 119 us -> 108 us (0.908)
  Pallas kernels: 30.6 us -> 22.2 us
  local copies, waits for them, and re-layouts: 7.75 us -> 4.44 us
  waiting for transfers between devices: 25.8 us -> 27.9 us
    pallas_call x1, Pallas kernels: 18.3 us -> 13.8 us  [local(): call(conv_kernel, [packed], scratch, smem=1, n_in=7)]
    unnamed x13 -> x19, local copies, waits for them, and re-layouts: 3.34 us -> 1.3 us
    all_to_all x3, waiting for transfers between devices: 23.4 us -> 25.5 us  [exchange(): lax.all_to_all(x, axes, split_axis=0, concat_axis=0, tiled=True)]
  transfers between devices with their start and end apart: 4 -> 4, of which waited for: 4 -> 4; matrix products, arithmetic and copies ran while one was open for 5% -> 4% of each run, Pallas kernels for 1% -> 1%
where the time goes in v4:
time: 108 us; the launch traced here: 107 us
  waiting for transfers between devices  27.9 us (26%)
  starting transfers between devices  27.8 us (26%)
  blocking collectives  23.2 us (21%)
  Pallas kernels  22.2 us (21%)
  local copies, waits for them, and re-layouts  4.44 us (4%)
    all_to_all x3, waiting for transfers between devices, exchange(): lax.all_to_all(x, axes, split_axis=0, concat_axis=0, tiled=True)  25.5 us
    all_to_all x3, starting transfers between devices, exchange(): lax.all_to_all(x, axes, split_axis=0, concat_axis=0, tiled=True)  25.2 us
    all_to_all x1, blocking collectives, exchange(): lax.all_to_all(x, axes, split_axis=0, concat_axis=0, tiled=True)  23.2 us
    pallas_call x1, Pallas kernels, local(): call(conv_kernel, [packed], scratch, smem=1, n_in=7)  13.8 us
    ppermute x1, starting transfers between devices, local(): lax.ppermute(message, BOTH, [(i, (i + 1) % n) for i in range(n)])  2.59 us
    ppermute x1, waiting for transfers between devices, local(): lax.ppermute(message, BOTH, [(i, (i + 1) % n) for i in range(n)])  2.42 us
  transfers between devices with their start and end apart: 4, of which 4 were waited for; matrix products, arithmetic and copies ran while one was open for 4% of the time, Pallas kernels for 1%

profile of v4, /device:TPU:1, one launch (start us, length us, event | category | flops | bytes accessed | tf_op | source)
XLA Modules:
  0.0 107.1 jit_solution(15951922919246025242)
XLA Ops:
  0.6 1.6 %shard_map.191 = bf16[96,768]{1,0:T(8,128)(2,1)} custom-call(bf16[64,4096]{1,0:T(8,128)(2,1)} %cot.3, f32[3,4096]{1,0:T(4,128)} %wh.3), custom_call_target="tpu_custom_call" | custom-call | tf_op jit(solution)/shard_map/pallas_call | solution.py:455
  2.3 2.6 %collective-permute-start = (bf16[96,768]{1,0:T(8,128)(2,1)}, bf16[96,768]{1,0:T(8,128)(2,1)S(1)}, u32[]{:S(2)}, u32[]{:S(2)}) collective-permute-start(bf16[96,768]{1,0:T(8,128)(2,1)} %shard_map.191), channel_id=1, source_target_pairs={{0,1},{1,2},{2,3},{3,4},{4,5},{5,6},{6,7},{7,8},{8,9},{9,10},{10,1... | collective-permute-start | bytes 442376 | tf_op jit(solution)/shard_map/ppermute | solution.py:462
  4.8 2.4 %collective-permute-done.got = bf16[96,768]{1,0:T(8,128)(2,1)S(1)} collective-permute-done((bf16[96,768]{1,0:T(8,128)(2,1)}, bf16[96,768]{1,0:T(8,128)(2,1)S(1)}, u32[]{:S(2)}, u32[]{:S(2)}) %collective-permute-start) | collective-permute-done | bytes 147488 | tf_op jit(solution)/shard_map/ppermute | solution.py:462
  7.3 13.8 %shard_map.192 = bf16[256,2,384]{2,1,0:T(2,128)(2,1)} custom-call(s32[3]{0:T(128)} %dil.1, bf16[96,768]{1,0:T(8,128)(2,1)S(1)} %collective-permute-done.got, f32[3,4096]{1,0:T(4,128)} %wh.3, bf16[64,4096]{1,0:T(8,128)(2,1)} %cot.3, f32[3,64]{1,0:T(4,128)} %bitcast.15, bf16[3,64,128]{2,1,0:T(8,128)(2,1)} %bitcast.13, bf16[3,64,128]{2,1,0:T(8,128)(2,1)} %bitcast.14, ...), custom_call_target="tpu_custom_call" | custom-call | tf_op jit(solution)/shard_map/pallas_call | solution.py:496
  21.1 15.8 %all-to-all-start = ((bf16[256,2,384]{2,1,0:T(2,128)(2,1)}), bf16[256,2,384]{2,1,0:T(2,128)(2,1)S(1)}, u32[]{:S(2)}, u32[]{:S(2)}) async-start(bf16[256,2,384]{2,1,0:T(2,128)(2,1)} %shard_map.192), calls=%async_computation | async-start | bytes 786432 | tf_op jit(solution)/shard_map/all_to_all | solution.py:446
  36.9 0.9 dynamic-slice_bitcast_fusion.1.table
  37.7 0.2 fusion.6
  37.9 16.0 %all-to-all-done.got = bf16[256,2,384]{2,1,0:T(2,128)(2,1)S(1)} async-done(((bf16[256,2,384]{2,1,0:T(2,128)(2,1)}), bf16[256,2,384]{2,1,0:T(2,128)(2,1)S(1)}, u32[]{:S(2)}, u32[]{:S(2)}) %all-to-all-start) | async-done | bytes 393248 | tf_op jit(solution)/shard_map/all_to_all | solution.py:446
  53.9 0.0 copy-start.8
  53.9 0.0 copy-start.7
  53.9 1.4 %shard_map.193 = (f32[32,4,128]{2,1,0:T(4,128)}, f32[8,256]{1,0:T(8,128)}) custom-call(bf16[256,2,384]{2,1,0:T(2,128)(2,1)S(1)} %all-to-all-done.got, bf16[128,256]{1,0:T(8,128)(2,1)S(1)} %dynamic-slice_bitcast_fusion.1.table, f32[32,128]{1,0:T(8,128)S(1)} %get-tuple-element.23.twist_cos, f32[32,128]{1,0:T(8,128)S(1)} %get-tuple-element.24.twist_sin), custom_call_target="tpu_custom_call" | custom-call | tf_op jit(solution)/shard_map/pallas_call | solution.py:502
  55.3 0.0 copy-start
  55.3 5.1 %all-to-all-start.1 = ((f32[32,4,128]{2,1,0:T(4,128)}), f32[32,4,128]{2,1,0:T(4,128)S(1)}, u32[]{:S(2)}, u32[]{:S(2)}) async-start(f32[32,4,128]{2,1,0:T(4,128)} %get-tuple-element.12), calls=%async_computation.1 | async-start | bytes 131072 | tf_op jit(solution)/shard_map/all_to_all | solution.py:446
  60.4 0.0 copy-done.8
  60.5 0.5 broadcast.50
  61.0 0.0 copy-done.7
  61.0 0.7 reduce.3
  61.7 0.1 reshape.16
  61.7 0.0 copy-start.4
  61.7 0.0 copy-start.5
  61.7 0.7 copy.21
  62.4 0.0 copy-start.3
  62.4 0.6 reshape.17.psd
  63.0 0.0 copy-start.2
  63.0 1.6 %shard_map.194.weights = f32[64,128]{1,0:T(8,128)} custom-call(s32[32,128]{1,0:T(8,128)} %bitcast.12, f32[16,128]{1,0:T(8,128)} %reshape.17.psd), custom_call_target="tpu_custom_call" | custom-call | tf_op jit(solution)/shard_map/pallas_call | solution.py:479
  64.6 3.1 %all-to-all-done.1.got = f32[32,4,128]{2,1,0:T(4,128)S(1)} async-done(((f32[32,4,128]{2,1,0:T(4,128)}), f32[32,4,128]{2,1,0:T(4,128)S(1)}, u32[]{:S(2)}, u32[]{:S(2)}) %all-to-all-start.1) | async-done | bytes 65568 | tf_op jit(solution)/shard_map/all_to_all | solution.py:446
  67.8 0.0 copy-done
  67.8 0.0 copy-done.4
  67.8 0.0 copy-done.5
  67.8 0.0 copy-done.3
  67.8 0.0 copy-done.2
  67.8 0.0 copy-start.1
  67.8 0.7 copy-done.1
  68.5 1.3 %shard_map.195 = f32[32,4,128]{2,1,0:T(4,128)} custom-call(f32[32,4,128]{2,1,0:T(4,128)S(1)} %all-to-all-done.1.got, f32[64,128]{1,0:T(8,128)S(1)} %copy-done.1, bf16[64,192]{1,0:T(8,128)(2,1)S(1)} %copy-done.2, bf16[2,256,256]{2,1,0:T(8,128)(2,1)S(1)} %copy-done, bf16[64,192]{1,0:T(8,128)(2,1)S(1)} %copy-done.3, f32[32,128]{1,0:T(8,128)S(1)} %copy-done.4, ...), custom_call_target="tpu_custom_call" | custom-call | tf_op jit(solution)/shard_map/pallas_call | solution.py:504
  69.9 4.3 %all-to-all-start.2 = ((f32[32,4,128]{2,1,0:T(4,128)}), f32[32,4,128]{2,1,0:T(4,128)S(1)}, u32[]{:S(2)}, u32[]{:S(2)}) async-start(f32[32,4,128]{2,1,0:T(4,128)} %shard_map.195), calls=%async_computation.2 | async-start | bytes 131072 | tf_op jit(solution)/shard_map/all_to_all | solution.py:446
  74.2 0.0 copy-start.6
  74.2 0.9 dynamic-slice_bitcast_fusion.table
  75.1 6.4 %all-to-all-done.2.got = f32[32,4,128]{2,1,0:T(4,128)S(1)} async-done(((f32[32,4,128]{2,1,0:T(4,128)}), f32[32,4,128]{2,1,0:T(4,128)S(1)}, u32[]{:S(2)}, u32[]{:S(2)}) %all-to-all-start.2) | async-done | bytes 65568 | tf_op jit(solution)/shard_map/all_to_all | solution.py:446
  81.5 0.0 copy-done.6
  81.5 1.3 %shard_map.196 = bf16[256,2,384]{2,1,0:T(2,128)(2,1)} custom-call(f32[32,4,128]{2,1,0:T(4,128)S(1)} %all-to-all-done.2.got, f32[8,256]{1,0:T(8,128)S(1)} %copy-done.6, bf16[256,192]{1,0:T(8,128)(2,1)S(1)} %dynamic-slice_bitcast_fusion.table, f32[32,128]{1,0:T(8,128)S(1)} %get-tuple-element.20.twist_cos, f32[32,128]{1,0:T(8,128)S(1)} %get-tuple-element.19.twist_sin), custom_call_target="tpu_custom_call" | custom-call | tf_op jit(solution)/shard_map/pallas_call | solution.py:508
  82.8 23.2 %all_to_all.20.got = bf16[256,2,384]{2,1,0:T(2,128)(2,1)S(1)} all-to-all(bf16[256,2,384]{2,1,0:T(2,128)(2,1)} %shard_map.196), channel_id=1, replica_groups=mesh['rows'=8,'cols'=32] {'rows','cols'}, dimensions={0} | all-to-all | bytes 786432 | tf_op jit(solution)/shard_map/all_to_all | solution.py:446
  105.9 1.1 %shard_map.197 = (f32[3,4096]{1,0:T(4,128)}, f32[3,64,128]{2,1,0:T(8,128)}, f32[3,64,128]{2,1,0:T(8,128)}, f32[3,64,64]{2,1,0:T(8,128)}, f32[3,64]{1,0:T(4,128)}) custom-call(bf16[256,2,384]{2,1,0:T(2,128)(2,1)S(1)} %all_to_all.20.got), custom_call_target="tpu_custom_call" | custom-call | tf_op jit(solution)/shard_map/pallas_call | solution.py:511
  (3 shorter events, 0.0 us)
Async XLA Ops:
  2.3 5.0 %collective-permute-start = (bf16[96,768]{1,0:T(8,128)(2,1)}, bf16[96,768]{1,0:T(8,128)(2,1)S(1)}, u32[]{:S(2)}, u32[]{:S(2)}) collective-permute-start(bf16[96,768]{1,0:T(8,128)(2,1)} %shard_map.191), channel_id=1, source_target_pairs={{0,1},{1,2},{2,3},{3,4},{4,5},{5,6},{6,7},{7,8},{8,9},{9,10},{10,1... | collective-permute-start | bytes 442376 | tf_op jit(solution)/shard_map/ppermute | solution.py:462
  21.1 32.8 %all-to-all-start = ((bf16[256,2,384]{2,1,0:T(2,128)(2,1)}), bf16[256,2,384]{2,1,0:T(2,128)(2,1)S(1)}, u32[]{:S(2)}, u32[]{:S(2)}) async-start(bf16[256,2,384]{2,1,0:T(2,128)(2,1)} %shard_map.192), calls=%async_computation | async-start | bytes 786432 | tf_op jit(solution)/shard_map/all_to_all | solution.py:446
  53.9 6.6 %copy-start.8 = (f32[2,1024]{1,0:T(2,128)S(1)}, f32[2,1024]{1,0:T(2,128)}, u32[]{:S(2)}) copy-start(f32[2,1024]{1,0:T(2,128)} %param.24) | copy-start | bytes 24580
  53.9 7.1 %copy-start.7 = (s32[4096,1,1]{0,2,1:T(1,128)S(1)}, s32[4096,1,1]{0,2,1:T(1,128)}, u32[]{:S(2)}) copy-start(s32[4096,1,1]{0,2,1:T(1,128)} %param.23) | copy-start | bytes 49156
  55.3 12.5 %copy-start = (bf16[2,256,256]{2,1,0:T(8,128)(2,1)S(1)}, bf16[2,256,256]{2,1,0:T(8,128)(2,1)}, u32[]{:S(2)}) copy-start(bf16[2,256,256]{2,1,0:T(8,128)(2,1)} %constant.64.clone.fast) | copy-start | bytes 786436
  55.3 12.5 %all-to-all-start.1 = ((f32[32,4,128]{2,1,0:T(4,128)}), f32[32,4,128]{2,1,0:T(4,128)S(1)}, u32[]{:S(2)}, u32[]{:S(2)}) async-start(f32[32,4,128]{2,1,0:T(4,128)} %get-tuple-element.12), calls=%async_computation.1 | async-start | bytes 131072 | tf_op jit(solution)/shard_map/all_to_all | solution.py:446
  61.7 6.0 %copy-start.4 = (f32[32,128]{1,0:T(8,128)S(1)}, f32[32,128]{1,0:T(8,128)}, u32[]{:S(2)}) copy-start(f32[32,128]{1,0:T(8,128)} %constant.66.clone.turn_cos) | copy-start | bytes 49156
  61.7 6.0 %copy-start.5 = (f32[32,128]{1,0:T(8,128)S(1)}, f32[32,128]{1,0:T(8,128)}, u32[]{:S(2)}) copy-start(f32[32,128]{1,0:T(8,128)} %constant.67.clone.turn_sin) | copy-start | bytes 49156
  62.4 5.3 %copy-start.3 = (bf16[64,192]{1,0:T(8,128)(2,1)S(1)}, bf16[64,192]{1,0:T(8,128)(2,1)}, u32[]{:S(2)}) copy-start(bf16[64,192]{1,0:T(8,128)(2,1)} %constant.65.clone.outer_back) | copy-start | bytes 73732
  63.0 4.7 %copy-start.2 = (bf16[64,192]{1,0:T(8,128)(2,1)S(1)}, bf16[64,192]{1,0:T(8,128)(2,1)}, u32[]{:S(2)}) copy-start(bf16[64,192]{1,0:T(8,128)(2,1)} %constant.63.clone.outer) | copy-start | bytes 73732
  67.8 0.8 copy-start.1
  69.9 11.6 %all-to-all-start.2 = ((f32[32,4,128]{2,1,0:T(4,128)}), f32[32,4,128]{2,1,0:T(4,128)S(1)}, u32[]{:S(2)}, u32[]{:S(2)}) async-start(f32[32,4,128]{2,1,0:T(4,128)} %shard_map.195), calls=%async_computation.2 | async-start | bytes 131072 | tf_op jit(solution)/shard_map/all_to_all | solution.py:446
  74.2 7.3 %copy-start.6 = (f32[8,256]{1,0:T(8,128)S(1)}, f32[8,256]{1,0:T(8,128)}, u32[]{:S(2)}) copy-start(f32[8,256]{1,0:T(8,128)} %get-tuple-element.13.sums) | copy-start | bytes 24580

commit v5 on v4

--- a/solution.py
+++ b/solution.py
@@ -255,13 +255,14 @@
             + dot_nt(seen_16, jnp.concatenate([blank, low], axis=0))[0:8]
         )
 
-    sent[:, 0, :] = jnp.concatenate([x_t[...].astype(BF16)] * 8, axis=0)
+    pair = x_t[:, 0:256].astype(BF16)
+    single = jnp.concatenate([x_t[:, 256:384], jnp.zeros((32, LANES), F32)], axis=1).astype(BF16)
+    sent[:, 0, :] = jnp.concatenate([pair] * 4 + [single] * 4, axis=0)
     corner = jnp.concatenate(
         [g_mix[0] + g_mix[1], g_mix[2, 0:8] + g_lift, g_mix[2, 8:64]], axis=0
     )
     sent[:, 1, 0:128] = jnp.concatenate([g_conv[0], g_conv[1]], axis=0).astype(BF16)
     sent[:, 1, 128:256] = jnp.concatenate([g_conv[2], corner], axis=0).astype(BF16)
-    sent[:, 1, 256:384] = jnp.zeros((256, LANES), BF16)
 
 
 def halves(value):
@@ -282,17 +283,17 @@
 
 
 def first_kernel(got, table, twist_cos, twist_sin, sent, sums):
-    grads = jnp.sum(got[:, 1, 0:256].astype(F32), axis=0, keepdims=True)
+    grads = jnp.sum(got[:, 1, :].astype(F32), axis=0, keepdims=True)
     sums[...] = jnp.broadcast_to(grads, (8, 256))
     both = dot32(table[...], got[:, 0, :])
-    both = both[0:64] + both[64:128]
-    cos = [both[0:32, k * LANES : (k + 1) * LANES] for k in range(3)]
-    sin = [both[32:64, k * LANES : (k + 1) * LANES] for k in range(3)]
-    for k, (real, imag) in enumerate(
-        ((cos[0] + sin[1], cos[1] - sin[0]), (cos[2], -sin[2]))
-    ):
-        sent[:, 2 * k, :] = real * twist_cos[...] + imag * twist_sin[...]
-        sent[:, 2 * k + 1, :] = imag * twist_cos[...] - real * twist_sin[...]
+    both = both[0:128] + both[128:256]
+    real = both[0:64, 0:LANES] + both[64:128, LANES:]
+    imag = both[0:64, LANES:] - both[64:128, 0:LANES]
+    turned_real = real * twist_cos[...] + imag * twist_sin[...]
+    turned_imag = imag * twist_cos[...] - real * twist_sin[...]
+    for k in range(2):
+        sent[:, 2 * k, :] = turned_real[32 * k : 32 * (k + 1)]
+        sent[:, 2 * k + 1, :] = turned_imag[32 * k : 32 * (k + 1)]
 
 
 def middle_kernel(got, weights, outer, fast, outer_back, turn_cos, turn_sin, sent):
@@ -331,31 +332,28 @@
 
 def third_kernel(got, sums, table, twist_cos, twist_sin, sent):
     cos, sin = twist_cos[...], twist_sin[...]
-    real = [got[:, k, :] * cos - got[:, k + 1, :] * sin for k in (0, 2)]
-    imag = [got[:, k + 1, :] * cos + got[:, k, :] * sin for k in (0, 2)]
+    real = jnp.concatenate([got[:, 0, :], got[:, 2, :]], axis=0)
+    imag = jnp.concatenate([got[:, 1, :], got[:, 3, :]], axis=0)
+    real, imag = real * cos - imag * sin, imag * cos + real * sin
     y = jnp.concatenate(
-        [
-            jnp.concatenate([real[0], imag[0], real[1]], axis=1),
-            jnp.concatenate([imag[0], -real[0], imag[1]], axis=1),
-        ],
-        axis=0,
+        [jnp.concatenate([real, imag], axis=1), jnp.concatenate([imag, -real], axis=1)], axis=0
     )
     sent[:, 0, :] = left_dot(table, y).astype(BF16)
-    sent[:, 1, 0:256] = jnp.broadcast_to(sums[0:1], (256, 256)).astype(BF16)
-    sent[:, 1, 256:384] = jnp.zeros((256, LANES), BF16)
+    sent[:, 1, :] = jnp.broadcast_to(sums[0:1], (256, 256)).astype(BF16)
 
 
 def last_kernel(scaling, got, data_grad, now_t, past_t, grad_mix, lift_t):
     value = got[:, 0, :].astype(F32)
-    total = value[0:32]
-    for k in range(1, 8):
-        total = total + value[32 * k : 32 * (k + 1)]
-    for piece in range(32):
-        for channel in range(3):
-            data_grad[channel : channel + 1, piece * LANES : (piece + 1) * LANES] = total[
-                piece : piece + 1, channel * LANES : (channel + 1) * LANES
+    pair, single = value[0:32], value[128:160, 0:LANES]
+    for k in range(1, 4):
+        pair = pair + value[32 * k : 32 * (k + 1)]
+        single = single + value[128 + 32 * k : 128 + 32 * (k + 1), 0:LANES]
+    for channel, part in enumerate((pair[:, 0:LANES], pair[:, LANES:], single)):
+        for piece in range(32):
+            data_grad[channel : channel + 1, piece * LANES : (piece + 1) * LANES] = part[
+                piece : piece + 1
             ]
-    grads = got[:, 1, 0:256].astype(F32) * scaling
+    grads = got[:, 1, :].astype(F32) * scaling
     layers = (grads[0:128, 0:128], grads[128:256, 0:128], grads[0:128, 128:256])
     for layer, value in enumerate(layers):
         now_t[layer] = value[0:64]
@@ -372,12 +370,11 @@
     at = bins[...]
     high = at // LANES
     low = at % LANES
-    for j in range(2):
-        total = jnp.zeros((32, LANES), F32)
-        for h in range(8):
-            row = jnp.broadcast_to(psd[8 * j + h : 8 * j + h + 1, :], (32, LANES))
-            total = jnp.where(high == h, jnp.take_along_axis(row, low, axis=1), total)
-        out[32 * j : 32 * (j + 1)] = total
+    total = jnp.zeros((64, LANES), F32)
+    for h in range(8):
+        row = jnp.broadcast_to(psd[h : h + 1, :], (64, LANES))
+        total = jnp.where(high == h, jnp.take_along_axis(row, low, axis=1), total)
+    out[...] = total
 
 
 def call(kernel, outs, scratch=(), smem=0, n_in=0, in_specs=None, grid=()):
@@ -412,7 +409,10 @@
 
 def tables(rows_count, cols_count):
     n = rows_count * cols_count
-    residue = rows_count * np.arange(cols_count)[None, :] + np.arange(rows_count)[:, None]
+    half = rows_count // 2
+    h = np.arange(2 * cols_count)
+    residue = rows_count * (h % cols_count) + half * (h // cols_count)
+    residue = residue[None, :] + np.arange(half)[:, None]
     angle = 2.0 * np.pi / n * (residue[:, :, None] * np.arange(n)[None, None, :] % n)
     outward = np.concatenate([np.cos(angle), np.sin(angle)], axis=1)
     inward = np.swapaxes(np.concatenate([np.cos(angle), -np.sin(angle)], axis=1), 1, 2)
@@ -461,25 +461,6 @@
     )(cotangent, whitened)
     received = near(lax.ppermute(message, BOTH, [(i, (i + 1) % n) for i in range(n)]))
 
-    outward, inward, outer, outer_back, fast, turn_cos, turn_sin = tables(rows_count, cols_count)
-    my_row, my_col = lax.axis_index("rows"), lax.axis_index("cols")
-    outward = lax.dynamic_index_in_dim(jnp.asarray(outward), my_row, 0, keepdims=False)
-    inward = lax.dynamic_index_in_dim(jnp.asarray(inward), my_row, 0, keepdims=False)
-
-    def twist(ahead):
-        residue = rows_count * lax.broadcasted_iota(jnp.int32, (cols_count, LANES), 0) + my_row
-        sample = lax.broadcasted_iota(jnp.int32, (cols_count, LANES), 1) + LANES * (my_col + ahead)
-        angle = (2.0 * math.pi / total) * ((residue * sample) % total).astype(F32)
-        return jnp.cos(angle), jnp.sin(angle)
-
-    twist_cos, twist_sin = twist(0)
-    back_cos, back_sin = twist(SHIFT // LANES)
-
-    bins = psd_bin.reshape(LANES, cols_count).T
-    weights = call(weight_kernel, [(2 * cols_count, LANES)], n_in=2)(
-        bins, (psd_weight * (1.0 / total)).reshape(16, LANES)
-    )[0]
-
     big = lambda rows, dtype: pltpu.VMEM((rows, WIDE), dtype)
     square = pltpu.VMEM((LANES, LANES), F32)
     scratch = (
@@ -492,17 +473,44 @@
         + [big(64, F32)] * 4
         + [pltpu.VMEM((3, 128, 128), F32), pltpu.VMEM((3, 64, 128), F32), pltpu.VMEM((32, 384), F32)]
     )
-    packed = jax.ShapeDtypeStruct((n, 2, 3 * LANES), BF16)
+    packed = jax.ShapeDtypeStruct((n, 2, 2 * LANES), BF16)
     sent, = call(conv_kernel, [packed], scratch, smem=1, n_in=7)(
         dilations, received, whitened, cotangent, lift_weight.T, jnp.swapaxes(conv_now, 1, 2),
         jnp.swapaxes(conv_past, 1, 2), mix_weight,
     )
+    outward, inward, outer, outer_back, fast, turn_cos, turn_sin = tables(rows_count, cols_count)
+    my_row, my_col, psd_bin, sent = lax.optimization_barrier(
+        (lax.axis_index("rows"), lax.axis_index("cols"), psd_bin, sent)
+    )
+    half = rows_count // 2
+    my_low, second = my_row % half, my_row >= half
+    outward = lax.dynamic_index_in_dim(jnp.asarray(outward), my_low, 0, keepdims=False)
+    inward = lax.dynamic_index_in_dim(jnp.asarray(inward), my_low, 0, keepdims=False)
+
+    def twist(ahead):
+        h = lax.broadcasted_iota(jnp.int32, (2 * cols_count, LANES), 0)
+        residue = rows_count * (h % cols_count) + half * (h // cols_count) + my_low
+        sample = lax.broadcasted_iota(jnp.int32, h.shape, 1) + LANES * (my_col + ahead)
+        angle = (2.0 * math.pi / total) * ((residue * sample) % total).astype(F32)
+        return jnp.cos(angle), jnp.sin(angle)
+
+    twist_cos, twist_sin = twist(0)
+    back_cos, back_sin = twist(SHIFT // LANES)
+
+    bins = psd_bin.reshape(LANES, cols_count).T
+    other = lax.ppermute(bins, "rows", [(i, (i + half) % rows_count) for i in range(rows_count)])
+    bins = jnp.concatenate(
+        [jnp.where(second, other, bins), jnp.where(second, bins, other)], axis=0
+    )
+    psd = jnp.where(second, psd_weight[1], psd_weight[0]) * (1.0 / total)
+    weights = call(weight_kernel, [(2 * cols_count, LANES)], n_in=2)(bins, psd.reshape(8, LANES))[0]
+
     got = exchange(sent, BOTH)
     pieces = (cols_count, 4, LANES)
     sent, sums = call(first_kernel, [pieces, (8, 256)], n_in=4)(got, near(outward), near(twist_cos), near(twist_sin))
     got = exchange(sent, "cols")
     sent, = call(middle_kernel, [pieces], n_in=7)(
-        got, near(weights), near(outer), near(fast), near(outer_back), near(turn_cos), near(turn_sin)
+        got, weights, near(outer), near(fast), near(outer_back), near(turn_cos), near(turn_sin)
     )
     got = exchange(sent, "cols")
     sent, = call(third_kernel, [packed], n_in=5)(got, near(sums), near(inward), near(back_cos), near(back_sin))

time: 108 us -> 103 us (0.954)
  waiting for transfers between devices: 27.9 us -> 19.5 us
  starting transfers between devices: 27.8 us -> 32.8 us
  local copies, waits for them, and re-layouts: 4.44 us -> 2.87 us
  other arithmetic: 0.91 us -> 2.27 us
    all_to_all x3, waiting for transfers between devices: 25.5 us -> 15.6 us  [exchange(): lax.all_to_all(x, axes, split_axis=0, concat_axis=0, tiled=True)]
    ppermute x0 -> x1, starting transfers between devices: none -> 6.26 us  [local(): lax.ppermute(bins, 'rows', [(i, (i + half) % rows_count) for i in range(r...]
    ppermute x0 -> x1, waiting for transfers between devices: none -> 1.42 us  [local(): lax.ppermute(bins, 'rows', [(i, (i + half) % rows_count) for i in range(r...]
    all_to_all x3, starting transfers between devices: 25.2 us -> 24 us  [exchange(): lax.all_to_all(x, axes, split_axis=0, concat_axis=0, tiled=True)]
  transfers between devices with their start and end apart: 4 -> 5, of which waited for: 4 -> 5; matrix products, arithmetic and copies ran while one was open for 4% -> 5% of each run, Pallas kernels for 1% -> 2%
where the time goes in v5:
time: 103 us
  starting transfers between devices  32.8 us (32%)
  blocking collectives  22.3 us (22%)
  Pallas kernels  22.2 us (22%)
  waiting for transfers between devices  19.5 us (19%)
  local copies, waits for them, and re-layouts  2.87 us (3%)
  other arithmetic  2.27 us (2%)
    all_to_all x3, starting transfers between devices, exchange(): lax.all_to_all(x, axes, split_axis=0, concat_axis=0, tiled=True)  24 us
    all_to_all x1, blocking collectives, exchange(): lax.all_to_all(x, axes, split_axis=0, concat_axis=0, tiled=True)  22.3 us
    all_to_all x3, waiting for transfers between devices, exchange(): lax.all_to_all(x, axes, split_axis=0, concat_axis=0, tiled=True)  15.6 us
    pallas_call x1, Pallas kernels, local(): call(conv_kernel, [packed], scratch, smem=1, n_in=7)  13.4 us
    ppermute x1, starting transfers between devices, local(): lax.ppermute(bins, 'rows', [(i, (i + half) % rows_count) for i in range(r...  6.26 us
    ppermute x1, starting transfers between devices, local(): lax.ppermute(message, BOTH, [(i, (i + 1) % n) for i in range(n)])  2.59 us
    ppermute x1, waiting for transfers between devices, local(): lax.ppermute(message, BOTH, [(i, (i + 1) % n) for i in range(n)])  2.4 us
    pallas_call x1, Pallas kernels, local(): call(middle_kernel, [pieces], n_in=7)  2.1 us
  transfers between devices with their start and end apart: 5, of which 5 were waited for; matrix products, arithmetic and copies ran while one was open for 5% of the time, Pallas kernels for 2%

profile of v5, /device:TPU:1, one launch (start us, length us, event | category | flops | bytes accessed | tf_op | source)
XLA Modules:
  0.0 102.7 jit_solution(6164853281639328666)
XLA Ops:
  0.6 1.6 %shard_map.191 = bf16[96,768]{1,0:T(8,128)(2,1)} custom-call(bf16[64,4096]{1,0:T(8,128)(2,1)} %cot.3, f32[3,4096]{1,0:T(4,128)} %wh.3), custom_call_target="tpu_custom_call" | custom-call | tf_op jit(solution)/shard_map/pallas_call | solution.py:455
  2.2 2.6 %collective-permute-start = (bf16[96,768]{1,0:T(8,128)(2,1)}, bf16[96,768]{1,0:T(8,128)(2,1)S(1)}, u32[]{:S(2)}, u32[]{:S(2)}) collective-permute-start(bf16[96,768]{1,0:T(8,128)(2,1)} %shard_map.191), channel_id=1, source_target_pairs={{0,1},{1,2},{2,3},{3,4},{4,5},{5,6},{6,7},{7,8},{8,9},{9,10},{10,1... | collective-permute-start | bytes 442376 | tf_op jit(solution)/shard_map/ppermute | solution.py:462
  4.8 2.4 %collective-permute-done.got = bf16[96,768]{1,0:T(8,128)(2,1)S(1)} collective-permute-done((bf16[96,768]{1,0:T(8,128)(2,1)}, bf16[96,768]{1,0:T(8,128)(2,1)S(1)}, u32[]{:S(2)}, u32[]{:S(2)}) %collective-permute-start) | collective-permute-done | bytes 147488 | tf_op jit(solution)/shard_map/ppermute | solution.py:462
  7.2 13.4 %shard_map.192 = bf16[256,2,256]{2,1,0:T(2,128)(2,1)} custom-call(s32[3]{0:T(128)} %dil.1, bf16[96,768]{1,0:T(8,128)(2,1)S(1)} %collective-permute-done.got, f32[3,4096]{1,0:T(4,128)} %wh.3, bf16[64,4096]{1,0:T(8,128)(2,1)} %cot.3, f32[3,64]{1,0:T(4,128)} %bitcast.19, bf16[3,64,128]{2,1,0:T(8,128)(2,1)} %bitcast.16, bf16[3,64,128]{2,1,0:T(8,128)(2,1)} %bitcast.17, ...), custom_call_target="tpu_custom_call" | custom-call | tf_op jit(solution)/shard_map/pallas_call | solution.py:477
  20.7 0.0 copy-start.6
  20.7 15.8 %all-to-all-start = ((bf16[256,2,256]{2,1,0:T(2,128)(2,1)}), bf16[256,2,256]{2,1,0:T(2,128)(2,1)S(1)}, u32[]{:S(2)}, u32[]{:S(2)}) async-start(bf16[256,2,256]{2,1,0:T(2,128)(2,1)} %shard_map.192), calls=%async_computation | async-start | bytes 524288 | tf_op jit(solution)/shard_map/all_to_all | solution.py:446
  36.5 0.5 broadcast.110
  37.0 0.0 copy-done.6
  37.0 0.7 reduce.3
  37.7 0.1 reshape.20
  37.7 0.1 copy.21
  37.8 6.3 %collective-permute-start.1 = (s32[32,128]{1,0:T(8,128)S(1)}, s32[32,128]{1,0:T(8,128)S(1)}, u32[]{:S(2)}, u32[]{:S(2)}) collective-permute-start(s32[32,128]{1,0:T(8,128)S(1)} %bitcast.15), channel_id=1, source_target_pairs={{0,128},{32,160},{64,192},{96,224},{128,0},{160,32},{192,64},{224,... | collective-permute-start | bytes 49160 | tf_op jit(solution)/shard_map/ppermute | solution.py:501
  44.1 0.0 copy-start.7
  44.1 0.4 fusion.6
  44.4 0.3 copy-done.7
  44.8 0.6 fusion.10
  45.4 0.9 dynamic-slice_bitcast_fusion.1.table
  46.3 1.4 %collective-permute-done.1 = s32[32,128]{1,0:T(8,128)S(1)} collective-permute-done((s32[32,128]{1,0:T(8,128)S(1)}, s32[32,128]{1,0:T(8,128)S(1)}, u32[]{:S(2)}, u32[]{:S(2)}) %collective-permute-start.1) | collective-permute-done | bytes 16416 | tf_op jit(solution)/shard_map/ppermute | solution.py:501
  47.7 4.0 %all-to-all-done.got = bf16[256,2,256]{2,1,0:T(2,128)(2,1)S(1)} async-done(((bf16[256,2,256]{2,1,0:T(2,128)(2,1)}), bf16[256,2,256]{2,1,0:T(2,128)(2,1)S(1)}, u32[]{:S(2)}, u32[]{:S(2)}) %all-to-all-start) | async-done | bytes 262176 | tf_op jit(solution)/shard_map/all_to_all | solution.py:446
  51.7 0.0 copy-start
  51.7 1.2 %shard_map.193 = (f32[32,4,128]{2,1,0:T(4,128)}, f32[8,256]{1,0:T(8,128)}) custom-call(bf16[256,2,256]{2,1,0:T(2,128)(2,1)S(1)} %all-to-all-done.got, bf16[256,256]{1,0:T(8,128)(2,1)S(1)} %dynamic-slice_bitcast_fusion.1.table, f32[64,128]{1,0:T(8,128)S(1)} %get-tuple-element.33.twist_cos, f32[64,128]{1,0:T(8,128)S(1)} %get-tuple-element.34.twist_sin), custom_call_target="tpu_custom_call" | custom-call | tf_op jit(solution)/shard_map/pallas_call | solution.py:510
  52.9 4.3 %all-to-all-start.1 = ((f32[32,4,128]{2,1,0:T(4,128)}), f32[32,4,128]{2,1,0:T(4,128)S(1)}, u32[]{:S(2)}, u32[]{:S(2)}) async-start(f32[32,4,128]{2,1,0:T(4,128)} %get-tuple-element.19), calls=%async_computation.1 | async-start | bytes 131072 | tf_op jit(solution)/shard_map/all_to_all | solution.py:446
  57.2 0.0 copy-start.3
  57.3 0.0 copy-start.4
  57.3 0.6 pad_add_fusion.bins
  57.9 0.0 copy-start.1
  57.9 0.0 copy-start.2
  57.9 1.6 %shard_map.194.weights = f32[64,128]{1,0:T(8,128)} custom-call(s32[64,128]{1,0:T(8,128)} %pad_add_fusion.bins, f32[8,128]{1,0:T(8,128)} %bitcast.18), custom_call_target="tpu_custom_call" | custom-call | tf_op jit(solution)/shard_map/pallas_call | solution.py:506
  59.5 5.2 %all-to-all-done.1.got = f32[32,4,128]{2,1,0:T(4,128)S(1)} async-done(((f32[32,4,128]{2,1,0:T(4,128)}), f32[32,4,128]{2,1,0:T(4,128)S(1)}, u32[]{:S(2)}, u32[]{:S(2)}) %all-to-all-start.1) | async-done | bytes 65568 | tf_op jit(solution)/shard_map/all_to_all | solution.py:446
  64.7 0.0 copy-done
  64.7 0.0 copy-done.3
  64.7 0.0 copy-done.4
  64.7 0.0 copy-done.1
  64.7 0.0 copy-done.2
  64.7 2.1 %shard_map.195 = f32[32,4,128]{2,1,0:T(4,128)} custom-call(f32[32,4,128]{2,1,0:T(4,128)S(1)} %all-to-all-done.1.got, f32[64,128]{1,0:T(8,128)} %shard_map.194.weights, bf16[64,192]{1,0:T(8,128)(2,1)S(1)} %copy-done.1, bf16[2,256,256]{2,1,0:T(8,128)(2,1)S(1)} %copy-done, bf16[64,192]{1,0:T(8,128)(2,1)S(1)} %copy-done.2, f32[32,128]{1,0:T(8,128)S(1)} %copy-done.3, ...), custom_call_target="tpu_custom_call" | custom-call | tf_op jit(solution)/shard_map/pallas_call | solution.py:512
  66.8 3.9 %all-to-all-start.2 = ((f32[32,4,128]{2,1,0:T(4,128)}), f32[32,4,128]{2,1,0:T(4,128)S(1)}, u32[]{:S(2)}, u32[]{:S(2)}) async-start(f32[32,4,128]{2,1,0:T(4,128)} %shard_map.195), calls=%async_computation.2 | async-start | bytes 131072 | tf_op jit(solution)/shard_map/all_to_all | solution.py:446
  70.7 0.0 copy-start.5
  70.7 1.0 dynamic-slice_bitcast_fusion.table
  71.7 6.5 %all-to-all-done.2.got = f32[32,4,128]{2,1,0:T(4,128)S(1)} async-done(((f32[32,4,128]{2,1,0:T(4,128)}), f32[32,4,128]{2,1,0:T(4,128)S(1)}, u32[]{:S(2)}, u32[]{:S(2)}) %all-to-all-start.2) | async-done | bytes 65568 | tf_op jit(solution)/shard_map/all_to_all | solution.py:446
  78.2 0.0 copy-done.5
  78.2 1.1 %shard_map.196 = bf16[256,2,256]{2,1,0:T(2,128)(2,1)} custom-call(f32[32,4,128]{2,1,0:T(4,128)S(1)} %all-to-all-done.2.got, f32[8,256]{1,0:T(8,128)S(1)} %copy-done.5, bf16[256,384]{1,0:T(8,128)(2,1)S(1)} %dynamic-slice_bitcast_fusion.table, f32[64,128]{1,0:T(8,128)S(1)} %get-tuple-element.30.twist_cos, f32[64,128]{1,0:T(8,128)S(1)} %get-tuple-element.29.twist_sin), custom_call_target="tpu_custom_call" | custom-call | tf_op jit(solution)/shard_map/pallas_call | solution.py:516
  79.3 22.3 %all_to_all.20.got = bf16[256,2,256]{2,1,0:T(2,128)(2,1)S(1)} all-to-all(bf16[256,2,256]{2,1,0:T(2,128)(2,1)} %shard_map.196), channel_id=1, replica_groups=mesh['rows'=8,'cols'=32] {'rows','cols'}, dimensions={0} | all-to-all | bytes 524288 | tf_op jit(solution)/shard_map/all_to_all | solution.py:446
  101.6 1.1 %shard_map.197 = (f32[3,4096]{1,0:T(4,128)}, f32[3,64,128]{2,1,0:T(8,128)}, f32[3,64,128]{2,1,0:T(8,128)}, f32[3,64,64]{2,1,0:T(8,128)}, f32[3,64]{1,0:T(4,128)}) custom-call(bf16[256,2,256]{2,1,0:T(2,128)(2,1)S(1)} %all_to_all.20.got), custom_call_target="tpu_custom_call" | custom-call | tf_op jit(solution)/shard_map/pallas_call | solution.py:519
  (5 shorter events, 0.0 us)
Async XLA Ops:
  2.2 5.0 %collective-permute-start = (bf16[96,768]{1,0:T(8,128)(2,1)}, bf16[96,768]{1,0:T(8,128)(2,1)S(1)}, u32[]{:S(2)}, u32[]{:S(2)}) collective-permute-start(bf16[96,768]{1,0:T(8,128)(2,1)} %shard_map.191), channel_id=1, source_target_pairs={{0,1},{1,2},{2,3},{3,4},{4,5},{5,6},{6,7},{7,8},{8,9},{9,10},{10,1... | collective-permute-start | bytes 442376 | tf_op jit(solution)/shard_map/ppermute | solution.py:462
  20.7 16.3 %copy-start.6 = (s32[4096,1,1]{0,2,1:T(1,128)S(1)}, s32[4096,1,1]{0,2,1:T(1,128)}, u32[]{:S(2)}) copy-start(s32[4096,1,1]{0,2,1:T(1,128)} %param.23) | copy-start | bytes 49156
  20.7 31.0 %all-to-all-start = ((bf16[256,2,256]{2,1,0:T(2,128)(2,1)}), bf16[256,2,256]{2,1,0:T(2,128)(2,1)S(1)}, u32[]{:S(2)}, u32[]{:S(2)}) async-start(bf16[256,2,256]{2,1,0:T(2,128)(2,1)} %shard_map.192), calls=%async_computation | async-start | bytes 524288 | tf_op jit(solution)/shard_map/all_to_all | solution.py:446
  37.8 9.9 %collective-permute-start.1 = (s32[32,128]{1,0:T(8,128)S(1)}, s32[32,128]{1,0:T(8,128)S(1)}, u32[]{:S(2)}, u32[]{:S(2)}) collective-permute-start(s32[32,128]{1,0:T(8,128)S(1)} %bitcast.15), channel_id=1, source_target_pairs={{0,128},{32,160},{64,192},{96,224},{128,0},{160,32},{192,64},{224,... | collective-permute-start | bytes 49160 | tf_op jit(solution)/shard_map/ppermute | solution.py:501
  44.1 0.7 copy-start.7
  51.7 13.0 %copy-start = (bf16[2,256,256]{2,1,0:T(8,128)(2,1)S(1)}, bf16[2,256,256]{2,1,0:T(8,128)(2,1)}, u32[]{:S(2)}) copy-start(bf16[2,256,256]{2,1,0:T(8,128)(2,1)} %constant.109.clone.fast) | copy-start | bytes 786436
  52.9 11.7 %all-to-all-start.1 = ((f32[32,4,128]{2,1,0:T(4,128)}), f32[32,4,128]{2,1,0:T(4,128)S(1)}, u32[]{:S(2)}, u32[]{:S(2)}) async-start(f32[32,4,128]{2,1,0:T(4,128)} %get-tuple-element.19), calls=%async_computation.1 | async-start | bytes 131072 | tf_op jit(solution)/shard_map/all_to_all | solution.py:446
  57.2 7.4 %copy-start.3 = (f32[32,128]{1,0:T(8,128)S(1)}, f32[32,128]{1,0:T(8,128)}, u32[]{:S(2)}) copy-start(f32[32,128]{1,0:T(8,128)} %constant.111.clone.turn_cos) | copy-start | bytes 49156
  57.3 7.4 %copy-start.4 = (f32[32,128]{1,0:T(8,128)S(1)}, f32[32,128]{1,0:T(8,128)}, u32[]{:S(2)}) copy-start(f32[32,128]{1,0:T(8,128)} %constant.112.clone.turn_sin) | copy-start | bytes 49156
  57.9 6.8 %copy-start.1 = (bf16[64,192]{1,0:T(8,128)(2,1)S(1)}, bf16[64,192]{1,0:T(8,128)(2,1)}, u32[]{:S(2)}) copy-start(bf16[64,192]{1,0:T(8,128)(2,1)} %constant.108.clone.outer) | copy-start | bytes 73732
  57.9 6.8 %copy-start.2 = (bf16[64,192]{1,0:T(8,128)(2,1)S(1)}, bf16[64,192]{1,0:T(8,128)(2,1)}, u32[]{:S(2)}) copy-start(bf16[64,192]{1,0:T(8,128)(2,1)} %constant.110.clone.outer_back) | copy-start | bytes 73732
  66.8 11.3 %all-to-all-start.2 = ((f32[32,4,128]{2,1,0:T(4,128)}), f32[32,4,128]{2,1,0:T(4,128)S(1)}, u32[]{:S(2)}, u32[]{:S(2)}) async-start(f32[32,4,128]{2,1,0:T(4,128)} %shard_map.195), calls=%async_computation.2 | async-start | bytes 131072 | tf_op jit(solution)/shard_map/all_to_all | solution.py:446
  70.7 7.4 %copy-start.5 = (f32[8,256]{1,0:T(8,128)S(1)}, f32[8,256]{1,0:T(8,128)}, u32[]{:S(2)}) copy-start(f32[8,256]{1,0:T(8,128)} %get-tuple-element.21.sums) | copy-start | bytes 24580

commit v6 on v5

--- a/solution.py
+++ b/solution.py
@@ -382,8 +382,7 @@
     if in_specs is None:
         in_specs = [pl.BlockSpec(memory_space=pltpu.SMEM)] * smem + [vmem] * n_in
     out_shape = [
-        out if isinstance(out, jax.ShapeDtypeStruct) else jax.ShapeDtypeStruct(out, F32)
-        for out in outs
+        jax.ShapeDtypeStruct(out, F32) if isinstance(out, tuple) else out for out in outs
     ]
     return pl.pallas_call(
         kernel,
@@ -453,7 +452,7 @@
     n = rows_count * cols_count
     total = n * SEG
     message, = call(
-        pack_kernel, [jax.ShapeDtypeStruct((96, SHIFT), BF16)], [pltpu.VMEM((32, SHIFT), F32)],
+        pack_kernel, [pltpu.VMEM((96, SHIFT), BF16)], [pltpu.VMEM((32, SHIFT), F32)],
         in_specs=[
             pl.BlockSpec((64, 1024), lambda i: (0, 3)), pl.BlockSpec((3, 2048), lambda i: (0, 1)),
         ],
@@ -473,7 +472,7 @@
         + [big(64, F32)] * 4
         + [pltpu.VMEM((3, 128, 128), F32), pltpu.VMEM((3, 64, 128), F32), pltpu.VMEM((32, 384), F32)]
     )
-    packed = jax.ShapeDtypeStruct((n, 2, 2 * LANES), BF16)
+    packed = pltpu.VMEM((n, 2, 2 * LANES), BF16)
     sent, = call(conv_kernel, [packed], scratch, smem=1, n_in=7)(
         dilations, received, whitened, cotangent, lift_weight.T, jnp.swapaxes(conv_now, 1, 2),
         jnp.swapaxes(conv_past, 1, 2), mix_weight,
@@ -503,14 +502,14 @@
         [jnp.where(second, other, bins), jnp.where(second, bins, other)], axis=0
     )
     psd = jnp.where(second, psd_weight[1], psd_weight[0]) * (1.0 / total)
-    weights = call(weight_kernel, [(2 * cols_count, LANES)], n_in=2)(bins, psd.reshape(8, LANES))[0]
+    weights = call(weight_kernel, [pltpu.VMEM((2 * cols_count, LANES), F32)], n_in=2)(bins, psd.reshape(8, LANES))[0]
 
     got = exchange(sent, BOTH)
-    pieces = (cols_count, 4, LANES)
-    sent, sums = call(first_kernel, [pieces, (8, 256)], n_in=4)(got, near(outward), near(twist_cos), near(twist_sin))
+    pieces = pltpu.VMEM((cols_count, 4, LANES), F32)
+    sent, sums = call(first_kernel, [pieces, pltpu.VMEM((8, 256), F32)], n_in=4)(got, near(outward), near(twist_cos), near(twist_sin))
     got = exchange(sent, "cols")
     sent, = call(middle_kernel, [pieces], n_in=7)(
-        got, weights, near(outer), near(fast), near(outer_back), near(turn_cos), near(turn_sin)
+        got, near(weights), near(outer), near(fast), near(outer_back), near(turn_cos), near(turn_sin)
     )
     got = exchange(sent, "cols")
     sent, = call(third_kernel, [packed], n_in=5)(got, near(sums), near(inward), near(back_cos), near(back_sin))

time: 103 us -> 101 us (0.981)
  Pallas kernels: 22.2 us -> 19.6 us
    pallas_call x3, Pallas kernels: 4.45 us -> 3.26 us  [the longest x1 1.31 us: local(): call(first_kernel, [pieces, pltpu.VMEM((8, 256), F32)], n_in=4)]
  transfers between devices with their start and end apart: 5 -> 5, of which waited for: 5 -> 5; matrix products, arithmetic and copies ran while one was open for 5% -> 5% of each run, Pallas kernels for 2% -> 1%
where the time goes in v6:
time: 101 us; the launch traced here: 100 us
  starting transfers between devices  33 us (33%)
  blocking collectives  22.1 us (22%)
  waiting for transfers between devices  19.8 us (20%)
  Pallas kernels  19.6 us (19%)
  local copies, waits for them, and re-layouts  2.87 us (3%)
  other arithmetic  2.29 us (2%)
    all_to_all x3, starting transfers between devices, exchange(): lax.all_to_all(x, axes, split_axis=0, concat_axis=0, tiled=True)  24.1 us
    all_to_all x1, blocking collectives, exchange(): lax.all_to_all(x, axes, split_axis=0, concat_axis=0, tiled=True)  22.1 us
    all_to_all x3, waiting for transfers between devices, exchange(): lax.all_to_all(x, axes, split_axis=0, concat_axis=0, tiled=True)  16.3 us
    pallas_call x1, Pallas kernels, local(): call(conv_kernel, [packed], scratch, smem=1, n_in=7)  13.4 us
    ppermute x1, starting transfers between devices, local(): lax.ppermute(bins, 'rows', [(i, (i + half) % rows_count) for i in range(r...  6.26 us
    ppermute x1, starting transfers between devices, local(): lax.ppermute(message, BOTH, [(i, (i + 1) % n) for i in range(n)])  2.67 us
    ppermute x1, waiting for transfers between devices, local(): lax.ppermute(message, BOTH, [(i, (i + 1) % n) for i in range(n)])  2.09 us
  transfers between devices with their start and end apart: 5, of which 5 were waited for; matrix products, arithmetic and copies ran while one was open for 5% of the time, Pallas kernels for 1%

profile of v6, /device:TPU:1, one launch (start us, length us, event | category | flops | bytes accessed | tf_op | source)
XLA Modules:
  0.0 100.3 jit_solution(7324943320397438475)
XLA Ops:
  0.6 0.9 shard_map.191
  1.6 2.7 %collective-permute-start = (bf16[96,768]{1,0:T(8,128)(2,1)S(1)}, bf16[96,768]{1,0:T(8,128)(2,1)S(1)}, u32[]{:S(2)}, u32[]{:S(2)}) collective-permute-start(bf16[96,768]{1,0:T(8,128)(2,1)S(1)} %shard_map.191), channel_id=1, source_target_pairs={{0,1},{1,2},{2,3},{3,4},{4,5},{5,6},{6,7},{7,8},{8,9},{9,10},{10,1... | collective-permute-start | bytes 442376 | tf_op jit(solution)/shard_map/ppermute | solution.py:461
  4.3 2.1 %collective-permute-done.got = bf16[96,768]{1,0:T(8,128)(2,1)S(1)} collective-permute-done((bf16[96,768]{1,0:T(8,128)(2,1)S(1)}, bf16[96,768]{1,0:T(8,128)(2,1)S(1)}, u32[]{:S(2)}, u32[]{:S(2)}) %collective-permute-start) | collective-permute-done | bytes 147488 | tf_op jit(solution)/shard_map/ppermute | solution.py:461
  6.4 13.4 %shard_map.192 = bf16[256,2,256]{2,1,0:T(2,128)(2,1)} custom-call(s32[3]{0:T(128)} %dil.1, bf16[96,768]{1,0:T(8,128)(2,1)S(1)} %collective-permute-done.got, f32[3,4096]{1,0:T(4,128)} %wh.3, bf16[64,4096]{1,0:T(8,128)(2,1)} %cot.3, f32[3,64]{1,0:T(4,128)} %bitcast.19, bf16[3,64,128]{2,1,0:T(8,128)(2,1)} %bitcast.16, bf16[3,64,128]{2,1,0:T(8,128)(2,1)} %bitcast.17, ...), custom_call_target="tpu_custom_call" | custom-call | tf_op jit(solution)/shard_map/pallas_call | solution.py:476
  19.8 0.0 copy-start.5
  19.8 15.9 %all-to-all-start = ((bf16[256,2,256]{2,1,0:T(2,128)(2,1)}), bf16[256,2,256]{2,1,0:T(2,128)(2,1)S(1)}, u32[]{:S(2)}, u32[]{:S(2)}) async-start(bf16[256,2,256]{2,1,0:T(2,128)(2,1)} %shard_map.192), calls=%async_computation | async-start | bytes 524288 | tf_op jit(solution)/shard_map/all_to_all | solution.py:445
  35.7 0.5 broadcast.110
  36.2 0.0 copy-done.5
  36.2 0.7 reduce.3
  36.9 0.1 reshape.20
  37.0 0.1 copy.21
  37.0 6.3 %collective-permute-start.1 = (s32[32,128]{1,0:T(8,128)S(1)}, s32[32,128]{1,0:T(8,128)S(1)}, u32[]{:S(2)}, u32[]{:S(2)}) collective-permute-start(s32[32,128]{1,0:T(8,128)S(1)} %bitcast.15), channel_id=1, source_target_pairs={{0,128},{32,160},{64,192},{96,224},{128,0},{160,32},{192,64},{224,... | collective-permute-start | bytes 49160 | tf_op jit(solution)/shard_map/ppermute | solution.py:500
  43.3 0.0 copy-start.6
  43.3 0.4 fusion.6
  43.7 0.3 copy-done.6
  44.0 0.6 fusion.10
  44.6 0.9 dynamic-slice_bitcast_fusion.1.table
  45.5 1.4 %collective-permute-done.1 = s32[32,128]{1,0:T(8,128)S(1)} collective-permute-done((s32[32,128]{1,0:T(8,128)S(1)}, s32[32,128]{1,0:T(8,128)S(1)}, u32[]{:S(2)}, u32[]{:S(2)}) %collective-permute-start.1) | collective-permute-done | bytes 16416 | tf_op jit(solution)/shard_map/ppermute | solution.py:500
  46.9 4.0 %all-to-all-done.got = bf16[256,2,256]{2,1,0:T(2,128)(2,1)S(1)} async-done(((bf16[256,2,256]{2,1,0:T(2,128)(2,1)}), bf16[256,2,256]{2,1,0:T(2,128)(2,1)S(1)}, u32[]{:S(2)}, u32[]{:S(2)}) %all-to-all-start) | async-done | bytes 262176 | tf_op jit(solution)/shard_map/all_to_all | solution.py:445
  50.9 0.0 copy-start
  50.9 1.3 %shard_map.193 = (f32[32,4,128]{2,1,0:T(4,128)}, f32[8,256]{1,0:T(8,128)S(1)}) custom-call(bf16[256,2,256]{2,1,0:T(2,128)(2,1)S(1)} %all-to-all-done.got, bf16[256,256]{1,0:T(8,128)(2,1)S(1)} %dynamic-slice_bitcast_fusion.1.table, f32[64,128]{1,0:T(8,128)S(1)} %get-tuple-element.33.twist_cos, f32[64,128]{1,0:T(8,128)S(1)} %get-tuple-element.34.twist_sin), custom_call_target="tpu_custom_call" | custom-call | tf_op jit(solution)/shard_map/pallas_call | solution.py:509
  52.2 4.3 %all-to-all-start.1 = ((f32[32,4,128]{2,1,0:T(4,128)}), f32[32,4,128]{2,1,0:T(4,128)S(1)}, u32[]{:S(2)}, u32[]{:S(2)}) async-start(f32[32,4,128]{2,1,0:T(4,128)} %get-tuple-element.19), calls=%async_computation.1 | async-start | bytes 131072 | tf_op jit(solution)/shard_map/all_to_all | solution.py:445
  56.5 0.0 copy-start.3
  56.6 0.0 copy-start.4
  56.6 0.6 pad_add_fusion.bins
  57.2 0.0 copy-start.1
  57.2 0.0 copy-start.2
  57.2 1.0 shard_map.194.weights
  58.2 5.8 %all-to-all-done.1.got = f32[32,4,128]{2,1,0:T(4,128)S(1)} async-done(((f32[32,4,128]{2,1,0:T(4,128)}), f32[32,4,128]{2,1,0:T(4,128)S(1)}, u32[]{:S(2)}, u32[]{:S(2)}) %all-to-all-start.1) | async-done | bytes 65568 | tf_op jit(solution)/shard_map/all_to_all | solution.py:445
  64.0 0.0 copy-done
  64.0 0.0 copy-done.3
  64.0 0.0 copy-done.4
  64.0 0.0 copy-done.1
  64.0 0.0 copy-done.2
  64.0 1.3 %shard_map.195 = f32[32,4,128]{2,1,0:T(4,128)} custom-call(f32[32,4,128]{2,1,0:T(4,128)S(1)} %all-to-all-done.1.got, f32[64,128]{1,0:T(8,128)S(1)} %shard_map.194.weights, bf16[64,192]{1,0:T(8,128)(2,1)S(1)} %copy-done.1, bf16[2,256,256]{2,1,0:T(8,128)(2,1)S(1)} %copy-done, bf16[64,192]{1,0:T(8,128)(2,1)S(1)} %copy-done.2, f32[32,128]{1,0:T(8,128)S(1)} %copy-done.3, ...), custom_call_target="tpu_custom_call" | custom-call | tf_op jit(solution)/shard_map/pallas_call | solution.py:511
  65.4 3.9 %all-to-all-start.2 = ((f32[32,4,128]{2,1,0:T(4,128)}), f32[32,4,128]{2,1,0:T(4,128)S(1)}, u32[]{:S(2)}, u32[]{:S(2)}) async-start(f32[32,4,128]{2,1,0:T(4,128)} %shard_map.195), calls=%async_computation.2 | async-start | bytes 131072 | tf_op jit(solution)/shard_map/all_to_all | solution.py:445
  69.3 1.0 dynamic-slice_bitcast_fusion.table
  70.2 6.5 %all-to-all-done.2.got = f32[32,4,128]{2,1,0:T(4,128)S(1)} async-done(((f32[32,4,128]{2,1,0:T(4,128)}), f32[32,4,128]{2,1,0:T(4,128)S(1)}, u32[]{:S(2)}, u32[]{:S(2)}) %all-to-all-start.2) | async-done | bytes 65568 | tf_op jit(solution)/shard_map/all_to_all | solution.py:445
  76.7 0.4 shard_map.196
  77.1 22.1 %all_to_all.20.got = bf16[256,2,256]{2,1,0:T(2,128)(2,1)S(1)} all-to-all(bf16[256,2,256]{2,1,0:T(2,128)(2,1)S(1)} %shard_map.196), channel_id=1, replica_groups=mesh['rows'=8,'cols'=32] {'rows','cols'}, dimensions={0} | all-to-all | bytes 524288 | tf_op jit(solution)/shard_map/all_to_all | solution.py:445
  99.2 1.1 %shard_map.197 = (f32[3,4096]{1,0:T(4,128)}, f32[3,64,128]{2,1,0:T(8,128)}, f32[3,64,128]{2,1,0:T(8,128)}, f32[3,64,64]{2,1,0:T(8,128)}, f32[3,64]{1,0:T(4,128)}) custom-call(bf16[256,2,256]{2,1,0:T(2,128)(2,1)S(1)} %all_to_all.20.got), custom_call_target="tpu_custom_call" | custom-call | tf_op jit(solution)/shard_map/pallas_call | solution.py:518
  (5 shorter events, 0.0 us)
Async XLA Ops:
  1.6 4.8 %collective-permute-start = (bf16[96,768]{1,0:T(8,128)(2,1)S(1)}, bf16[96,768]{1,0:T(8,128)(2,1)S(1)}, u32[]{:S(2)}, u32[]{:S(2)}) collective-permute-start(bf16[96,768]{1,0:T(8,128)(2,1)S(1)} %shard_map.191), channel_id=1, source_target_pairs={{0,1},{1,2},{2,3},{3,4},{4,5},{5,6},{6,7},{7,8},{8,9},{9,10},{10,1... | collective-permute-start | bytes 442376 | tf_op jit(solution)/shard_map/ppermute | solution.py:461
  19.8 16.4 %copy-start.5 = (s32[4096,1,1]{0,2,1:T(1,128)S(1)}, s32[4096,1,1]{0,2,1:T(1,128)}, u32[]{:S(2)}) copy-start(s32[4096,1,1]{0,2,1:T(1,128)} %param.23) | copy-start | bytes 49156
  19.8 31.1 %all-to-all-start = ((bf16[256,2,256]{2,1,0:T(2,128)(2,1)}), bf16[256,2,256]{2,1,0:T(2,128)(2,1)S(1)}, u32[]{:S(2)}, u32[]{:S(2)}) async-start(bf16[256,2,256]{2,1,0:T(2,128)(2,1)} %shard_map.192), calls=%async_computation | async-start | bytes 524288 | tf_op jit(solution)/shard_map/all_to_all | solution.py:445
  37.0 9.9 %collective-permute-start.1 = (s32[32,128]{1,0:T(8,128)S(1)}, s32[32,128]{1,0:T(8,128)S(1)}, u32[]{:S(2)}, u32[]{:S(2)}) collective-permute-start(s32[32,128]{1,0:T(8,128)S(1)} %bitcast.15), channel_id=1, source_target_pairs={{0,128},{32,160},{64,192},{96,224},{128,0},{160,32},{192,64},{224,... | collective-permute-start | bytes 49160 | tf_op jit(solution)/shard_map/ppermute | solution.py:500
  43.3 0.7 copy-start.6
  50.9 13.0 %copy-start = (bf16[2,256,256]{2,1,0:T(8,128)(2,1)S(1)}, bf16[2,256,256]{2,1,0:T(8,128)(2,1)}, u32[]{:S(2)}) copy-start(bf16[2,256,256]{2,1,0:T(8,128)(2,1)} %constant.109.clone.fast) | copy-start | bytes 786436
  52.2 11.7 %all-to-all-start.1 = ((f32[32,4,128]{2,1,0:T(4,128)}), f32[32,4,128]{2,1,0:T(4,128)S(1)}, u32[]{:S(2)}, u32[]{:S(2)}) async-start(f32[32,4,128]{2,1,0:T(4,128)} %get-tuple-element.19), calls=%async_computation.1 | async-start | bytes 131072 | tf_op jit(solution)/shard_map/all_to_all | solution.py:445
  56.5 7.4 %copy-start.3 = (f32[32,128]{1,0:T(8,128)S(1)}, f32[32,128]{1,0:T(8,128)}, u32[]{:S(2)}) copy-start(f32[32,128]{1,0:T(8,128)} %constant.111.clone.turn_cos) | copy-start | bytes 49156
  56.6 7.4 %copy-start.4 = (f32[32,128]{1,0:T(8,128)S(1)}, f32[32,128]{1,0:T(8,128)}, u32[]{:S(2)}) copy-start(f32[32,128]{1,0:T(8,128)} %constant.112.clone.turn_sin) | copy-start | bytes 49156
  57.2 6.8 %copy-start.1 = (bf16[64,192]{1,0:T(8,128)(2,1)S(1)}, bf16[64,192]{1,0:T(8,128)(2,1)}, u32[]{:S(2)}) copy-start(bf16[64,192]{1,0:T(8,128)(2,1)} %constant.108.clone.outer) | copy-start | bytes 73732
  57.2 6.8 %copy-start.2 = (bf16[64,192]{1,0:T(8,128)(2,1)S(1)}, bf16[64,192]{1,0:T(8,128)(2,1)}, u32[]{:S(2)}) copy-start(bf16[64,192]{1,0:T(8,128)(2,1)} %constant.110.clone.outer_back) | copy-start | bytes 73732
  65.4 11.3 %all-to-all-start.2 = ((f32[32,4,128]{2,1,0:T(4,128)}), f32[32,4,128]{2,1,0:T(4,128)S(1)}, u32[]{:S(2)}, u32[]{:S(2)}) async-start(f32[32,4,128]{2,1,0:T(4,128)} %shard_map.195), calls=%async_computation.2 | async-start | bytes 131072 | tf_op jit(solution)/shard_map/all_to_all | solution.py:445

commit v7 on v6

--- a/solution.py
+++ b/solution.py
@@ -232,8 +232,8 @@
     lax.fori_loop(0, SEG // STEP, step1, 0)
     saved_layer(0, x1, fl1, sg1, gt1, ah2, dp2, ah, dp, BASE + SEG, 256, False)
 
-    g_lift = jnp.zeros((8, LANES), F32)
-    blank = jnp.zeros((64, 256), BF16)
+    on_high_sum = jnp.zeros((64, 16), F32)
+    on_low_sum = jnp.zeros((64, 16), F32)
     for m in range(16):
         start = BASE + m * 256
         dfield = dp[:, start : start + 256] + beyond(ah, start, 256, 0)
@@ -249,11 +249,13 @@
         seen = whu[:, LEFT + m * 256 : LEFT + (m + 1) * 256]
         seen_high = seen.astype(BF16).astype(F32)
         seen_16 = jnp.concatenate([seen_high, seen - seen_high], axis=0).astype(BF16)
-        on_high = dot_nt(seen_16, jnp.concatenate([blank, high], axis=0))
-        g_lift += (
-            on_high[0:8] + on_high[8:16]
-            + dot_nt(seen_16, jnp.concatenate([blank, low], axis=0))[0:8]
-        )
+        on_high_sum += dot_nt(high, seen_16)
+        on_low_sum += dot_nt(low, seen_16)
+    square[...] = jnp.zeros_like(square)
+    square[64:128, 0:16] = on_high_sum
+    square[64:128, 16:32] = on_low_sum
+    g_lift = square[...].T
+    g_lift = g_lift[0:8] + g_lift[8:16] + g_lift[16:24]
 
     pair = x_t[:, 0:256].astype(BF16)
     single = jnp.concatenate([x_t[:, 256:384], jnp.zeros((32, LANES), F32)], axis=1).astype(BF16)
@@ -283,9 +285,8 @@
 
 
 def first_kernel(got, table, twist_cos, twist_sin, sent, sums):
-    grads = jnp.sum(got[:, 1, :].astype(F32), axis=0, keepdims=True)
-    sums[...] = jnp.broadcast_to(grads, (8, 256))
-    both = dot32(table[...], got[:, 0, :])
+    both = dot32(table[...], got[...].reshape(512, 256))
+    sums[...] = both[256:264]
     both = both[0:128] + both[128:256]
     real = both[0:64, 0:LANES] + both[64:128, LANES:]
     imag = both[0:64, LANES:] - both[64:128, 0:LANES]
@@ -416,6 +417,9 @@
     outward = np.concatenate([np.cos(angle), np.sin(angle)], axis=1)
     inward = np.swapaxes(np.concatenate([np.cos(angle), -np.sin(angle)], axis=1), 1, 2)
     outward = np.concatenate(two_parts(outward), axis=1)
+    spread = np.zeros((half, 272, 2 * n), outward.dtype)
+    spread[:, 0:256, 0::2] = outward
+    spread[:, 256:264, 1::2] = 1
     inward = for_left(inward)
 
     def mixing(product, size, sign):
@@ -432,7 +436,7 @@
     fast = np.stack(two_parts(mixing(l[:, None] * l[None, :], LANES, -1.0)))
     angle = 2.0 * np.pi / SEG * (c[:, None] * l[None, :])
     return (
-        outward, inward, outer, outer_back, fast,
+        spread, inward, outer, outer_back, fast,
         np.cos(angle).astype(np.float32), np.sin(angle).astype(np.float32),
     )
 
@@ -478,9 +482,8 @@
         jnp.swapaxes(conv_past, 1, 2), mix_weight,
     )
     outward, inward, outer, outer_back, fast, turn_cos, turn_sin = tables(rows_count, cols_count)
-    my_row, my_col, psd_bin, sent = lax.optimization_barrier(
-        (lax.axis_index("rows"), lax.axis_index("cols"), psd_bin, sent)
-    )
+    my_row, my_col = lax.axis_index("rows"), lax.axis_index("cols")
+    psd_bin, sent = lax.optimization_barrier((psd_bin, sent))
     half = rows_count // 2
     my_low, second = my_row % half, my_row >= half
     outward = lax.dynamic_index_in_dim(jnp.asarray(outward), my_low, 0, keepdims=False)

time: 101 us -> 101 us (level)
  no operation moved by 1% of the time
where the time goes in v7:
time: 101 us; the launch traced here: 100 us
  starting transfers between devices  33 us (33%)
  blocking collectives  22.5 us (22%)
  waiting for transfers between devices  20 us (20%)
  Pallas kernels  19.1 us (19%)
  local copies, waits for them, and re-layouts  2.61 us (3%)
  other arithmetic  2.3 us (2%)
    all_to_all x3, starting transfers between devices, exchange(): lax.all_to_all(x, axes, split_axis=0, concat_axis=0, tiled=True)  24.1 us
    all_to_all x1, blocking collectives, exchange(): lax.all_to_all(x, axes, split_axis=0, concat_axis=0, tiled=True)  22.5 us
    all_to_all x3, waiting for transfers between devices, exchange(): lax.all_to_all(x, axes, split_axis=0, concat_axis=0, tiled=True)  16.3 us
    pallas_call x1, Pallas kernels, local(): call(conv_kernel, [packed], scratch, smem=1, n_in=7)  13.3 us
    ppermute x1, starting transfers between devices, local(): lax.ppermute(bins, 'rows', [(i, (i + half) % rows_count) for i in range(r...  6.26 us
    ppermute x1, starting transfers between devices, local(): lax.ppermute(message, BOTH, [(i, (i + 1) % n) for i in range(n)])  2.67 us
    ppermute x1, waiting for transfers between devices, local(): lax.ppermute(bins, 'rows', [(i, (i + half) % rows_count) for i in range(r...  2.04 us
  transfers between devices with their start and end apart: 5, of which 5 were waited for; matrix products, arithmetic and copies ran while one was open for 5% of the time, Pallas kernels for 1%

profile of v7, /device:TPU:1, one launch (start us, length us, event | category | flops | bytes accessed | tf_op | source)
XLA Modules:
  0.0 100.3 jit_solution(14731705613398460435)
XLA Ops:
  0.6 0.9 shard_map.191
  1.6 0.0 copy-start.6
  1.6 0.0 copy-start.5
  1.6 2.7 %collective-permute-start = (bf16[96,768]{1,0:T(8,128)(2,1)S(1)}, bf16[96,768]{1,0:T(8,128)(2,1)S(1)}, u32[]{:S(2)}, u32[]{:S(2)}) collective-permute-start(bf16[96,768]{1,0:T(8,128)(2,1)S(1)} %shard_map.191), channel_id=1, source_target_pairs={{0,1},{1,2},{2,3},{3,4},{4,5},{5,6},{6,7},{7,8},{8,9},{9,10},{10,1... | collective-permute-start | bytes 442376 | tf_op jit(solution)/shard_map/ppermute | solution.py:465
  4.3 0.4 fusion.6
  4.7 1.7 %collective-permute-done.got = bf16[96,768]{1,0:T(8,128)(2,1)S(1)} collective-permute-done((bf16[96,768]{1,0:T(8,128)(2,1)S(1)}, bf16[96,768]{1,0:T(8,128)(2,1)S(1)}, u32[]{:S(2)}, u32[]{:S(2)}) %collective-permute-start) | collective-permute-done | bytes 147488 | tf_op jit(solution)/shard_map/ppermute | solution.py:465
  6.4 13.3 %shard_map.192 = bf16[256,2,256]{2,1,0:T(2,128)(2,1)} custom-call(s32[3]{0:T(128)} %dil.1, bf16[96,768]{1,0:T(8,128)(2,1)S(1)} %collective-permute-done.got, f32[3,4096]{1,0:T(4,128)} %wh.3, bf16[64,4096]{1,0:T(8,128)(2,1)} %cot.3, f32[3,64]{1,0:T(4,128)} %bitcast.19, bf16[3,64,128]{2,1,0:T(8,128)(2,1)} %bitcast.16, bf16[3,64,128]{2,1,0:T(8,128)(2,1)} %bitcast.17, ...), custom_call_target="tpu_custom_call" | custom-call | tf_op jit(solution)/shard_map/pallas_call | solution.py:480
  19.7 0.0 copy-start
  19.7 0.0 copy-start.1
  19.7 0.0 copy-start.2
  19.7 0.0 copy-start.3
  19.7 0.0 copy-start.4
  19.7 15.9 %all-to-all-start = ((bf16[256,2,256]{2,1,0:T(2,128)(2,1)}), bf16[256,2,256]{2,1,0:T(2,128)(2,1)S(1)}, u32[]{:S(2)}, u32[]{:S(2)}) async-start(bf16[256,2,256]{2,1,0:T(2,128)(2,1)} %shard_map.192), calls=%async_computation | async-start | bytes 524288 | tf_op jit(solution)/shard_map/all_to_all | solution.py:449
  35.6 0.0 copy-done.6
  35.6 0.6 fusion.10
  36.2 0.5 broadcast.110
  36.7 0.0 copy-done.5
  36.7 0.7 reduce.3
  37.4 0.1 reshape.20
  37.5 0.1 copy.21
  37.5 6.3 %collective-permute-start.1 = (s32[32,128]{1,0:T(8,128)S(1)}, s32[32,128]{1,0:T(8,128)S(1)}, u32[]{:S(2)}, u32[]{:S(2)}) collective-permute-start(s32[32,128]{1,0:T(8,128)S(1)} %bitcast.15), channel_id=1, source_target_pairs={{0,128},{32,160},{64,192},{96,224},{128,0},{160,32},{192,64},{224,... | collective-permute-start | bytes 49160 | tf_op jit(solution)/shard_map/ppermute | solution.py:503
  43.8 1.0 dynamic-slice_bitcast_fusion.table
  44.8 2.0 %collective-permute-done.1 = s32[32,128]{1,0:T(8,128)S(1)} collective-permute-done((s32[32,128]{1,0:T(8,128)S(1)}, s32[32,128]{1,0:T(8,128)S(1)}, u32[]{:S(2)}, u32[]{:S(2)}) %collective-permute-start.1) | collective-permute-done | bytes 16416 | tf_op jit(solution)/shard_map/ppermute | solution.py:503
  46.8 4.0 %all-to-all-done.got = bf16[256,2,256]{2,1,0:T(2,128)(2,1)S(1)} async-done(((bf16[256,2,256]{2,1,0:T(2,128)(2,1)}), bf16[256,2,256]{2,1,0:T(2,128)(2,1)S(1)}, u32[]{:S(2)}, u32[]{:S(2)}) %all-to-all-start) | async-done | bytes 262176 | tf_op jit(solution)/shard_map/all_to_all | solution.py:449
  50.8 0.9 shard_map.193
  51.8 4.3 %all-to-all-start.1 = ((f32[32,4,128]{2,1,0:T(4,128)}), f32[32,4,128]{2,1,0:T(4,128)S(1)}, u32[]{:S(2)}, u32[]{:S(2)}) async-start(f32[32,4,128]{2,1,0:T(4,128)} %get-tuple-element.15), calls=%async_computation.1 | async-start | bytes 131072 | tf_op jit(solution)/shard_map/all_to_all | solution.py:449
  56.1 0.6 pad_add_fusion.bins
  56.7 1.0 shard_map.194.weights
  57.7 5.8 %all-to-all-done.1.got = f32[32,4,128]{2,1,0:T(4,128)S(1)} async-done(((f32[32,4,128]{2,1,0:T(4,128)}), f32[32,4,128]{2,1,0:T(4,128)S(1)}, u32[]{:S(2)}, u32[]{:S(2)}) %all-to-all-start.1) | async-done | bytes 65568 | tf_op jit(solution)/shard_map/all_to_all | solution.py:449
  63.5 0.0 copy-done
  63.5 0.0 copy-done.1
  63.5 0.0 copy-done.2
  63.5 0.0 copy-done.3
  63.5 0.0 copy-done.4
  63.6 1.3 %shard_map.195 = f32[32,4,128]{2,1,0:T(4,128)} custom-call(f32[32,4,128]{2,1,0:T(4,128)S(1)} %all-to-all-done.1.got, f32[64,128]{1,0:T(8,128)S(1)} %shard_map.194.weights, bf16[64,192]{1,0:T(8,128)(2,1)S(1)} %copy-done.1, bf16[2,256,256]{2,1,0:T(8,128)(2,1)S(1)} %copy-done, bf16[64,192]{1,0:T(8,128)(2,1)S(1)} %copy-done.2, f32[32,128]{1,0:T(8,128)S(1)} %copy-done.3, ...), custom_call_target="tpu_custom_call" | custom-call | tf_op jit(solution)/shard_map/pallas_call | solution.py:514
  64.9 3.9 %all-to-all-start.2 = ((f32[32,4,128]{2,1,0:T(4,128)}), f32[32,4,128]{2,1,0:T(4,128)S(1)}, u32[]{:S(2)}, u32[]{:S(2)}) async-start(f32[32,4,128]{2,1,0:T(4,128)} %shard_map.195), calls=%async_computation.2 | async-start | bytes 131072 | tf_op jit(solution)/shard_map/all_to_all | solution.py:449
  68.8 1.0 dynamic-slice_bitcast_fusion.1.table
  69.8 6.5 %all-to-all-done.2.got = f32[32,4,128]{2,1,0:T(4,128)S(1)} async-done(((f32[32,4,128]{2,1,0:T(4,128)}), f32[32,4,128]{2,1,0:T(4,128)S(1)}, u32[]{:S(2)}, u32[]{:S(2)}) %all-to-all-start.2) | async-done | bytes 65568 | tf_op jit(solution)/shard_map/all_to_all | solution.py:449
  76.2 0.4 shard_map.196
  76.7 22.5 %all_to_all.20.got = bf16[256,2,256]{2,1,0:T(2,128)(2,1)S(1)} all-to-all(bf16[256,2,256]{2,1,0:T(2,128)(2,1)S(1)} %shard_map.196), channel_id=1, replica_groups=mesh['rows'=8,'cols'=32] {'rows','cols'}, dimensions={0} | all-to-all | bytes 524288 | tf_op jit(solution)/shard_map/all_to_all | solution.py:449
  99.2 1.1 %shard_map.197 = (f32[3,4096]{1,0:T(4,128)}, f32[3,64,128]{2,1,0:T(8,128)}, f32[3,64,128]{2,1,0:T(8,128)}, f32[3,64,64]{2,1,0:T(8,128)}, f32[3,64]{1,0:T(4,128)}) custom-call(bf16[256,2,256]{2,1,0:T(2,128)(2,1)S(1)} %all_to_all.20.got), custom_call_target="tpu_custom_call" | custom-call | tf_op jit(solution)/shard_map/pallas_call | solution.py:521
  (5 shorter events, 0.0 us)
Async XLA Ops:
  1.6 34.0 %copy-start.6 = (f32[2,1024]{1,0:T(2,128)S(1)}, f32[2,1024]{1,0:T(2,128)}, u32[]{:S(2)}) copy-start(f32[2,1024]{1,0:T(2,128)} %param.24) | copy-start | bytes 24580
  1.6 35.1 %copy-start.5 = (s32[4096,1,1]{0,2,1:T(1,128)S(1)}, s32[4096,1,1]{0,2,1:T(1,128)}, u32[]{:S(2)}) copy-start(s32[4096,1,1]{0,2,1:T(1,128)} %param.23) | copy-start | bytes 49156
  1.6 4.8 %collective-permute-start = (bf16[96,768]{1,0:T(8,128)(2,1)S(1)}, bf16[96,768]{1,0:T(8,128)(2,1)S(1)}, u32[]{:S(2)}, u32[]{:S(2)}) collective-permute-start(bf16[96,768]{1,0:T(8,128)(2,1)S(1)} %shard_map.191), channel_id=1, source_target_pairs={{0,1},{1,2},{2,3},{3,4},{4,5},{5,6},{6,7},{7,8},{8,9},{9,10},{10,1... | collective-permute-start | bytes 442376 | tf_op jit(solution)/shard_map/ppermute | solution.py:465
  19.7 43.8 %copy-start = (bf16[2,256,256]{2,1,0:T(8,128)(2,1)S(1)}, bf16[2,256,256]{2,1,0:T(8,128)(2,1)}, u32[]{:S(2)}) copy-start(bf16[2,256,256]{2,1,0:T(8,128)(2,1)} %constant.109.clone.fast) | copy-start | bytes 786436
  19.7 43.8 %copy-start.1 = (bf16[64,192]{1,0:T(8,128)(2,1)S(1)}, bf16[64,192]{1,0:T(8,128)(2,1)}, u32[]{:S(2)}) copy-start(bf16[64,192]{1,0:T(8,128)(2,1)} %constant.108.clone.outer) | copy-start | bytes 73732
  19.7 43.8 %copy-start.2 = (bf16[64,192]{1,0:T(8,128)(2,1)S(1)}, bf16[64,192]{1,0:T(8,128)(2,1)}, u32[]{:S(2)}) copy-start(bf16[64,192]{1,0:T(8,128)(2,1)} %constant.110.clone.outer_back) | copy-start | bytes 73732
  19.7 43.8 %copy-start.3 = (f32[32,128]{1,0:T(8,128)S(1)}, f32[32,128]{1,0:T(8,128)}, u32[]{:S(2)}) copy-start(f32[32,128]{1,0:T(8,128)} %constant.111.clone.turn_cos) | copy-start | bytes 49156
  19.7 43.8 %copy-start.4 = (f32[32,128]{1,0:T(8,128)S(1)}, f32[32,128]{1,0:T(8,128)}, u32[]{:S(2)}) copy-start(f32[32,128]{1,0:T(8,128)} %constant.112.clone.turn_sin) | copy-start | bytes 49156
  19.7 31.1 %all-to-all-start = ((bf16[256,2,256]{2,1,0:T(2,128)(2,1)}), bf16[256,2,256]{2,1,0:T(2,128)(2,1)S(1)}, u32[]{:S(2)}, u32[]{:S(2)}) async-start(bf16[256,2,256]{2,1,0:T(2,128)(2,1)} %shard_map.192), calls=%async_computation | async-start | bytes 524288 | tf_op jit(solution)/shard_map/all_to_all | solution.py:449
  37.5 9.3 %collective-permute-start.1 = (s32[32,128]{1,0:T(8,128)S(1)}, s32[32,128]{1,0:T(8,128)S(1)}, u32[]{:S(2)}, u32[]{:S(2)}) collective-permute-start(s32[32,128]{1,0:T(8,128)S(1)} %bitcast.15), channel_id=1, source_target_pairs={{0,128},{32,160},{64,192},{96,224},{128,0},{160,32},{192,64},{224,... | collective-permute-start | bytes 49160 | tf_op jit(solution)/shard_map/ppermute | solution.py:503
  51.8 11.7 %all-to-all-start.1 = ((f32[32,4,128]{2,1,0:T(4,128)}), f32[32,4,128]{2,1,0:T(4,128)S(1)}, u32[]{:S(2)}, u32[]{:S(2)}) async-start(f32[32,4,128]{2,1,0:T(4,128)} %get-tuple-element.15), calls=%async_computation.1 | async-start | bytes 131072 | tf_op jit(solution)/shard_map/all_to_all | solution.py:449
  64.9 11.3 %all-to-all-start.2 = ((f32[32,4,128]{2,1,0:T(4,128)}), f32[32,4,128]{2,1,0:T(4,128)S(1)}, u32[]{:S(2)}, u32[]{:S(2)}) async-start(f32[32,4,128]{2,1,0:T(4,128)} %shard_map.195), calls=%async_computation.2 | async-start | bytes 131072 | tf_op jit(solution)/shard_map/all_to_all | solution.py:449

commit v8 on v7

--- a/solution.py
+++ b/solution.py
@@ -501,15 +501,15 @@
 
     bins = psd_bin.reshape(LANES, cols_count).T
     other = lax.ppermute(bins, "rows", [(i, (i + half) % rows_count) for i in range(rows_count)])
-    bins = jnp.concatenate(
-        [jnp.where(second, other, bins), jnp.where(second, bins, other)], axis=0
-    )
-    psd = jnp.where(second, psd_weight[1], psd_weight[0]) * (1.0 / total)
-    weights = call(weight_kernel, [pltpu.VMEM((2 * cols_count, LANES), F32)], n_in=2)(bins, psd.reshape(8, LANES))[0]
-
     got = exchange(sent, BOTH)
     pieces = pltpu.VMEM((cols_count, 4, LANES), F32)
     sent, sums = call(first_kernel, [pieces, pltpu.VMEM((8, 256), F32)], n_in=4)(got, near(outward), near(twist_cos), near(twist_sin))
+    second, sent = lax.optimization_barrier((second, sent))
+    bins = jnp.concatenate(
+        [jnp.where(second, other, bins), jnp.where(second, bins, other)], axis=0
+    )
+    psd = jnp.where(second, psd_weight[1], psd_weight[0]) * (1.0 / total)
+    weights = call(weight_kernel, [pltpu.VMEM((2 * cols_count, LANES), F32)], n_in=2)(bins, psd.reshape(8, LANES))[0]
     got = exchange(sent, "cols")
     sent, = call(middle_kernel, [pieces], n_in=7)(
         got, near(weights), near(outer), near(fast), near(outer_back), near(turn_cos), near(turn_sin)

time: 101 us -> 98.7 us (0.977)
  blocking collectives: 22.5 us -> 20.5 us
    all_to_all x1, blocking collectives: 22.5 us -> 20.5 us  [exchange(): lax.all_to_all(x, axes, split_axis=0, concat_axis=0, tiled=True)]
    ppermute x1, waiting for transfers between devices: 2.04 us -> 0.01 us  [local(): lax.ppermute(bins, 'rows', [(i, (i + half) % rows_count) for i in range(r...]
    all_to_all x3, waiting for transfers between devices: 16.3 us -> 17.9 us  [exchange(): lax.all_to_all(x, axes, split_axis=0, concat_axis=0, tiled=True)]
  transfers between devices with their start and end apart: 5 -> 5, of which waited for: 5 -> 4; matrix products, arithmetic and copies ran while one was open for 5% -> 5% of each run, Pallas kernels for 1% -> 2%
where the time goes in v8:
time: 98.7 us; the launch traced here: 98.3 us
  starting transfers between devices  33 us (33%)
  blocking collectives  20.5 us (21%)
  waiting for transfers between devices  20 us (20%)
  Pallas kernels  19.1 us (19%)
  local copies, waits for them, and re-layouts  2.62 us (3%)
  other arithmetic  2.3 us (2%)
    all_to_all x3, starting transfers between devices, exchange(): lax.all_to_all(x, axes, split_axis=0, concat_axis=0, tiled=True)  24 us
    all_to_all x1, blocking collectives, exchange(): lax.all_to_all(x, axes, split_axis=0, concat_axis=0, tiled=True)  20.5 us
    all_to_all x3, waiting for transfers between devices, exchange(): lax.all_to_all(x, axes, split_axis=0, concat_axis=0, tiled=True)  17.9 us
    pallas_call x1, Pallas kernels, local(): call(conv_kernel, [packed], scratch, smem=1, n_in=7)  13.3 us
    ppermute x1, starting transfers between devices, local(): lax.ppermute(bins, 'rows', [(i, (i + half) % rows_count) for i in range(r...  6.26 us
    ppermute x1, starting transfers between devices, local(): lax.ppermute(message, BOTH, [(i, (i + 1) % n) for i in range(n)])  2.67 us
    ppermute x1, waiting for transfers between devices, local(): lax.ppermute(message, BOTH, [(i, (i + 1) % n) for i in range(n)])  2.09 us
  transfers between devices with their start and end apart: 5, of which 4 were waited for; matrix products, arithmetic and copies ran while one was open for 5% of the time, Pallas kernels for 2%

profile of v8, /device:TPU:1, one launch (start us, length us, event | category | flops | bytes accessed | tf_op | source)
XLA Modules:
  0.0 98.3 jit_solution(761856219398643269)
XLA Ops:
  0.6 0.9 shard_map.191
  1.6 2.7 %collective-permute-start = (bf16[96,768]{1,0:T(8,128)(2,1)S(1)}, bf16[96,768]{1,0:T(8,128)(2,1)S(1)}, u32[]{:S(2)}, u32[]{:S(2)}) collective-permute-start(bf16[96,768]{1,0:T(8,128)(2,1)S(1)} %shard_map.191), channel_id=1, source_target_pairs={{0,1},{1,2},{2,3},{3,4},{4,5},{5,6},{6,7},{7,8},{8,9},{9,10},{10,1... | collective-permute-start | bytes 442376 | tf_op jit(solution)/shard_map/ppermute | solution.py:465
  4.3 2.1 %collective-permute-done.got = bf16[96,768]{1,0:T(8,128)(2,1)S(1)} collective-permute-done((bf16[96,768]{1,0:T(8,128)(2,1)S(1)}, bf16[96,768]{1,0:T(8,128)(2,1)S(1)}, u32[]{:S(2)}, u32[]{:S(2)}) %collective-permute-start) | collective-permute-done | bytes 147488 | tf_op jit(solution)/shard_map/ppermute | solution.py:465
  6.4 0.0 copy-start.5
  6.4 13.3 %shard_map.192 = bf16[256,2,256]{2,1,0:T(2,128)(2,1)} custom-call(s32[3]{0:T(128)} %dil.1, bf16[96,768]{1,0:T(8,128)(2,1)S(1)} %collective-permute-done.got, f32[3,4096]{1,0:T(4,128)} %wh.3, bf16[64,4096]{1,0:T(8,128)(2,1)} %cot.3, f32[3,64]{1,0:T(4,128)} %bitcast.19, bf16[3,64,128]{2,1,0:T(8,128)(2,1)} %bitcast.16, bf16[3,64,128]{2,1,0:T(8,128)(2,1)} %bitcast.17, ...), custom_call_target="tpu_custom_call" | custom-call | tf_op jit(solution)/shard_map/pallas_call | solution.py:480
  19.6 0.0 copy-start.6
  19.6 0.0 copy-start
  19.6 0.0 copy-start.1
  19.7 0.0 copy-start.2
  19.7 0.0 copy-start.3
  19.7 0.0 copy-start.4
  19.7 15.9 %all-to-all-start = ((bf16[256,2,256]{2,1,0:T(2,128)(2,1)}), bf16[256,2,256]{2,1,0:T(2,128)(2,1)S(1)}, u32[]{:S(2)}, u32[]{:S(2)}) async-start(bf16[256,2,256]{2,1,0:T(2,128)(2,1)} %shard_map.192), calls=%async_computation | async-start | bytes 524288 | tf_op jit(solution)/shard_map/all_to_all | solution.py:449
  35.6 1.0 dynamic-slice_bitcast_fusion.table
  36.6 0.4 fusion.6
  36.9 0.5 broadcast.110
  37.5 0.0 copy-done.5
  37.5 0.7 reduce.3
  38.1 0.1 reshape.20
  38.2 0.1 copy.21
  38.3 6.3 %collective-permute-start.1 = (s32[32,128]{1,0:T(8,128)S(1)}, s32[32,128]{1,0:T(8,128)S(1)}, u32[]{:S(2)}, u32[]{:S(2)}) collective-permute-start(s32[32,128]{1,0:T(8,128)S(1)} %bitcast.15), channel_id=1, source_target_pairs={{0,128},{32,160},{64,192},{96,224},{128,0},{160,32},{192,64},{224,... | collective-permute-start | bytes 49160 | tf_op jit(solution)/shard_map/ppermute | solution.py:503
  44.5 6.3 %all-to-all-done.got = bf16[256,2,256]{2,1,0:T(2,128)(2,1)S(1)} async-done(((bf16[256,2,256]{2,1,0:T(2,128)(2,1)}), bf16[256,2,256]{2,1,0:T(2,128)(2,1)S(1)}, u32[]{:S(2)}, u32[]{:S(2)}) %all-to-all-start) | async-done | bytes 262176 | tf_op jit(solution)/shard_map/all_to_all | solution.py:449
  50.8 0.9 shard_map.193
  51.8 4.3 %all-to-all-start.1 = ((f32[32,4,128]{2,1,0:T(4,128)}), f32[32,4,128]{2,1,0:T(4,128)S(1)}, u32[]{:S(2)}, u32[]{:S(2)}) async-start(f32[32,4,128]{2,1,0:T(4,128)} %get-tuple-element.18), calls=%async_computation.1 | async-start | bytes 131072 | tf_op jit(solution)/shard_map/all_to_all | solution.py:449
  56.0 0.0 copy-done.6
  56.1 0.6 fusion.10
  56.7 0.0 collective-permute-done.1
  56.7 0.6 pad_add_fusion.bins
  57.3 1.0 %shard_map.194.weights = f32[64,128]{1,0:T(8,128)S(1)} custom-call(s32[64,128]{1,0:T(8,128)} %pad_add_fusion.bins, f32[8,128]{1,0:T(8,128)} %bitcast.18), custom_call_target="tpu_custom_call" | custom-call | tf_op jit(solution)/shard_map/pallas_call | solution.py:512
  58.3 5.2 %all-to-all-done.1.got = f32[32,4,128]{2,1,0:T(4,128)S(1)} async-done(((f32[32,4,128]{2,1,0:T(4,128)}), f32[32,4,128]{2,1,0:T(4,128)S(1)}, u32[]{:S(2)}, u32[]{:S(2)}) %all-to-all-start.1) | async-done | bytes 65568 | tf_op jit(solution)/shard_map/all_to_all | solution.py:449
  63.5 0.0 copy-done
  63.5 0.0 copy-done.1
  63.5 0.0 copy-done.2
  63.5 0.0 copy-done.3
  63.5 0.0 copy-done.4
  63.5 1.3 %shard_map.195 = f32[32,4,128]{2,1,0:T(4,128)} custom-call(f32[32,4,128]{2,1,0:T(4,128)S(1)} %all-to-all-done.1.got, f32[64,128]{1,0:T(8,128)S(1)} %shard_map.194.weights, bf16[64,192]{1,0:T(8,128)(2,1)S(1)} %copy-done.1, bf16[2,256,256]{2,1,0:T(8,128)(2,1)S(1)} %copy-done, bf16[64,192]{1,0:T(8,128)(2,1)S(1)} %copy-done.2, f32[32,128]{1,0:T(8,128)S(1)} %copy-done.3, ...), custom_call_target="tpu_custom_call" | custom-call | tf_op jit(solution)/shard_map/pallas_call | solution.py:514
  64.9 3.9 %all-to-all-start.2 = ((f32[32,4,128]{2,1,0:T(4,128)}), f32[32,4,128]{2,1,0:T(4,128)S(1)}, u32[]{:S(2)}, u32[]{:S(2)}) async-start(f32[32,4,128]{2,1,0:T(4,128)} %shard_map.195), calls=%async_computation.2 | async-start | bytes 131072 | tf_op jit(solution)/shard_map/all_to_all | solution.py:449
  68.8 1.0 dynamic-slice_bitcast_fusion.1.table
  69.7 6.5 %all-to-all-done.2.got = f32[32,4,128]{2,1,0:T(4,128)S(1)} async-done(((f32[32,4,128]{2,1,0:T(4,128)}), f32[32,4,128]{2,1,0:T(4,128)S(1)}, u32[]{:S(2)}, u32[]{:S(2)}) %all-to-all-start.2) | async-done | bytes 65568 | tf_op jit(solution)/shard_map/all_to_all | solution.py:449
  76.2 0.4 shard_map.196
  76.6 20.5 %all_to_all.20.got = bf16[256,2,256]{2,1,0:T(2,128)(2,1)S(1)} all-to-all(bf16[256,2,256]{2,1,0:T(2,128)(2,1)S(1)} %shard_map.196), channel_id=1, replica_groups=mesh['rows'=8,'cols'=32] {'rows','cols'}, dimensions={0} | all-to-all | bytes 524288 | tf_op jit(solution)/shard_map/all_to_all | solution.py:449
  97.1 1.1 %shard_map.197 = (f32[3,4096]{1,0:T(4,128)}, f32[3,64,128]{2,1,0:T(8,128)}, f32[3,64,128]{2,1,0:T(8,128)}, f32[3,64,64]{2,1,0:T(8,128)}, f32[3,64]{1,0:T(4,128)}) custom-call(bf16[256,2,256]{2,1,0:T(2,128)(2,1)S(1)} %all_to_all.20.got), custom_call_target="tpu_custom_call" | custom-call | tf_op jit(solution)/shard_map/pallas_call | solution.py:521
  (5 shorter events, 0.0 us)
Async XLA Ops:
  1.6 4.8 %collective-permute-start = (bf16[96,768]{1,0:T(8,128)(2,1)S(1)}, bf16[96,768]{1,0:T(8,128)(2,1)S(1)}, u32[]{:S(2)}, u32[]{:S(2)}) collective-permute-start(bf16[96,768]{1,0:T(8,128)(2,1)S(1)} %shard_map.191), channel_id=1, source_target_pairs={{0,1},{1,2},{2,3},{3,4},{4,5},{5,6},{6,7},{7,8},{8,9},{9,10},{10,1... | collective-permute-start | bytes 442376 | tf_op jit(solution)/shard_map/ppermute | solution.py:465
  6.4 31.1 %copy-start.5 = (s32[4096,1,1]{0,2,1:T(1,128)S(1)}, s32[4096,1,1]{0,2,1:T(1,128)}, u32[]{:S(2)}) copy-start(s32[4096,1,1]{0,2,1:T(1,128)} %param.23) | copy-start | bytes 49156
  19.6 36.4 %copy-start.6 = (f32[2,1024]{1,0:T(2,128)S(1)}, f32[2,1024]{1,0:T(2,128)}, u32[]{:S(2)}) copy-start(f32[2,1024]{1,0:T(2,128)} %param.24) | copy-start | bytes 24580
  19.6 43.8 %copy-start = (bf16[2,256,256]{2,1,0:T(8,128)(2,1)S(1)}, bf16[2,256,256]{2,1,0:T(8,128)(2,1)}, u32[]{:S(2)}) copy-start(bf16[2,256,256]{2,1,0:T(8,128)(2,1)} %constant.109.clone.fast) | copy-start | bytes 786436
  19.6 43.8 %copy-start.1 = (bf16[64,192]{1,0:T(8,128)(2,1)S(1)}, bf16[64,192]{1,0:T(8,128)(2,1)}, u32[]{:S(2)}) copy-start(bf16[64,192]{1,0:T(8,128)(2,1)} %constant.108.clone.outer) | copy-start | bytes 73732
  19.7 43.8 %copy-start.2 = (bf16[64,192]{1,0:T(8,128)(2,1)S(1)}, bf16[64,192]{1,0:T(8,128)(2,1)}, u32[]{:S(2)}) copy-start(bf16[64,192]{1,0:T(8,128)(2,1)} %constant.110.clone.outer_back) | copy-start | bytes 73732
  19.7 43.8 %copy-start.3 = (f32[32,128]{1,0:T(8,128)S(1)}, f32[32,128]{1,0:T(8,128)}, u32[]{:S(2)}) copy-start(f32[32,128]{1,0:T(8,128)} %constant.111.clone.turn_cos) | copy-start | bytes 49156
  19.7 43.8 %copy-start.4 = (f32[32,128]{1,0:T(8,128)S(1)}, f32[32,128]{1,0:T(8,128)}, u32[]{:S(2)}) copy-start(f32[32,128]{1,0:T(8,128)} %constant.112.clone.turn_sin) | copy-start | bytes 49156
  19.7 31.1 %all-to-all-start = ((bf16[256,2,256]{2,1,0:T(2,128)(2,1)}), bf16[256,2,256]{2,1,0:T(2,128)(2,1)S(1)}, u32[]{:S(2)}, u32[]{:S(2)}) async-start(bf16[256,2,256]{2,1,0:T(2,128)(2,1)} %shard_map.192), calls=%async_computation | async-start | bytes 524288 | tf_op jit(solution)/shard_map/all_to_all | solution.py:449
  38.3 18.4 %collective-permute-start.1 = (s32[32,128]{1,0:T(8,128)S(1)}, s32[32,128]{1,0:T(8,128)S(1)}, u32[]{:S(2)}, u32[]{:S(2)}) collective-permute-start(s32[32,128]{1,0:T(8,128)S(1)} %bitcast.15), channel_id=1, source_target_pairs={{0,128},{32,160},{64,192},{96,224},{128,0},{160,32},{192,64},{224,... | collective-permute-start | bytes 49160 | tf_op jit(solution)/shard_map/ppermute | solution.py:503
  51.8 11.7 %all-to-all-start.1 = ((f32[32,4,128]{2,1,0:T(4,128)}), f32[32,4,128]{2,1,0:T(4,128)S(1)}, u32[]{:S(2)}, u32[]{:S(2)}) async-start(f32[32,4,128]{2,1,0:T(4,128)} %get-tuple-element.18), calls=%async_computation.1 | async-start | bytes 131072 | tf_op jit(solution)/shard_map/all_to_all | solution.py:449
  64.9 11.3 %all-to-all-start.2 = ((f32[32,4,128]{2,1,0:T(4,128)}), f32[32,4,128]{2,1,0:T(4,128)S(1)}, u32[]{:S(2)}, u32[]{:S(2)}) async-start(f32[32,4,128]{2,1,0:T(4,128)} %shard_map.195), calls=%async_computation.2 | async-start | bytes 131072 | tf_op jit(solution)/shard_map/all_to_all | solution.py:449

commit v9 on v8

--- a/solution.py
+++ b/solution.py
@@ -478,8 +478,8 @@
     )
     packed = pltpu.VMEM((n, 2, 2 * LANES), BF16)
     sent, = call(conv_kernel, [packed], scratch, smem=1, n_in=7)(
-        dilations, received, whitened, cotangent, lift_weight.T, jnp.swapaxes(conv_now, 1, 2),
-        jnp.swapaxes(conv_past, 1, 2), mix_weight,
+        dilations, received, near(whitened), near(cotangent), near(lift_weight.T),
+        near(jnp.swapaxes(conv_now, 1, 2)), near(jnp.swapaxes(conv_past, 1, 2)), near(mix_weight),
     )
     outward, inward, outer, outer_back, fast, turn_cos, turn_sin = tables(rows_count, cols_count)
     my_row, my_col = lax.axis_index("rows"), lax.axis_index("cols")

time: 98.7 us -> 103 us (1.044)
  local copies, waits for them, and re-layouts: 2.62 us -> 6.53 us
    unnamed x14 -> x26, local copies, waits for them, and re-layouts: 0.04 us -> 3.95 us
where the time goes in v9:
time: 103 us; the launch traced here: 102 us
  starting transfers between devices  33 us (32%)
  blocking collectives  20.5 us (20%)
  waiting for transfers between devices  20 us (19%)
  Pallas kernels  18.8 us (18%)
  local copies, waits for them, and re-layouts  6.53 us (6%)
  other arithmetic  2.3 us (2%)
    all_to_all x3, starting transfers between devices, exchange(): lax.all_to_all(x, axes, split_axis=0, concat_axis=0, tiled=True)  24.1 us
    all_to_all x1, blocking collectives, exchange(): lax.all_to_all(x, axes, split_axis=0, concat_axis=0, tiled=True)  20.5 us
    all_to_all x3, waiting for transfers between devices, exchange(): lax.all_to_all(x, axes, split_axis=0, concat_axis=0, tiled=True)  17.9 us
    pallas_call x1, Pallas kernels, local(): call(conv_kernel, [packed], scratch, smem=1, n_in=7)  13 us
    ppermute x1, starting transfers between devices, local(): lax.ppermute(bins, 'rows', [(i, (i + half) % rows_count) for i in range(r...  6.26 us
    unnamed x26, local copies, waits for them, and re-layouts  3.95 us
    ppermute x1, starting transfers between devices, local(): lax.ppermute(message, BOTH, [(i, (i + 1) % n) for i in range(n)])  2.67 us
    ppermute x1, waiting for transfers between devices, local(): lax.ppermute(message, BOTH, [(i, (i + 1) % n) for i in range(n)])  2.09 us
  transfers between devices with their start and end apart: 5, of which 4 were waited for; matrix products, arithmetic and copies ran while one was open for 5% of the time, Pallas kernels for 2%

profile of v9, /device:TPU:1, one launch (start us, length us, event | category | flops | bytes accessed | tf_op | source)
XLA Modules:
  0.0 102.0 jit_solution(6681403028172673492)
XLA Ops:
  0.6 0.0 copy-start
  0.6 1.0 shard_map.191
  1.7 2.7 %collective-permute-start = (bf16[96,768]{1,0:T(8,128)(2,1)S(1)}, bf16[96,768]{1,0:T(8,128)(2,1)S(1)}, u32[]{:S(2)}, u32[]{:S(2)}) collective-permute-start(bf16[96,768]{1,0:T(8,128)(2,1)S(1)} %shard_map.191), channel_id=1, source_target_pairs={{0,1},{1,2},{2,3},{3,4},{4,5},{5,6},{6,7},{7,8},{8,9},{9,10},{10,1... | collective-permute-start | bytes 442376 | tf_op jit(solution)/shard_map/ppermute | solution.py:465
  4.3 2.1 %collective-permute-done.got = bf16[96,768]{1,0:T(8,128)(2,1)S(1)} collective-permute-done((bf16[96,768]{1,0:T(8,128)(2,1)S(1)}, bf16[96,768]{1,0:T(8,128)(2,1)S(1)}, u32[]{:S(2)}, u32[]{:S(2)}) %collective-permute-start) | collective-permute-done | bytes 147488 | tf_op jit(solution)/shard_map/ppermute | solution.py:465
  6.4 0.0 copy-done
  6.4 0.0 copy-start.1
  6.4 0.8 copy-done.1
  7.3 0.0 copy-start.3
  7.3 0.8 copy-done.3
  8.1 0.8 copy-done.4
  8.9 0.0 copy-start.5
  8.9 0.8 copy-done.5
  9.7 0.0 copy-start.10
  9.7 0.7 copy-done.10
  10.3 13.0 %shard_map.192 = bf16[256,2,256]{2,1,0:T(2,128)(2,1)} custom-call(s32[3]{0:T(128)} %dil.1, bf16[96,768]{1,0:T(8,128)(2,1)S(1)} %collective-permute-done.got, f32[3,4096]{1,0:T(4,128)S(1)} %copy-done.1, bf16[64,4096]{1,0:T(8,128)(2,1)S(1)} %copy-done, f32[3,64]{1,0:T(4,128)S(1)} %bitcast.17, bf16[3,64,128]{2,1,0:T(8,128)(2,1)S(1)} %bitcast.15, ...), custom_call_target="tpu_custom_call" | custom-call | tf_op jit(solution)/shard_map/pallas_call | solution.py:480
  23.3 0.0 copy-start.12
  23.3 0.0 copy-start.8
  23.4 0.0 copy-start.9
  23.4 15.9 %all-to-all-start = ((bf16[256,2,256]{2,1,0:T(2,128)(2,1)}), bf16[256,2,256]{2,1,0:T(2,128)(2,1)S(1)}, u32[]{:S(2)}, u32[]{:S(2)}) async-start(bf16[256,2,256]{2,1,0:T(2,128)(2,1)} %shard_map.192), calls=%async_computation | async-start | bytes 524288 | tf_op jit(solution)/shard_map/all_to_all | solution.py:449
  39.3 1.0 dynamic-slice_bitcast_fusion.table
  40.3 0.4 fusion.6
  40.6 0.5 broadcast.110
  41.2 0.0 copy-done.11
  41.2 0.7 reduce.3
  41.8 0.1 reshape.20
  41.9 0.1 copy.21
  42.0 6.3 %collective-permute-start.1 = (s32[32,128]{1,0:T(8,128)S(1)}, s32[32,128]{1,0:T(8,128)S(1)}, u32[]{:S(2)}, u32[]{:S(2)}) collective-permute-start(s32[32,128]{1,0:T(8,128)S(1)} %bitcast.18), channel_id=1, source_target_pairs={{0,128},{32,160},{64,192},{96,224},{128,0},{160,32},{192,64},{224,... | collective-permute-start | bytes 49160 | tf_op jit(solution)/shard_map/ppermute | solution.py:503
  48.2 6.3 %all-to-all-done.got = bf16[256,2,256]{2,1,0:T(2,128)(2,1)S(1)} async-done(((bf16[256,2,256]{2,1,0:T(2,128)(2,1)}), bf16[256,2,256]{2,1,0:T(2,128)(2,1)S(1)}, u32[]{:S(2)}, u32[]{:S(2)}) %all-to-all-start) | async-done | bytes 262176 | tf_op jit(solution)/shard_map/all_to_all | solution.py:449
  54.5 0.9 shard_map.193
  55.5 4.3 %all-to-all-start.1 = ((f32[32,4,128]{2,1,0:T(4,128)}), f32[32,4,128]{2,1,0:T(4,128)S(1)}, u32[]{:S(2)}, u32[]{:S(2)}) async-start(f32[32,4,128]{2,1,0:T(4,128)} %get-tuple-element.18), calls=%async_computation.1 | async-start | bytes 131072 | tf_op jit(solution)/shard_map/all_to_all | solution.py:449
  59.8 0.0 copy-done.12
  59.8 0.6 fusion.10
  60.4 0.0 collective-permute-done.1
  60.4 0.6 pad_add_fusion.bins
  61.0 1.0 shard_map.194.weights
  62.0 5.2 %all-to-all-done.1.got = f32[32,4,128]{2,1,0:T(4,128)S(1)} async-done(((f32[32,4,128]{2,1,0:T(4,128)}), f32[32,4,128]{2,1,0:T(4,128)S(1)}, u32[]{:S(2)}, u32[]{:S(2)}) %all-to-all-start.1) | async-done | bytes 65568 | tf_op jit(solution)/shard_map/all_to_all | solution.py:449
  67.2 0.0 copy-done.2
  67.2 0.0 copy-done.6
  67.2 0.0 copy-done.7
  67.2 0.0 copy-done.8
  67.2 0.0 copy-done.9
  67.2 1.3 %shard_map.195 = f32[32,4,128]{2,1,0:T(4,128)} custom-call(f32[32,4,128]{2,1,0:T(4,128)S(1)} %all-to-all-done.1.got, f32[64,128]{1,0:T(8,128)S(1)} %shard_map.194.weights, bf16[64,192]{1,0:T(8,128)(2,1)S(1)} %copy-done.6, bf16[2,256,256]{2,1,0:T(8,128)(2,1)S(1)} %copy-done.2, bf16[64,192]{1,0:T(8,128)(2,1)S(1)} %copy-done.7, f32[32,128]{1,0:T(8,128)S(1)} %copy-done.8, ...), custom_call_target="tpu_custom_call" | custom-call | tf_op jit(solution)/shard_map/pallas_call | solution.py:514
  68.6 3.9 %all-to-all-start.2 = ((f32[32,4,128]{2,1,0:T(4,128)}), f32[32,4,128]{2,1,0:T(4,128)S(1)}, u32[]{:S(2)}, u32[]{:S(2)}) async-start(f32[32,4,128]{2,1,0:T(4,128)} %shard_map.195), calls=%async_computation.2 | async-start | bytes 131072 | tf_op jit(solution)/shard_map/all_to_all | solution.py:449
  72.5 1.0 dynamic-slice_bitcast_fusion.1.table
  73.4 6.5 %all-to-all-done.2.got = f32[32,4,128]{2,1,0:T(4,128)S(1)} async-done(((f32[32,4,128]{2,1,0:T(4,128)}), f32[32,4,128]{2,1,0:T(4,128)S(1)}, u32[]{:S(2)}, u32[]{:S(2)}) %all-to-all-start.2) | async-done | bytes 65568 | tf_op jit(solution)/shard_map/all_to_all | solution.py:449
  79.9 0.4 shard_map.196
  80.4 20.5 %all_to_all.20.got = bf16[256,2,256]{2,1,0:T(2,128)(2,1)S(1)} all-to-all(bf16[256,2,256]{2,1,0:T(2,128)(2,1)S(1)} %shard_map.196), channel_id=1, replica_groups=mesh['rows'=8,'cols'=32] {'rows','cols'}, dimensions={0} | all-to-all | bytes 524288 | tf_op jit(solution)/shard_map/all_to_all | solution.py:449
  100.8 1.1 %shard_map.197 = (f32[3,4096]{1,0:T(4,128)}, f32[3,64,128]{2,1,0:T(8,128)}, f32[3,64,128]{2,1,0:T(8,128)}, f32[3,64,64]{2,1,0:T(8,128)}, f32[3,64]{1,0:T(4,128)}) custom-call(bf16[256,2,256]{2,1,0:T(2,128)(2,1)S(1)} %all_to_all.20.got), custom_call_target="tpu_custom_call" | custom-call | tf_op jit(solution)/shard_map/pallas_call | solution.py:521
  (10 shorter events, 0.0 us)
Async XLA Ops:
  0.6 5.8 %copy-start = (bf16[64,4096]{1,0:T(8,128)(2,1)S(1)}, bf16[64,4096]{1,0:T(8,128)(2,1)}, u32[]{:S(2)}) copy-start(bf16[64,4096]{1,0:T(8,128)(2,1)} %cot.3) | copy-start | bytes 1572868
  1.7 4.8 %collective-permute-start = (bf16[96,768]{1,0:T(8,128)(2,1)S(1)}, bf16[96,768]{1,0:T(8,128)(2,1)S(1)}, u32[]{:S(2)}, u32[]{:S(2)}) collective-permute-start(bf16[96,768]{1,0:T(8,128)(2,1)S(1)} %shard_map.191), channel_id=1, source_target_pairs={{0,1},{1,2},{2,3},{3,4},{4,5},{5,6},{6,7},{7,8},{8,9},{9,10},{10,1... | collective-permute-start | bytes 442376 | tf_op jit(solution)/shard_map/ppermute | solution.py:465
  6.4 0.8 copy-start.1
  7.3 0.8 copy-start.3
  8.1 0.8 copy-start.4
  8.9 0.8 copy-start.5
  9.7 0.7 copy-start.10
  10.3 30.8 %copy-start.11 = (s32[4096,1,1]{0,2,1:T(1,128)S(1)}, s32[4096,1,1]{0,2,1:T(1,128)}, u32[]{:S(2)}) copy-start(s32[4096,1,1]{0,2,1:T(1,128)} %param.23) | copy-start | bytes 49156
  23.3 36.4 %copy-start.12 = (f32[2,1024]{1,0:T(2,128)S(1)}, f32[2,1024]{1,0:T(2,128)}, u32[]{:S(2)}) copy-start(f32[2,1024]{1,0:T(2,128)} %param.24) | copy-start | bytes 24580
  23.3 43.9 %copy-start.2 = (bf16[2,256,256]{2,1,0:T(8,128)(2,1)S(1)}, bf16[2,256,256]{2,1,0:T(8,128)(2,1)}, u32[]{:S(2)}) copy-start(bf16[2,256,256]{2,1,0:T(8,128)(2,1)} %constant.109.clone.fast) | copy-start | bytes 786436
  23.3 43.9 %copy-start.6 = (bf16[64,192]{1,0:T(8,128)(2,1)S(1)}, bf16[64,192]{1,0:T(8,128)(2,1)}, u32[]{:S(2)}) copy-start(bf16[64,192]{1,0:T(8,128)(2,1)} %constant.108.clone.outer) | copy-start | bytes 73732
  23.3 43.9 %copy-start.7 = (bf16[64,192]{1,0:T(8,128)(2,1)S(1)}, bf16[64,192]{1,0:T(8,128)(2,1)}, u32[]{:S(2)}) copy-start(bf16[64,192]{1,0:T(8,128)(2,1)} %constant.110.clone.outer_back) | copy-start | bytes 73732
  23.3 43.9 %copy-start.8 = (f32[32,128]{1,0:T(8,128)S(1)}, f32[32,128]{1,0:T(8,128)}, u32[]{:S(2)}) copy-start(f32[32,128]{1,0:T(8,128)} %constant.111.clone.turn_cos) | copy-start | bytes 49156
  23.4 43.9 %copy-start.9 = (f32[32,128]{1,0:T(8,128)S(1)}, f32[32,128]{1,0:T(8,128)}, u32[]{:S(2)}) copy-start(f32[32,128]{1,0:T(8,128)} %constant.112.clone.turn_sin) | copy-start | bytes 49156
  23.4 31.1 %all-to-all-start = ((bf16[256,2,256]{2,1,0:T(2,128)(2,1)}), bf16[256,2,256]{2,1,0:T(2,128)(2,1)S(1)}, u32[]{:S(2)}, u32[]{:S(2)}) async-start(bf16[256,2,256]{2,1,0:T(2,128)(2,1)} %shard_map.192), calls=%async_computation | async-start | bytes 524288 | tf_op jit(solution)/shard_map/all_to_all | solution.py:449
  42.0 18.4 %collective-permute-start.1 = (s32[32,128]{1,0:T(8,128)S(1)}, s32[32,128]{1,0:T(8,128)S(1)}, u32[]{:S(2)}, u32[]{:S(2)}) collective-permute-start(s32[32,128]{1,0:T(8,128)S(1)} %bitcast.18), channel_id=1, source_target_pairs={{0,128},{32,160},{64,192},{96,224},{128,0},{160,32},{192,64},{224,... | collective-permute-start | bytes 49160 | tf_op jit(solution)/shard_map/ppermute | solution.py:503
  55.5 11.7 %all-to-all-start.1 = ((f32[32,4,128]{2,1,0:T(4,128)}), f32[32,4,128]{2,1,0:T(4,128)S(1)}, u32[]{:S(2)}, u32[]{:S(2)}) async-start(f32[32,4,128]{2,1,0:T(4,128)} %get-tuple-element.18), calls=%async_computation.1 | async-start | bytes 131072 | tf_op jit(solution)/shard_map/all_to_all | solution.py:449
  68.6 11.3 %all-to-all-start.2 = ((f32[32,4,128]{2,1,0:T(4,128)}), f32[32,4,128]{2,1,0:T(4,128)S(1)}, u32[]{:S(2)}, u32[]{:S(2)}) async-start(f32[32,4,128]{2,1,0:T(4,128)} %shard_map.195), calls=%async_computation.2 | async-start | bytes 131072 | tf_op jit(solution)/shard_map/all_to_all | solution.py:449
